TPU v7x, 256 devices: a whole 4x4x8 slice. The times are simulated.
256 devices in a mesh: grp: 32 (over x_lo, z, core), tp: 8 (over y, x_hi).
Axes of the slice: x: 4 (x_hi: 2, x_lo: 2; x = x_hi * 2 + x_lo), y: 4, z: 8, core: 2. Of those that a mesh axis runs over, the one named last changes fastest.
Arguments:
- tokens: bfloat16 [32, 1024, 2048], P(None, 'grp'), may hold values from -6 to 6
- w_query: bfloat16 [2048, 2048], P(None, 'tp'), may hold values from -0.375 to 0.375
- w_key: bfloat16 [2048, 2048], P(None, 'tp'), may hold values from -0.125 to 0.125
- w_value: bfloat16 [2048, 2048], P(None, 'tp'), may hold values from -0.125 to 0.125
- w_out: bfloat16 [2048, 2048], P('tp'), may hold values from -0.125 to 0.125
- own_cache: bfloat16 [32, 2, 2048, 2048], P('grp', None, None, 'tp'), may hold values from -330 to 330
- guest_cache: bfloat16 [32, 2, 2048, 2048], P('grp', None, None, 'tp'), may hold values from -6 to 6
- rec_hidden: bfloat16 [32, 256, 2048], P('grp'), may hold values from -6 to 6
- deal_order: int32 [32], replicated, may hold values from 0 to 31, each once
- own_len: int32 [32], replicated, may hold values from 256 to 2048, as said below
- guest_len: int32 [32], replicated, may hold values from 0 to 2048, as said below
- rec_index: int32 [32, 256], P('grp'), may hold values from 0 to 2047, as said below
Outputs:
- attn_out: bfloat16 [32, 1024, 2048], P(None, 'grp', 'tp')
Inputs may be any that keep to these rules, and one draw needn't show every extreme that they name: Rows 0 to own_len[g] - 1 of group g's own slot hold cached positions 0 to own_len[g] - 1 of the request served at group g; a request whose cache continues in a guest region fills its own slot. The guest_len[g] used rows of group g's guest region continue the cache of the request served at group (g + 16) mod 32. rec_index[g] holds 256 distinct rows of group g's own slot, each below own_len[g].
All inputs are finite; a program needn't handle non-finite values.
Results may differ from a plain program's by a relative error of at most 0.02.
The roundings to bfloat16 on the way count: a program that leaves them out, or rounds other values in their place, can miss the bound.
Values may be sent and summed in bfloat16 or wider, within the bound.
A program may use at most 128 MiB of HBM per device.

v0:
```python
import jax
import jax.numpy as jnp
from jax import lax
from jax.sharding import PartitionSpec as P

HEAD_DIM = 128


rope_base = 10000.0
norm_eps = 1e-05


def swapped(value, axis, apart):
    mask = 2**apart
    pairs = [(source, source ^ mask) for source in range(lax.axis_size(axis))]
    return lax.ppermute(value, axis, pairs)


def layer_norm(token_rows):
    widened = token_rows.astype(jnp.float32)
    centred = widened - jnp.mean(widened, axis=-1, keepdims=True)
    variance = jnp.mean(centred * centred, axis=-1, keepdims=True)
    return centred * lax.rsqrt(variance + norm_eps)


def rotate(projected, positions, head_dim):
    half_dim = head_dim // 2
    frequency = jnp.exp(-jnp.log(rope_base) * jnp.arange(half_dim, dtype=jnp.float32) / half_dim)
    angles = positions.astype(jnp.float32)[:, None] * frequency[None, :]
    cosine = jnp.cos(angles)[:, None, :]
    sine_part = jnp.sin(angles)[:, None, :]
    shaped = projected.reshape(projected.shape[0], -1, head_dim)
    first_half = shaped[..., :half_dim]
    second = shaped[..., half_dim:]
    turned = jnp.concatenate(
        [first_half * cosine - second * sine_part, second * cosine + first_half * sine_part],
        axis=-1,
    )
    return turned.reshape(projected.shape)


def absorb(softmax_state, queries, key_rows, value_rows, is_valid):
    running_max, weight_sum, numerator = softmax_state
    score_scale = queries.shape[-1] ** (-0.5)
    scores = (
        jnp.einsum("qhd,khd->hqk", queries, key_rows, preferred_element_type=jnp.float32)
        * score_scale
    )
    scores = jnp.where(is_valid[None], scores, -jnp.inf)
    new_max = jnp.maximum(running_max, jnp.max(scores, axis=-1))
    factor = jnp.exp(running_max - new_max)
    expanded = jnp.exp(scores - new_max[..., None])
    weight_sum = weight_sum * factor + jnp.sum(expanded, axis=-1)
    product = jnp.einsum(
        "hqk,khd->qhd",
        expanded.astype(jnp.bfloat16),
        value_rows,
        preferred_element_type=jnp.float32,
    )
    numerator = numerator * jnp.transpose(factor)[:, :, None] + product
    return (new_max, weight_sum, numerator)


def sweep_keys(softmax_state, queries, key_rows, value_rows, live_count):
    block_len = min(512, key_rows.shape[0])
    block_count = (live_count + block_len - 1) // block_len

    def visit_block(block_index, carried):
        block_start = block_index * block_len
        key_block = lax.dynamic_slice_in_dim(key_rows, block_start, block_len, 0)
        value_block = lax.dynamic_slice_in_dim(value_rows, block_start, block_len, 0)
        is_valid = block_start + jnp.arange(block_len, dtype=jnp.int32) < live_count
        return absorb(carried, queries, key_block, value_block, is_valid[None, :])

    return lax.fori_loop(jnp.int32(0), block_count, visit_block, softmax_state)


def shards(
    tokens,
    w_query,
    w_key,
    w_value,
    w_out,
    own_cache,
    guest_cache,
    rec_hidden,
    deal_order,
    own_len,
    guest_len,
    rec_index,
):
    groups = lax.axis_size("grp")
    group_id = lax.axis_index("grp")
    partner_id = (group_id + groups // 2) % groups
    swap_bit = groups.bit_length() - 2
    local_width = w_query.shape[1]
    local_heads = local_width // HEAD_DIM
    arranged = jnp.take(tokens, deal_order, axis=0)
    dealt_rows = lax.all_to_all(arranged, "grp", split_axis=0, concat_axis=1, tiled=True)
    token_rows = dealt_rows[0]
    span_len = token_rows.shape[0]
    own_count = own_len[group_id]
    guest_count = guest_len[partner_id]
    positions = own_count + guest_count + jnp.arange(span_len, dtype=jnp.int32)
    normed = layer_norm(token_rows).astype(jnp.bfloat16)
    queries = rotate(
        jnp.dot(normed, w_query, preferred_element_type=jnp.float32), positions, HEAD_DIM
    ).astype(jnp.bfloat16)
    new_keys = rotate(
        jnp.dot(normed, w_key, preferred_element_type=jnp.float32), positions, HEAD_DIM
    ).astype(jnp.bfloat16)
    new_values = jnp.dot(normed, w_value, preferred_element_type=jnp.float32).astype(jnp.bfloat16)
    rec_rows = layer_norm(rec_hidden[0]).astype(jnp.bfloat16)
    rec_positions = rec_index[0]
    rec_keys = rotate(
        jnp.dot(rec_rows, w_key, preferred_element_type=jnp.float32), rec_positions, HEAD_DIM
    ).astype(jnp.bfloat16)
    rec_values = jnp.dot(rec_rows, w_value, preferred_element_type=jnp.float32).astype(jnp.bfloat16)
    cached_keys = own_cache[0, 0].at[rec_positions].set(rec_keys)
    cached_values = own_cache[0, 1].at[rec_positions].set(rec_values)

    def by_head(matrix):
        return matrix.reshape(matrix.shape[0], local_heads, HEAD_DIM)

    empty_state = (
        jnp.full((local_heads, span_len), -jnp.inf, jnp.float32),
        jnp.zeros((local_heads, span_len), jnp.float32),
        jnp.zeros((span_len, local_heads, HEAD_DIM), jnp.float32),
    )
    causal = jnp.arange(span_len)[None, :] <= jnp.arange(span_len)[:, None]
    query_heads = by_head(queries)
    softmax_state = absorb(empty_state, query_heads, by_head(new_keys), by_head(new_values), causal)
    softmax_state = sweep_keys(
        softmax_state, query_heads, by_head(cached_keys), by_head(cached_values), own_count
    )
    fetched = swapped(guest_cache[0], "grp", swap_bit)
    softmax_state = sweep_keys(
        softmax_state, query_heads, by_head(fetched[0]), by_head(fetched[1]), guest_count
    )
    weight_sum = softmax_state[1]
    numerator = softmax_state[2]
    attended = (
        (numerator / jnp.transpose(weight_sum)[:, :, None])
        .astype(jnp.bfloat16)
        .reshape(span_len, local_width)
    )
    partial_value = jnp.dot(attended, w_out, preferred_element_type=jnp.float32).astype(
        jnp.bfloat16
    )
    summed = lax.psum_scatter(partial_value, "tp", scatter_dimension=1, tiled=True).astype(
        jnp.float32
    )
    mixed_rows = summed.astype(jnp.bfloat16)
    returned_rows = lax.all_to_all(mixed_rows[None], "grp", split_axis=1, concat_axis=0, tiled=True)
    return jnp.zeros_like(returned_rows).at[deal_order].set(returned_rows)


def solution(mesh):
    return jax.shard_map(
        shards,
        mesh=mesh,
        in_specs=(
            P(None, "grp", None),
            P(None, "tp"),
            P(None, "tp"),
            P(None, "tp"),
            P("tp", None),
            P("grp", None, None, "tp"),
            P("grp", None, None, "tp"),
            P("grp", None, None),
            P(),
            P(),
            P(),
            P("grp", None),
        ),
        out_specs=P(None, "grp", "tp"),
        check_vma=False,
    )
```

profile of v0, /device:TPU:1, one launch (start us, length us, event | category | flops | bytes accessed | tf_op | source)
XLA Modules:
  0.0 334.1 jit_solution(3945670386425968742)
XLA Ops:
  8.0 5.0 %gather_fusion = bf16[32,32,2048]{2,1,0:T(8,128)(2,1)} fusion(bf16[32,32,2048]{2,1,0:T(8,128)(2,1)} %param.16, s32[1024]{0:T(1024)S(1)} %pad_clamp_fusion), kind=kCustom, calls=%fused_computation | custom fusion | bytes 8388736 | tf_op jit(solution)/shard_map/jit(_take)/gather | solution.py:98
  12.9 4.6 %broadcast_select_fusion = bf16[32,32,2048]{2,1,0:T(8,128)(2,1)} fusion(bf16[32,32,2048]{2,1,0:T(8,128)(2,1)} %gather_fusion, pred[32]{0:T(512)(128)(4,1)S(1)} %compare_and_fusion), kind=kLoop, calls=%fused_computation.65 | loop fusion | flops 2097152 | bytes 8388640 | tf_op jit(solution)/shard_map/jit(_take)/select_n | solution.py:98
  17.6 11.1 %all-to-all-start = ((bf16[32,32,2048]{2,1,0:T(8,128)(2,1)}), bf16[32,32,2048]{2,1,0:T(8,128)(2,1)}, u32[]{:S(2)}, u32[]{:S(2)}) async-start(bf16[32,32,2048]{2,1,0:T(8,128)(2,1)} %broadcast_select_fusion), calls=%async_computation | async-start | bytes 8388608 | tf_op jit(solution)/shard_map/all_to_all | solution.py:99
  28.8 4.1 %copy.72 = bf16[1,2,2048,256]{2,3,1,0:T(8,128)(2,1)} copy(bf16[1,2,2048,256]{3,2,1,0:T(8,128)(2,1)} %param.22) | data formatting | bytes 4194304 | tf_op args[6]
  39.4 2.4 copy.81
  45.2 2.1 scatter_fusion
  50.8 2.3 scatter_fusion.1
  55.8 62.3 %collective-permute-done = bf16[2,2048,256]{1,2,0:T(8,128)(2,1)} collective-permute-done((bf16[2,2048,256]{1,2,0:T(8,128)(2,1)}, bf16[2,2048,256]{1,2,0:T(8,128)(2,1)}, u32[]{:S(2)}, u32[]{:S(2)}) %collective-permute-start) | collective-permute-done | bytes 2097184 | tf_op jit(solution)/shard_map/ppermute | solution.py:16
  118.1 3.1 fusion.84
  121.2 2.1 all-to-all-done
  123.3 2.8 convert_reduce_fusion
  126.2 3.4 %multiply_reduce_fusion = f32[32,32]{1,0:T(8,128)S(1)} fusion(bf16[32,32,2048]{2,1,0:T(8,128)(2,1)} %all-to-all-done, f32[32,32]{1,0:T(8,128)S(1)} %broadcast_multiply_fusion), kind=kLoop, calls=%fused_computation.58 | loop fusion | flops 8387584 | bytes 4202496 | tf_op jit(solution)/shard_map/reduce_sum | solution.py:22
  129.7 2.9 multiply_convert_fusion
  137.4 3.0 fusion.48
  142.4 3.1 fusion.47
  146.9 2.8 fusion.64
  149.8 12.0 %while.28 = (s32[]{:T(128)}, f32[2,1024]{1,0:T(2,128)S(1)}, f32[2,1024]{1,0:T(2,128)S(1)}, f32[1024,2,128]{0,2,1:T(8,128)S(1)}, s32[]{:T(128)}, /*index=5*/s32[]...) while((s32[]{:T(128)}, f32[2,1024]{1,0:T(2,128)S(1)}, ...), condition=%wide.region_11.12_spmd, body=%wide.region_8.11_spmd.sunk | while | flops 548936704 | bytes 15861947 | solution.py:75
  152.5 2.3 fusion.117
  158.4 2.3 fusion.117
  162.1 3.2 convolution_convert_fusion
  165.4 124.6 %reduce-scatter.2.cloned.1.call-done = bf16[1024,256]{1,0:T(8,128)(2,1)} async-done(((bf16[1024,2048]{1,0:T(8,128)(2,1)}), bf16[1024,256]{1,0:T(8,128)(2,1)}) %reduce-scatter.2.cloned.1.call-update) | async-done | bytes 524304 | tf_op jit(solution)/shard_map/reduce_scatter | solution.py:150
  292.3 3.8 %reduce.9 = bf16[1024,256]{1,0:T(8,128)(2,1)S(1)} reduce(bf16[1024,1,256]{2,1,0:T(2,128)(2,1)S(1)} %bitcast.145, bf16[]{:T(256)} %broadcast.254), dimensions={1}, to_apply=%bitcast.113.reduce_sub_computation | reduce | bytes 1048578
  296.3 25.2 %all_to_all.21 = bf16[32,2,4096]{2,1,0:T(2,128)(2,1)S(1)} all-to-all(bf16[32,2,4096]{2,1,0:T(2,128)(2,1)S(1)} %reshape.350), channel_id=1, replica_groups=mesh['grp'=32,'tp'=8] {'grp'}, dimensions={0} | all-to-all | bytes 1048576 | tf_op jit(solution)/shard_map/all_to_all | solution.py:154
  322.9 4.4 %scatter_fusion.2 = bf16[32,32,256]{2,1,0:T(8,128)(2,1)} fusion(bf16[32,32,256]{2,1,0:T(8,128)(2,1)} %broadcast_in_dim.55, s32[32]{0:T(128)S(1)} %compare_select_fusion.1, bf16[32,32,256]{2,1,0:T(8,128)(2,1)S(1)} %bitcast.147), kind=kCustom, calls=%fused_computation.3 | custom fusion | bytes 1572992 | tf_op jit(solution)/shard_map/scatter | solution.py:155
  (86 shorter events, 34.8 us)
Async XLA Ops:
  6.5 155.6 %copy-start = (bf16[256,2048]{1,0:T(8,128)(2,1)S(1)}, bf16[256,2048]{1,0:T(8,128)(2,1)}, u32[]{:S(2)}) copy-start(bf16[256,2048]{1,0:T(8,128)(2,1)} %param.20) | copy-start | bytes 3145732
  17.6 105.7 %all-to-all-start = ((bf16[32,32,2048]{2,1,0:T(8,128)(2,1)}), bf16[32,32,2048]{2,1,0:T(8,128)(2,1)}, u32[]{:S(2)}, u32[]{:S(2)}) async-start(bf16[32,32,2048]{2,1,0:T(8,128)(2,1)} %broadcast_select_fusion), calls=%async_computation | async-start | bytes 8388608 | tf_op jit(solution)/shard_map/all_to_all | solution.py:99
  28.7 5.6 %copy-start.11 = (s32[32]{0:T(128)S(1)}, s32[32]{0:T(128)}, u32[]{:S(2)}) copy-start(s32[32]{0:T(128)} %param.25) | copy-start | bytes 388
  28.7 6.9 %copy-start.12 = (s32[32]{0:T(128)S(1)}, s32[32]{0:T(128)}, u32[]{:S(2)}) copy-start(s32[32]{0:T(128)} %param.26) | copy-start | bytes 388
  28.7 9.2 %copy-start.5 = (bf16[2048,256]{1,0:T(8,128)(2,1)S(1)}, bf16[2048,256]{1,0:T(8,128)(2,1)}, u32[]{:S(2)}) copy-start(bf16[2048,256]{1,0:T(8,128)(2,1)} %param.18) | copy-start | bytes 3145732
  28.7 13.0 %copy-start.9 = (s32[1,256]{1,0:T(1,128)S(1)}, s32[1,256]{1,0:T(1,128)}, u32[]{:S(2)}) copy-start(s32[1,256]{1,0:T(1,128)} %param.27) | copy-start | bytes 3076
  28.7 13.0 %copy-start.3 = (bf16[1,256,2048]{2,1,0:T(8,128)(2,1)S(1)}, bf16[1,256,2048]{2,1,0:T(8,128)(2,1)}, u32[]{:S(2)}) copy-start(bf16[1,256,2048]{2,1,0:T(8,128)(2,1)} %param.23) | copy-start | bytes 3145732
  28.7 261.2 %reduce-scatter.2.cloned.1.call-start = ((), (), s32[]{:S(2)}) async-start(), calls=%async_computation.3 | async-start | bytes 4718592 | tf_op jit(solution)/shard_map/reduce_scatter | solution.py:150
  32.9 85.2 %collective-permute-start = (bf16[2,2048,256]{1,2,0:T(8,128)(2,1)}, bf16[2,2048,256]{1,2,0:T(8,128)(2,1)}, u32[]{:S(2)}, u32[]{:S(2)}) collective-permute-start(bf16[2,2048,256]{1,2,0:T(8,128)(2,1)} %bitcast.148), channel_id=1, source_target_pairs={{0,128},{8,136},{16,144},{24,152},{32,160},{40,168},{48,176},{56,1... | collective-permute-start | bytes 6291464 | tf_op jit(solution)/shard_map/ppermute | solution.py:16
  39.4 3.0 copy-start.7
  54.8 85.7 %copy-start.1 = (pred[1024,1024]{0,1:T(8,128)(4,1)}, pred[1024,1024]{0,1:T(8,128)(4,1)S(1)}, u32[]{:S(2)}) copy-start(pred[1024,1024]{0,1:T(8,128)(4,1)S(1)} %iota_compare_fusion) | copy-start | bytes 3145732
  129.7 2.9 copy-start.8
  132.6 1.3 copy-start.6
  136.4 0.7 copy-start.4
  142.4 3.2 copy-start.10
  145.6 1.3 copy-start.2
Sparse Core Ops, SparseCore 0:
  165.5 124.3 reduce-scatter.1
where the time goes:
time: 336 us; the launch traced here: 334 us
  waiting for transfers between devices  189 us (56%)
  local copies, waits for them, and re-layouts  35.7 us (11%)
  other arithmetic  30.9 us (9%)
  blocking collectives  25.2 us (8%)
  matrix products  24.2 us (7%)
  between operations  16.2 us (5%)
  starting transfers between devices  12.5 us (4%)
    reduce_scatter x1, waiting for transfers between devices, shards(): lax.psum_scatter(partial_value, 'tp', scatter_dimension=1, tiled=True)  125 us
    ppermute x1, waiting for transfers between devices, swapped(): return lax.ppermute(value, axis, pairs)  62.3 us
    all_to_all x1, blocking collectives, shards(): lax.all_to_all(mixed_rows[None], 'grp', split_axis=1, concat_axis=0, tile...  25.2 us
    all_to_all x1, starting transfers between devices, shards(): lax.all_to_all(arranged, 'grp', split_axis=0, concat_axis=1, tiled=True)  11.1 us
    dot_general x3, matrix products, absorb(): jnp.einsum('hqk,khd->qhd', expanded.astype(jnp.bfloat16), value_rows, pre...  7.46 us
    dot_general x3, matrix products, absorb(): jnp.einsum('qhd,khd->hqk', queries, key_rows, preferred_element_type=jnp....  7.03 us
  transfers between devices with their start and end apart: 3, of which 3 were waited for; matrix products, arithmetic and copies ran while one was open for 8% of the time, Pallas kernels for 0%

commit v1 on v0

--- a/solution.py
+++ b/solution.py
@@ -61,7 +61,7 @@
     return (new_max, weight_sum, numerator)
 
 
-def sweep_keys(softmax_state, queries, key_rows, value_rows, live_count):
+def sweep_keys(softmax_state, queries, key_rows, value_rows, live_count, skip=None):
     block_len = min(512, key_rows.shape[0])
     block_count = (live_count + block_len - 1) // block_len
 
@@ -70,6 +70,8 @@
         key_block = lax.dynamic_slice_in_dim(key_rows, block_start, block_len, 0)
         value_block = lax.dynamic_slice_in_dim(value_rows, block_start, block_len, 0)
         is_valid = block_start + jnp.arange(block_len, dtype=jnp.int32) < live_count
+        if skip is not None:
+            is_valid = is_valid & ~lax.dynamic_slice_in_dim(skip, block_start, block_len, 0)
         return absorb(carried, queries, key_block, value_block, is_valid[None, :])
 
     return lax.fori_loop(jnp.int32(0), block_count, visit_block, softmax_state)
@@ -95,29 +97,43 @@
     swap_bit = groups.bit_length() - 2
     local_width = w_query.shape[1]
     local_heads = local_width // HEAD_DIM
-    arranged = jnp.take(tokens, deal_order, axis=0)
-    dealt_rows = lax.all_to_all(arranged, "grp", split_axis=0, concat_axis=1, tiled=True)
-    token_rows = dealt_rows[0]
-    span_len = token_rows.shape[0]
+    requests, local_rows, model_width = tokens.shape
+
+    fetched = swapped(guest_cache[0], "grp", swap_bit)
+
+    server = jnp.zeros_like(deal_order).at[deal_order].set(jnp.arange(groups, dtype=jnp.int32))
+    start_of = own_len[server] + guest_len[(server + groups // 2) % groups]
+    local_positions = (
+        start_of[:, None] + group_id * local_rows + jnp.arange(local_rows, dtype=jnp.int32)[None, :]
+    ).reshape(-1)
+
+    normed = layer_norm(tokens.reshape(-1, model_width)).astype(jnp.bfloat16)
+    queries = rotate(
+        jnp.dot(normed, w_query, preferred_element_type=jnp.float32), local_positions, HEAD_DIM
+    ).astype(jnp.bfloat16)
+    new_keys = rotate(
+        jnp.dot(normed, w_key, preferred_element_type=jnp.float32), local_positions, HEAD_DIM
+    ).astype(jnp.bfloat16)
+    new_values = jnp.dot(normed, w_value, preferred_element_type=jnp.float32).astype(jnp.bfloat16)
+    projected = jnp.concatenate([queries, new_keys, new_values], axis=-1).reshape(
+        requests, local_rows, 3 * local_width
+    )
+    arranged = jnp.take(projected, deal_order, axis=0)
+    dealt = lax.all_to_all(arranged, "grp", split_axis=0, concat_axis=1, tiled=True)[0]
+    span_len = dealt.shape[0]
+    queries = dealt[:, :local_width]
+    new_keys = dealt[:, local_width : 2 * local_width]
+    new_values = dealt[:, 2 * local_width :]
+
     own_count = own_len[group_id]
     guest_count = guest_len[partner_id]
-    positions = own_count + guest_count + jnp.arange(span_len, dtype=jnp.int32)
-    normed = layer_norm(token_rows).astype(jnp.bfloat16)
-    queries = rotate(
-        jnp.dot(normed, w_query, preferred_element_type=jnp.float32), positions, HEAD_DIM
-    ).astype(jnp.bfloat16)
-    new_keys = rotate(
-        jnp.dot(normed, w_key, preferred_element_type=jnp.float32), positions, HEAD_DIM
-    ).astype(jnp.bfloat16)
-    new_values = jnp.dot(normed, w_value, preferred_element_type=jnp.float32).astype(jnp.bfloat16)
     rec_rows = layer_norm(rec_hidden[0]).astype(jnp.bfloat16)
     rec_positions = rec_index[0]
     rec_keys = rotate(
         jnp.dot(rec_rows, w_key, preferred_element_type=jnp.float32), rec_positions, HEAD_DIM
     ).astype(jnp.bfloat16)
     rec_values = jnp.dot(rec_rows, w_value, preferred_element_type=jnp.float32).astype(jnp.bfloat16)
-    cached_keys = own_cache[0, 0].at[rec_positions].set(rec_keys)
-    cached_values = own_cache[0, 1].at[rec_positions].set(rec_values)
+    replaced = jnp.zeros((own_cache.shape[2],), jnp.bool_).at[rec_positions].set(True)
 
     def by_head(matrix):
         return matrix.reshape(matrix.shape[0], local_heads, HEAD_DIM)
@@ -130,10 +146,21 @@
     causal = jnp.arange(span_len)[None, :] <= jnp.arange(span_len)[:, None]
     query_heads = by_head(queries)
     softmax_state = absorb(empty_state, query_heads, by_head(new_keys), by_head(new_values), causal)
+    softmax_state = absorb(
+        softmax_state,
+        query_heads,
+        by_head(rec_keys),
+        by_head(rec_values),
+        jnp.ones((1, rec_keys.shape[0]), jnp.bool_),
+    )
     softmax_state = sweep_keys(
-        softmax_state, query_heads, by_head(cached_keys), by_head(cached_values), own_count
-    )
-    fetched = swapped(guest_cache[0], "grp", swap_bit)
+        softmax_state,
+        query_heads,
+        by_head(own_cache[0, 0]),
+        by_head(own_cache[0, 1]),
+        own_count,
+        replaced,
+    )
     softmax_state = sweep_keys(
         softmax_state, query_heads, by_head(fetched[0]), by_head(fetched[1]), guest_count
     )
@@ -147,12 +174,15 @@
     partial_value = jnp.dot(attended, w_out, preferred_element_type=jnp.float32).astype(
         jnp.bfloat16
     )
-    summed = lax.psum_scatter(partial_value, "tp", scatter_dimension=1, tiled=True).astype(
-        jnp.float32
-    )
-    mixed_rows = summed.astype(jnp.bfloat16)
-    returned_rows = lax.all_to_all(mixed_rows[None], "grp", split_axis=1, concat_axis=0, tiled=True)
-    return jnp.zeros_like(returned_rows).at[deal_order].set(returned_rows)
+    blocks = lax.axis_size("tp")
+    exchanged = lax.all_to_all(
+        partial_value.reshape(span_len, blocks, -1), "tp", split_axis=1, concat_axis=1, tiled=True
+    )
+    mixed_rows = exchanged.astype(jnp.float32).sum(axis=1).astype(jnp.bfloat16)
+    returned_rows = lax.all_to_all(
+        mixed_rows.reshape(groups, local_rows, -1), "grp", split_axis=0, concat_axis=0, tiled=True
+    )
+    return jnp.take(returned_rows, server, axis=0)
 
 
 def solution(mesh):

time: 336 us -> 249 us (0.74)
  waiting for transfers between devices: 189 us -> 57.8 us
  starting transfers between devices: 12.5 us -> 42.5 us
  matrix products: 24.2 us -> 42.1 us
  between operations: 16.2 us -> 1.78 us
  blocking collectives: 25.2 us -> 35 us
  other arithmetic: 30.9 us -> 35.7 us
    reduce_scatter x1 -> x0, waiting for transfers between devices: 125 us -> none  [shards(): lax.psum_scatter(partial_value, 'tp', scatter_dimension=1, tiled=True)]
    all_to_all x1 -> x2, starting transfers between devices: 11.1 us -> 41.1 us  [the longest x1 30 us: shards(): lax.all_to_all(mixed_rows.reshape(groups, local_rows, -1), 'grp', split_a...]
    ppermute x1, waiting for transfers between devices: 62.3 us -> 41.3 us  [swapped(): return lax.ppermute(value, axis, pairs)]
    all_to_all x1 -> x2, waiting for transfers between devices: 2.14 us -> 16.6 us  [the longest x1 16.6 us: shards(): lax.all_to_all(mixed_rows.reshape(groups, local_rows, -1), 'grp', split_a...]
    slice x0 -> x6, local copies, waits for them, and re-layouts: none -> 9.89 us  [the longest x2 5.33 us: shards(): own_cache[0, 1]]
    all_to_all x1, blocking collectives: 25.2 us -> 35 us  [shards(): lax.all_to_all(partial_value.reshape(span_len, blocks, -1), 'tp', split_a...]
    scatter x5 -> x2, local copies, waits for them, and re-layouts: 11.6 us -> 2.16 us  [the longest x1 1.48 us: shards(): jnp.zeros((own_cache.shape[2],), jnp.bool_).at[rec_positions].set(True)]
    dot_general x3 -> x6, matrix products: 7.03 us -> 16.2 us  [absorb(): jnp.einsum('qhd,khd->hqk', queries, key_rows, preferred_element_type=jnp....]
  transfers between devices with their start and end apart: 3 -> 3, of which waited for: 3 -> 2; matrix products, arithmetic and copies ran while one was open for 8% -> 10% of each run, Pallas kernels for 0% -> 0%
where the time goes in v1:
time: 249 us; the launch traced here: 248 us
  waiting for transfers between devices  57.8 us (23%)
  starting transfers between devices  42.5 us (17%)
  matrix products  42.1 us (17%)
  other arithmetic  35.7 us (14%)
  blocking collectives  35 us (14%)
  local copies, waits for them, and re-layouts  32.7 us (13%)
    ppermute x1, waiting for transfers between devices, swapped(): return lax.ppermute(value, axis, pairs)  41.3 us
    all_to_all x1, blocking collectives, shards(): lax.all_to_all(partial_value.reshape(span_len, blocks, -1), 'tp', split_a...  35 us
    all_to_all x1, starting transfers between devices, shards(): lax.all_to_all(mixed_rows.reshape(groups, local_rows, -1), 'grp', split_a...  30 us
    all_to_all x1, waiting for transfers between devices, shards(): lax.all_to_all(mixed_rows.reshape(groups, local_rows, -1), 'grp', split_a...  16.6 us
    dot_general x6, matrix products, absorb(): jnp.einsum('qhd,khd->hqk', queries, key_rows, preferred_element_type=jnp....  16.2 us
    dot_general x6, matrix products, absorb(): jnp.einsum('hqk,khd->qhd', expanded.astype(jnp.bfloat16), value_rows, pre...  15.1 us
    all_to_all x1, starting transfers between devices, shards(): lax.all_to_all(arranged, 'grp', split_axis=0, concat_axis=1, tiled=True)[0]  11.1 us
    reduce_sum x6, other arithmetic, absorb(): weight_sum = weight_sum * factor + jnp.sum(expanded, axis=-1)  10.3 us
  transfers between devices with their start and end apart: 3, of which 2 were waited for; matrix products, arithmetic and copies ran while one was open for 10% of the time, Pallas kernels for 0%

profile of v1, /device:TPU:1, one launch (start us, length us, event | category | flops | bytes accessed | tf_op | source)
XLA Modules:
  0.0 248.0 jit_solution(4990457965109336415)
XLA Ops:
  0.0 3.0 %convert_reduce_fusion = f32[32,32]{1,0:T(8,128)S(1)} fusion(bf16[32,32,2048]{2,1,0:T(8,128)(2,1)} %param.16), kind=kLoop, calls=%fused_computation.62 | loop fusion | flops 4193280 | bytes 4198400 | tf_op jit(solution)/shard_map/reduce_sum | solution.py:21
  5.0 4.2 %multiply_convert_fusion = bf16[32,32,2048]{2,1,0:T(8,128)(2,1)} fusion(bf16[32,32,2048]{2,1,0:T(8,128)(2,1)} %param.16, f32[32,32]{1,0:T(8,128)S(1)} %add_rsqrt_fusion, f32[32,32]{1,0:T(8,128)S(1)} %broadcast_multiply_fusion), kind=kLoop, calls=%fused_computation.60 | loop fusion | flops 8388608 | bytes 8396800 | tf_op jit(solution)/shard_map/convert_element_type | solution.py:110
  13.7 4.2 %fusion.104 = f32[1024,2,128]{0,2,1:T(8,128)S(1)} fusion(bf16[1024,2048,1]{1,0,2:T(8,128)(2,1)} %bitcast.167, bf16[2,128,2048]{2,1,0:T(8,128)(2,1)} %bitcast.178), kind=kOutput, calls=%fused_computation.157 | convolution fusion | flops 1073741824 | bytes 6291456 | tf_op jit(solution)/shard_map/dot_general | solution.py:112
  25.8 2.1 gather_fusion.2
  29.3 11.1 %all-to-all-start = ((bf16[32,32,768]{2,1,0:T(8,128)(2,1)}), bf16[32,32,768]{2,1,0:T(8,128)(2,1)S(1)}, u32[]{:S(2)}, u32[]{:S(2)}) async-start(bf16[32,32,768]{2,1,0:T(8,128)(2,1)} %broadcast_select_fusion), calls=%async_computation | async-start | bytes 3145728 | tf_op jit(solution)/shard_map/all_to_all | solution.py:122
  40.4 4.0 %copy.64 = bf16[1,2,2048,256]{2,3,1,0:T(8,128)(2,1)} copy(bf16[1,2,2048,256]{3,2,1,0:T(8,128)(2,1)} %param.22) | data formatting | bytes 4194304 | tf_op args[6]
  45.8 3.1 %fusion.102 = (bf16[1,1,2048,256]{3,2,1,0:T(8,128)(2,1)}, bf16[1,1,2048,256]{3,2,1,0:T(8,128)(2,1)}) fusion(bf16[1,2,2048,256]{3,2,1,0:T(8,128)(2,1)} %param.21), kind=kLoop, calls=%fused_computation.155 | loop fusion | bytes 4194304 | tf_op jit(solution)/shard_map/slice | solution.py:160
  51.4 2.3 copy.80
  53.7 2.3 copy.61
  62.3 2.1 fusion.77
  65.2 41.3 %collective-permute-done = bf16[2,2048,256]{1,2,0:T(8,128)(2,1)} collective-permute-done((bf16[2,2048,256]{1,2,0:T(8,128)(2,1)}, bf16[2,2048,256]{1,2,0:T(8,128)(2,1)}, u32[]{:S(2)}, u32[]{:S(2)}) %collective-permute-start) | collective-permute-done | bytes 2097184 | tf_op jit(solution)/shard_map/ppermute | solution.py:16
  106.5 3.1 %fusion.101 = (bf16[1,2048,256]{1,2,0:T(8,128)(2,1)}, bf16[1,2048,256]{1,2,0:T(8,128)(2,1)}) fusion(bf16[2,2048,256]{1,2,0:T(8,128)(2,1)} %collective-permute-done), kind=kLoop, calls=%fused_computation.154 | loop fusion | bytes 4194304 | tf_op jit(solution)/shard_map/slice | solution.py:165
  113.1 6.3 %fusion.49 = (f32[2,1024]{1,0:T(2,128)S(1)}, f32[2,1024,1024]{1,2,0:T(8,128)}) fusion(pred[1024,1024]{0,1:T(8,128)(4,1)} %iota_compare_fusion, bf16[1024,2,128]{0,2,1:T(8,128)(2,1)S(1)} %bitcast.164, bf16[1024,2,128]{0,2,1:T(8,128)(2,1)S(1)} %bitcast.180), kind=kOutput, calls=%fused_computation.63 | convolution fusion | flops 543160320 | bytes 10493952 | tf_op jit(solution)/shard_map/qhd,khd->hqk/dot_general | solution.py:46
  121.7 4.7 %fusion.51 = f32[2,1024]{1,0:T(2,128)S(1)} fusion(f32[2,1024,1024]{1,2,0:T(8,128)} %get-tuple-element.222, f32[2,1024]{1,0:T(2,128)S(1)} %get-tuple-element.221, pred[1024,1024]{0,1:T(8,128)(4,1)} %iota_compare_fusion), kind=kLoop, calls=%fused_computation.65 | loop fusion | flops 8386560 | bytes 9453568 | tf_op jit(solution)/shard_map/reduce_sum | solution.py:53
  129.4 5.2 %fusion.71 = f32[1024,2,128]{0,2,1:T(8,128)S(1)} fusion(bf16[1024,2,128]{0,2,1:T(8,128)(2,1)} %bitcast.179, f32[2,1024,1024]{1,2,0:T(8,128)} %get-tuple-element.222, f32[2,1024]{1,0:T(2,128)S(1)} %get-tuple-element.221, pred[1024,1024]{0,1:T(8,128)(4,1)S(1)} %copy-done.6, f32[1024,2]{0,1:T(2,128)S(1)} %get-tuple-element.214, ...), kind=kOutput, calls=%fused_computation.91 | convolution fusion | flops 545783808 | bytes 11034624 | tf_op jit(solution)/shard_map/hqk,khd->qhd/dot_general | solution.py:54
  135.2 24.3 %while.28 = (s32[]{:T(128)}, f32[2,1024]{1,0:T(2,128)S(1)}, f32[2,1024]{1,0:T(2,128)S(1)}, f32[1024,2,128]{0,2,1:T(8,128)S(1)}, s32[]{:T(128)}, /*index=5*/s32[]...) while((s32[]{:T(128)}, f32[2,1024]{1,0:T(2,128)S(1)}, ...), condition=%wide.region_13.14_spmd, body=%wide.region_10.13_spmd.sunk | while | flops 548937728 | bytes 15862479 | solution.py:77
  139.1 2.3 fusion.142
  145.1 2.3 fusion.142
  151.2 2.3 fusion.142
  157.2 2.3 fusion.142
  161.3 35.0 %all_to_all.19 = bf16[1024,8,256]{2,0,1:T(8,128)(2,1)} all-to-all(bf16[1024,8,256]{2,0,1:T(8,128)(2,1)S(1)} %bitcast.157), channel_id=1, replica_groups=mesh['grp'=32,'tp'=8] {'tp'}, dimensions={1} | all-to-all | bytes 8388608 | tf_op jit(solution)/shard_map/all_to_all | solution.py:178
  196.2 3.7 %reduce_sum.90 = bf16[1024,256]{1,0:T(8,128)(2,1)} reduce(bf16[1024,8,256]{2,0,1:T(8,128)(2,1)} %all_to_all.19, bf16[]{:T(256)} %constant.147.clone.1), dimensions={1}, to_apply=%region_18.19 | reduce | flops 1835008 | bytes 4718594 | tf_op jit(solution)/shard_map/reduce_sum | solution.py:181
  199.9 30.0 %all-to-all-start.2 = ((bf16[32,32,256]{2,1,0:T(8,128)(2,1)}), bf16[32,32,256]{2,1,0:T(8,128)(2,1)S(1)}, u32[]{:S(2)}, u32[]{:S(2)}) async-start(bf16[32,32,256]{2,1,0:T(8,128)(2,1)} %bitcast.40), calls=%async_computation.2 | async-start | bytes 1048576 | tf_op jit(solution)/shard_map/all_to_all | solution.py:182
  230.0 16.6 %all-to-all-done.2 = bf16[32,32,256]{2,1,0:T(8,128)(2,1)S(1)} async-done(((bf16[32,32,256]{2,1,0:T(8,128)(2,1)}), bf16[32,32,256]{2,1,0:T(8,128)(2,1)S(1)}, u32[]{:S(2)}, u32[]{:S(2)}) %all-to-all-start.2) | async-done | bytes 524320 | tf_op jit(solution)/shard_map/all_to_all | solution.py:182
  (120 shorter events, 52.4 us)
Async XLA Ops:
  0.0 159.7 %copy-start = (bf16[256,2048]{1,0:T(8,128)(2,1)S(1)}, bf16[256,2048]{1,0:T(8,128)(2,1)}, u32[]{:S(2)}) copy-start(bf16[256,2048]{1,0:T(8,128)(2,1)} %param.20) | copy-start | bytes 3145732
  0.0 3.5 %copy-start.3 = (bf16[32,32,2048]{2,1,0:T(8,128)(2,1)S(1)}, bf16[32,32,2048]{2,1,0:T(8,128)(2,1)}, u32[]{:S(2)}) copy-start(bf16[32,32,2048]{2,1,0:T(8,128)(2,1)} %param.16) | copy-start | bytes 12582916
  4.9 4.3 %copy-start.15 = (s32[32]{0:T(128)S(1)}, s32[32]{0:T(128)}, u32[]{:S(2)}) copy-start(s32[32]{0:T(128)} %param.24) | copy-start | bytes 388
  4.9 4.3 %copy-start.9 = (bf16[2048,256]{1,0:T(8,128)(2,1)S(1)}, bf16[2048,256]{1,0:T(8,128)(2,1)}, u32[]{:S(2)}) copy-start(bf16[2048,256]{1,0:T(8,128)(2,1)} %param.17) | copy-start | bytes 3145732
  5.0 6.5 %copy-start.1 = (s32[32]{0:T(128)S(1)}, s32[32]{0:T(128)}, u32[]{:S(2)}) copy-start(s32[32]{0:T(128)} %param.25) | copy-start | bytes 388
  5.0 7.2 %copy-start.2 = (s32[32]{0:T(128)S(1)}, s32[32]{0:T(128)}, u32[]{:S(2)}) copy-start(s32[32]{0:T(128)} %param.26) | copy-start | bytes 388
  5.0 8.0 %copy-start.10 = (bf16[2048,256]{1,0:T(8,128)(2,1)S(1)}, bf16[2048,256]{1,0:T(8,128)(2,1)}, u32[]{:S(2)}) copy-start(bf16[2048,256]{1,0:T(8,128)(2,1)} %param.18) | copy-start | bytes 3145732
  13.7 5.5 %copy-start.11 = (bf16[256,2048]{1,0:T(8,128)(2,1)}, bf16[256,2048]{1,0:T(8,128)(2,1)S(1)}, u32[]{:S(2)}) copy-start(bf16[256,2048]{1,0:T(8,128)(2,1)S(1)} %copy.77) | copy-start | bytes 3145732
  13.7 4.2 %copy-start.7 = (bf16[32,32,2048]{2,1,0:T(8,128)(2,1)S(1)}, bf16[32,32,2048]{2,1,0:T(8,128)(2,1)}, u32[]{:S(2)}) copy-start(bf16[32,32,2048]{2,1,0:T(8,128)(2,1)} %multiply_convert_fusion) | copy-start | bytes 12582916
  17.9 2.2 copy-start.4
  20.1 1.3 copy-start.13
  29.3 80.3 %all-to-all-start = ((bf16[32,32,768]{2,1,0:T(8,128)(2,1)}), bf16[32,32,768]{2,1,0:T(8,128)(2,1)S(1)}, u32[]{:S(2)}, u32[]{:S(2)}) async-start(bf16[32,32,768]{2,1,0:T(8,128)(2,1)} %broadcast_select_fusion), calls=%async_computation | async-start | bytes 3145728 | tf_op jit(solution)/shard_map/all_to_all | solution.py:122
  40.3 8.5 %copy-start.12 = (s32[1,256]{1,0:T(1,128)S(1)}, s32[1,256]{1,0:T(1,128)}, u32[]{:S(2)}) copy-start(s32[1,256]{1,0:T(1,128)} %param.27) | copy-start | bytes 3076
  44.4 62.1 %collective-permute-start = (bf16[2,2048,256]{1,2,0:T(8,128)(2,1)}, bf16[2,2048,256]{1,2,0:T(8,128)(2,1)}, u32[]{:S(2)}, u32[]{:S(2)}) collective-permute-start(bf16[2,2048,256]{1,2,0:T(8,128)(2,1)} %bitcast.170), channel_id=1, source_target_pairs={{0,128},{8,136},{16,144},{24,152},{32,160},{40,168},{48,176},{56,1... | collective-permute-start | bytes 6291464 | tf_op jit(solution)/shard_map/ppermute | solution.py:16
  57.4 7.0 %copy-start.8 = (bf16[1,256,2048]{2,1,0:T(8,128)(2,1)S(1)}, bf16[1,256,2048]{2,1,0:T(8,128)(2,1)}, u32[]{:S(2)}) copy-start(bf16[1,256,2048]{2,1,0:T(8,128)(2,1)} %param.23) | copy-start | bytes 3145732
  57.5 7.0 %copy-start.14 = (bf16[2048,256]{1,0:T(8,128)(2,1)S(1)}, bf16[2048,256]{1,0:T(8,128)(2,1)}, u32[]{:S(2)}) copy-start(bf16[2048,256]{1,0:T(8,128)(2,1)} %param.19) | copy-start | bytes 3145732
  121.7 7.7 %copy-start.6 = (pred[1024,1024]{0,1:T(8,128)(4,1)S(1)}, pred[1024,1024]{0,1:T(8,128)(4,1)}, u32[]{:S(2)}) copy-start(pred[1024,1024]{0,1:T(8,128)(4,1)} %iota_compare_fusion) | copy-start | bytes 3145732
  129.4 5.2 %copy-start.5 = (f32[2,1024,256]{1,2,0:T(8,128)S(1)}, f32[2,1024,256]{1,2,0:T(8,128)}, u32[]{:S(2)}) copy-start(f32[2,1024,256]{1,2,0:T(8,128)} %get-tuple-element.224) | copy-start | bytes 6291460
  199.9 46.6 %all-to-all-start.2 = ((bf16[32,32,256]{2,1,0:T(8,128)(2,1)}), bf16[32,32,256]{2,1,0:T(8,128)(2,1)S(1)}, u32[]{:S(2)}, u32[]{:S(2)}) async-start(bf16[32,32,256]{2,1,0:T(8,128)(2,1)} %bitcast.40), calls=%async_computation.2 | async-start | bytes 1048576 | tf_op jit(solution)/shard_map/all_to_all | solution.py:182

commit v2 on v1

--- a/solution.py
+++ b/solution.py
@@ -1,9 +1,70 @@
 import jax
 import jax.numpy as jnp
 from jax import lax
+from jax.experimental import pallas as pl
+from jax.experimental.pallas import tpu as pltpu
 from jax.sharding import PartitionSpec as P
 
 HEAD_DIM = 128
+
+
+FLOOR = -1e30
+
+
+def flash_step(flags_ref, qrow_ref, rank_ref, q_ref, k_ref, v_ref, m_in, l_in, acc_in, m_out, l_out, acc_out):
+    kb = pl.program_id(1)
+
+    @pl.when(kb == 0)
+    def _():
+        m_out[...] = m_in[...]
+        l_out[...] = l_in[...]
+        acc_out[...] = acc_in[...]
+
+    @pl.when(flags_ref[kb] > 0)
+    def _():
+        scores = lax.dot_general(
+            q_ref[...], k_ref[...], (((1,), (1,)), ((), ())), preferred_element_type=jnp.float32
+        ) * (HEAD_DIM ** -0.5)
+        scores = jnp.where(rank_ref[...] <= qrow_ref[...], scores, FLOOR)
+        m_prev = m_out[...]
+        m_new = jnp.maximum(m_prev, jnp.max(scores, axis=1, keepdims=True))
+        factor = jnp.exp(m_prev - m_new)
+        expanded = jnp.exp(scores - m_new[:, :1])
+        l_out[...] = factor * l_out[...] + jnp.sum(expanded, axis=1, keepdims=True)
+        acc_out[...] = factor * acc_out[...] + jnp.dot(
+            expanded.astype(jnp.bfloat16), v_ref[...], preferred_element_type=jnp.float32
+        )
+        m_out[...] = m_new
+
+
+def attend(state, flags, qrow, rank, q_src, k_src, k_map, v_src, v_map, key_count, heads, block_len):
+    query_count = qrow.shape[0]
+    state_spec = pl.BlockSpec((query_count, HEAD_DIM), lambda h, kb, f: (0, h))
+    k_block = (block_len, HEAD_DIM) if k_src.ndim == 2 else (None, block_len, HEAD_DIM)
+    v_block = (block_len, HEAD_DIM) if v_src.ndim == 2 else (None, block_len, HEAD_DIM)
+    grid_spec = pltpu.PrefetchScalarGridSpec(
+        num_scalar_prefetch=1,
+        grid=(heads, key_count // block_len),
+        in_specs=[
+            pl.BlockSpec((query_count, 1), lambda h, kb, f: (0, 0)),
+            pl.BlockSpec((1, block_len), lambda h, kb, f: (0, kb)),
+            pl.BlockSpec((query_count, HEAD_DIM), lambda h, kb, f: (0, h)),
+            pl.BlockSpec(k_block, lambda h, kb, f: k_map(h, kb)),
+            pl.BlockSpec(v_block, lambda h, kb, f: v_map(h, kb)),
+            state_spec,
+            state_spec,
+            state_spec,
+        ],
+        out_specs=[state_spec, state_spec, state_spec],
+    )
+    shape = jax.ShapeDtypeStruct(state[0].shape, jnp.float32)
+    return pl.pallas_call(
+        flash_step,
+        grid_spec=grid_spec,
+        out_shape=[shape, shape, shape],
+        input_output_aliases={6: 0, 7: 1, 8: 2},
+        compiler_params=pltpu.CompilerParams(dimension_semantics=("arbitrary", "arbitrary")),
+    )(flags, qrow, rank, q_src, k_src, v_src, *state)
 
 
 rope_base = 10000.0
@@ -37,44 +98,6 @@
         axis=-1,
     )
     return turned.reshape(projected.shape)
-
-
-def absorb(softmax_state, queries, key_rows, value_rows, is_valid):
-    running_max, weight_sum, numerator = softmax_state
-    score_scale = queries.shape[-1] ** (-0.5)
-    scores = (
-        jnp.einsum("qhd,khd->hqk", queries, key_rows, preferred_element_type=jnp.float32)
-        * score_scale
-    )
-    scores = jnp.where(is_valid[None], scores, -jnp.inf)
-    new_max = jnp.maximum(running_max, jnp.max(scores, axis=-1))
-    factor = jnp.exp(running_max - new_max)
-    expanded = jnp.exp(scores - new_max[..., None])
-    weight_sum = weight_sum * factor + jnp.sum(expanded, axis=-1)
-    product = jnp.einsum(
-        "hqk,khd->qhd",
-        expanded.astype(jnp.bfloat16),
-        value_rows,
-        preferred_element_type=jnp.float32,
-    )
-    numerator = numerator * jnp.transpose(factor)[:, :, None] + product
-    return (new_max, weight_sum, numerator)
-
-
-def sweep_keys(softmax_state, queries, key_rows, value_rows, live_count, skip=None):
-    block_len = min(512, key_rows.shape[0])
-    block_count = (live_count + block_len - 1) // block_len
-
-    def visit_block(block_index, carried):
-        block_start = block_index * block_len
-        key_block = lax.dynamic_slice_in_dim(key_rows, block_start, block_len, 0)
-        value_block = lax.dynamic_slice_in_dim(value_rows, block_start, block_len, 0)
-        is_valid = block_start + jnp.arange(block_len, dtype=jnp.int32) < live_count
-        if skip is not None:
-            is_valid = is_valid & ~lax.dynamic_slice_in_dim(skip, block_start, block_len, 0)
-        return absorb(carried, queries, key_block, value_block, is_valid[None, :])
-
-    return lax.fori_loop(jnp.int32(0), block_count, visit_block, softmax_state)
 
 
 def shards(
@@ -121,9 +144,6 @@
     arranged = jnp.take(projected, deal_order, axis=0)
     dealt = lax.all_to_all(arranged, "grp", split_axis=0, concat_axis=1, tiled=True)[0]
     span_len = dealt.shape[0]
-    queries = dealt[:, :local_width]
-    new_keys = dealt[:, local_width : 2 * local_width]
-    new_values = dealt[:, 2 * local_width :]
 
     own_count = own_len[group_id]
     guest_count = guest_len[partner_id]
@@ -135,42 +155,46 @@
     rec_values = jnp.dot(rec_rows, w_value, preferred_element_type=jnp.float32).astype(jnp.bfloat16)
     replaced = jnp.zeros((own_cache.shape[2],), jnp.bool_).at[rec_positions].set(True)
 
-    def by_head(matrix):
-        return matrix.reshape(matrix.shape[0], local_heads, HEAD_DIM)
-
-    empty_state = (
-        jnp.full((local_heads, span_len), -jnp.inf, jnp.float32),
-        jnp.zeros((local_heads, span_len), jnp.float32),
-        jnp.zeros((span_len, local_heads, HEAD_DIM), jnp.float32),
-    )
-    causal = jnp.arange(span_len)[None, :] <= jnp.arange(span_len)[:, None]
-    query_heads = by_head(queries)
-    softmax_state = absorb(empty_state, query_heads, by_head(new_keys), by_head(new_values), causal)
-    softmax_state = absorb(
-        softmax_state,
-        query_heads,
-        by_head(rec_keys),
-        by_head(rec_values),
-        jnp.ones((1, rec_keys.shape[0]), jnp.bool_),
-    )
-    softmax_state = sweep_keys(
-        softmax_state,
-        query_heads,
-        by_head(own_cache[0, 0]),
-        by_head(own_cache[0, 1]),
-        own_count,
-        replaced,
-    )
-    softmax_state = sweep_keys(
-        softmax_state, query_heads, by_head(fetched[0]), by_head(fetched[1]), guest_count
-    )
-    weight_sum = softmax_state[1]
-    numerator = softmax_state[2]
-    attended = (
-        (numerator / jnp.transpose(weight_sum)[:, :, None])
-        .astype(jnp.bfloat16)
-        .reshape(span_len, local_width)
-    )
+    heads = local_heads
+    query_rows = jnp.arange(span_len, dtype=jnp.int32)[:, None]
+    never = jnp.int32(1 << 30)
+    state = (
+        jnp.full((span_len, local_width), FLOOR, jnp.float32),
+        jnp.zeros((span_len, local_width), jnp.float32),
+        jnp.zeros((span_len, local_width), jnp.float32),
+    )
+    state = attend(
+        state, jnp.ones((2,), jnp.int32), query_rows,
+        jnp.arange(span_len, dtype=jnp.int32)[None, :],
+        dealt, dealt, lambda h, kb: (kb, heads + h), dealt, lambda h, kb: (kb, 2 * heads + h),
+        span_len, heads, span_len // 2,
+    )
+    rec_count = rec_keys.shape[0]
+    state = attend(
+        state, jnp.ones((1,), jnp.int32), query_rows, jnp.full((1, rec_count), -1, jnp.int32),
+        dealt, rec_keys, lambda h, kb: (kb, h), rec_values, lambda h, kb: (kb, h),
+        rec_count, heads, rec_count,
+    )
+    cap = own_cache.shape[2]
+    block_len = 512
+    key_rows = jnp.arange(cap, dtype=jnp.int32)
+    own_rank = jnp.where((key_rows < own_count) & ~replaced, -1, never)[None, :]
+    own_flags = (jnp.arange(cap // block_len, dtype=jnp.int32) * block_len < own_count).astype(jnp.int32)
+    state = attend(
+        state, own_flags, query_rows, own_rank,
+        dealt, own_cache[0], lambda h, kb: (0, kb, h), own_cache[0], lambda h, kb: (1, kb, h),
+        cap, heads, block_len,
+    )
+    gcap = fetched.shape[1]
+    guest_rows = jnp.arange(gcap, dtype=jnp.int32)
+    guest_rank = jnp.where(guest_rows < guest_count, -1, never)[None, :]
+    guest_flags = (jnp.arange(gcap // block_len, dtype=jnp.int32) * block_len < guest_count).astype(jnp.int32)
+    state = attend(
+        state, guest_flags, query_rows, guest_rank,
+        dealt, fetched, lambda h, kb: (0, kb, h), fetched, lambda h, kb: (1, kb, h),
+        gcap, heads, block_len,
+    )
+    attended = (state[2] / state[1]).astype(jnp.bfloat16)
     partial_value = jnp.dot(attended, w_out, preferred_element_type=jnp.float32).astype(
         jnp.bfloat16
     )

time: 249 us -> 226 us (0.908)
  Pallas kernels: 0 us -> 40.2 us
  matrix products: 42.1 us -> 14.1 us
  waiting for transfers between devices: 57.8 us -> 36.6 us
  other arithmetic: 35.7 us -> 24 us
  local copies, waits for them, and re-layouts: 32.7 us -> 21.9 us
  starting transfers between devices: 42.5 us -> 47.7 us
  blocking collectives: 35 us -> 40 us
    ppermute x1, waiting for transfers between devices: 41.3 us -> 0.01 us  [swapped(): return lax.ppermute(value, axis, pairs)]
    pallas_call x0 -> x4, Pallas kernels: none -> 40.2 us  [attend(): pl.pallas_call(flash_step, grid_spec=grid_spec, out_shape=[shape, shape,...]
    dot_general x12 -> x0, matrix products: 31.2 us -> none  [the longest x6 16.2 us: absorb(): jnp.einsum('qhd,khd->hqk', queries, key_rows, preferred_element_type=jnp....]
    all_to_all x1, waiting for transfers between devices: 0.01 us -> 20 us  [shards(): lax.all_to_all(arranged, 'grp', split_axis=0, concat_axis=1, tiled=True)[0]]
    slice x7 -> x0, local copies, waits for them, and re-layouts: 13 us -> none  [the longest x2 5.33 us: shards(): own_cache[0, 1]]
    reduce_sum x6 -> x0, other arithmetic: 10.3 us -> none  [absorb(): weight_sum = weight_sum * factor + jnp.sum(expanded, axis=-1)]
    unnamed x34 -> x24, local copies, waits for them, and re-layouts: 7.83 us -> 1.35 us
    all_to_all x1, blocking collectives: 35 us -> 40 us  [shards(): lax.all_to_all(partial_value.reshape(span_len, blocks, -1), 'tp', split_a...]
  transfers between devices with their start and end apart: 3 -> 3, of which waited for: 2 -> 2; matrix products, arithmetic and copies ran while one was open for 10% -> 11% of each run, Pallas kernels for 0% -> 14%
where the time goes in v2:
time: 226 us; the launch traced here: 225 us
  starting transfers between devices  47.7 us (21%)
  Pallas kernels  40.2 us (18%)
  blocking collectives  40 us (18%)
  waiting for transfers between devices  36.6 us (16%)
  other arithmetic  24 us (11%)
  local copies, waits for them, and re-layouts  21.9 us (10%)
  matrix products  14.1 us (6%)
    pallas_call x4, Pallas kernels, attend(): pl.pallas_call(flash_step, grid_spec=grid_spec, out_shape=[shape, shape,...  40.2 us
    all_to_all x1, blocking collectives, shards(): lax.all_to_all(partial_value.reshape(span_len, blocks, -1), 'tp', split_a...  40 us
    all_to_all x1, starting transfers between devices, shards(): lax.all_to_all(mixed_rows.reshape(groups, local_rows, -1), 'grp', split_a...  34.8 us
    all_to_all x1, waiting for transfers between devices, shards(): lax.all_to_all(arranged, 'grp', split_axis=0, concat_axis=1, tiled=True)[0]  20 us
    all_to_all x1, waiting for transfers between devices, shards(): lax.all_to_all(mixed_rows.reshape(groups, local_rows, -1), 'grp', split_a...  16.6 us
    all_to_all x1, starting transfers between devices, shards(): lax.all_to_all(arranged, 'grp', split_axis=0, concat_axis=1, tiled=True)[0]  11.2 us
  transfers between devices with their start and end apart: 3, of which 2 were waited for; matrix products, arithmetic and copies ran while one was open for 11% of the time, Pallas kernels for 14%

profile of v2, /device:TPU:1, one launch (start us, length us, event | category | flops | bytes accessed | tf_op | source)
XLA Modules:
  0.0 224.9 jit_solution(14085436311866175604)
XLA Ops:
  0.0 3.0 %convert_reduce_fusion = f32[32,32]{1,0:T(8,128)S(1)} fusion(bf16[32,32,2048]{2,1,0:T(8,128)(2,1)} %param.12), kind=kLoop, calls=%fused_computation.11 | loop fusion | flops 4193280 | bytes 4198400 | tf_op jit(solution)/shard_map/reduce_sum | solution.py:82
  4.9 2.5 %multiply_convert_fusion = bf16[32,32,2048]{2,1,0:T(8,128)(2,1)} fusion(bf16[32,32,2048]{2,1,0:T(8,128)(2,1)S(1)} %copy-done.4, f32[32,32]{1,0:T(8,128)S(1)} %add_rsqrt_fusion, f32[32,32]{1,0:T(8,128)S(1)} %broadcast_multiply_fusion), kind=kLoop, calls=%fused_computation.9 | loop fusion | flops 8388608 | bytes 8396800 | tf_op jit(solution)/shard_map/convert_element_type | solution.py:133
  9.9 1.4 copy.42
  12.0 3.9 %fusion.25 = f32[1024,2,128]{0,2,1:T(8,128)S(1)} fusion(bf16[1024,2048,1]{1,0,2:T(8,128)(2,1)} %bitcast.69, bf16[2,128,2048]{2,1,0:T(8,128)(2,1)} %bitcast.75), kind=kOutput, calls=%fused_computation.81 | convolution fusion | flops 1073741824 | bytes 6291456 | tf_op jit(solution)/shard_map/dot_general | solution.py:138
  22.1 1.6 copy.36
  23.7 2.1 gather_fusion.2
  25.8 1.4 broadcast_select_fusion
  27.1 11.2 %all-to-all-start = ((bf16[32,32,768]{2,1,0:T(8,128)(2,1)}), bf16[32,32,768]{2,1,0:T(8,128)(2,1)S(1)}, u32[]{:S(2)}, u32[]{:S(2)}) async-start(bf16[32,32,768]{2,1,0:T(8,128)(2,1)} %broadcast_select_fusion), calls=%async_computation | async-start | bytes 3145728 | tf_op jit(solution)/shard_map/all_to_all | solution.py:145
  38.3 1.7 collective-permute-start
  40.0 1.4 convert_reduce_fusion.1
  41.4 1.6 fusion.7
  43.4 2.1 fusion.11
  47.5 1.5 scatter_custom_fusion.1
  53.9 2.7 %convolution_convert_fusion.2.v_ref = bf16[256,256]{1,0:T(8,128)(2,1)} fusion(bf16[2048,256]{1,0:T(8,128)(2,1)} %param.15, bf16[1,256,2048]{2,1,0:T(8,128)(2,1)} %param.19, f32[256]{0:T(256)S(1)} %add_rsqrt_fusion.1, f32[256]{0:T(256)S(1)} %broadcast_multiply_fusion.1), kind=kOutput, calls=%fused_computation.27 | convolution fusion | flops 270598144 | bytes 2230272 | tf_op jit(solution)/shard_map/dot_general | solution.py:155
  56.6 20.0 %all-to-all-done = bf16[32,32,768]{2,1,0:T(8,128)(2,1)S(1)} async-done(((bf16[32,32,768]{2,1,0:T(8,128)(2,1)}), bf16[32,32,768]{2,1,0:T(8,128)(2,1)S(1)}, u32[]{:S(2)}, u32[]{:S(2)}) %all-to-all-start) | async-done | bytes 1572896 | tf_op jit(solution)/shard_map/all_to_all | solution.py:145
  81.9 11.4 %shard_map.118 = (f32[1024,256]{1,0:T(8,128)}, f32[1024,256]{1,0:T(8,128)}, f32[1024,256]{1,0:T(8,128)}) custom-call(s32[2]{0:T(128)} %broadcast_12_flags_ref.2.flags_ref, s32[1024,1]{1,0:T(8,128)} %iota.51.qrow_ref, s32[1,1024]{1,0:T(1,128)} %iota.52.rank_ref, ...), custom_call_target="tpu_custom_call", output_to_operand_aliasing={{0}: (6, {}), {1}: (7, {}), {2}: (8, {})} | custom-call | tf_op jit(solution)/shard_map/pallas_call | solution.py:61
  94.6 6.7 %shard_map.119 = (f32[1024,256]{1,0:T(8,128)}, f32[1024,256]{1,0:T(8,128)}, f32[1024,256]{1,0:T(8,128)}) custom-call(s32[1]{0:T(128)} %constant.94.clone.1.flags_ref, s32[1024,1]{1,0:T(8,128)} %iota.50.qrow_ref, s32[1,256]{1,0:T(1,128)} %broadcast_in_dim.93.rank_ref, ...), custom_call_target="tpu_custom_call", output_to_operand_aliasing={{0}: (6, {}), {1}: (7, {}), {2}: (8, {})} | custom-call | tf_op jit(solution)/shard_map/pallas_call | solution.py:61
  102.2 14.0 %shard_map.120 = (f32[1024,256]{1,0:T(8,128)}, f32[1024,256]{1,0:T(8,128)}, f32[1024,256]{1,0:T(8,128)}) custom-call(s32[4]{0:T(128)} %compare_convert_fusion.flags_ref, s32[1024,1]{1,0:T(8,128)} %iota.48.qrow_ref, s32[1,2048]{1,0:T(1,128)} %bitcast.79, bf16[1024,768]{1,0:T(8,128)(2,1)} %bitcast.62, ...), custom_call_target="tpu_custom_call", output_to_operand_aliasing={{0}: (6, {}), {1}: (7, {}), {2}: (8, {})} | custom-call | tf_op jit(solution)/shard_map/pallas_call | solution.py:61
  117.0 8.2 %shard_map.121 = (f32[1024,256]{1,0:T(8,128)}, f32[1024,256]{1,0:T(8,128)}, f32[1024,256]{1,0:T(8,128)}) custom-call(s32[4]{0:T(128)} %compare_convert_fusion.1.flags_ref, s32[1024,1]{1,0:T(8,128)} %iota.45.qrow_ref, s32[1,2048]{1,0:T(1,128)} %compare_select_fusion.rank_ref, ...), custom_call_target="tpu_custom_call", output_to_operand_aliasing={{0}: (6, {}), {1}: (7, {}), {2}: (8, {})} | custom-call | tf_op jit(solution)/shard_map/pallas_call | solution.py:61
  125.2 2.8 %convolution_convert_fusion = bf16[1024,2048]{1,0:T(8,128)(2,1)S(1)} fusion(bf16[256,2048]{1,0:T(8,128)(2,1)S(1)} %copy-done, f32[1024,256]{1,0:T(8,128)} %get-tuple-element.25, f32[1024,256]{1,0:T(8,128)} %get-tuple-element.26), kind=kOutput, calls=%fused_computation.13 | convolution fusion | flops 1076363264 | bytes 7340032 | tf_op jit(solution)/shard_map/dot_general | solution.py:198
  128.2 40.0 %all_to_all.19 = bf16[1024,8,256]{2,0,1:T(8,128)(2,1)} all-to-all(bf16[1024,8,256]{2,0,1:T(8,128)(2,1)S(1)} %bitcast.65), channel_id=1, replica_groups=mesh['grp'=32,'tp'=8] {'tp'}, dimensions={1} | all-to-all | bytes 8388608 | tf_op jit(solution)/shard_map/all_to_all | solution.py:202
  168.3 3.7 %reduce_sum.52 = bf16[1024,256]{1,0:T(8,128)(2,1)} reduce(bf16[1024,8,256]{2,0,1:T(8,128)(2,1)} %all_to_all.19, bf16[]{:T(256)} %constant.97.clone.1), dimensions={1}, to_apply=%region_6.7 | reduce | flops 1835008 | bytes 4718594 | tf_op jit(solution)/shard_map/reduce_sum | solution.py:205
  172.0 34.8 %all-to-all-start.2 = ((bf16[32,32,256]{2,1,0:T(8,128)(2,1)}), bf16[32,32,256]{2,1,0:T(8,128)(2,1)S(1)}, u32[]{:S(2)}, u32[]{:S(2)}) async-start(bf16[32,32,256]{2,1,0:T(8,128)(2,1)} %bitcast.23), calls=%async_computation.2 | async-start | bytes 1048576 | tf_op jit(solution)/shard_map/all_to_all | solution.py:206
  206.8 16.6 %all-to-all-done.2 = bf16[32,32,256]{2,1,0:T(8,128)(2,1)S(1)} async-done(((bf16[32,32,256]{2,1,0:T(8,128)(2,1)}), bf16[32,32,256]{2,1,0:T(8,128)(2,1)S(1)}, u32[]{:S(2)}, u32[]{:S(2)}) %all-to-all-start.2) | async-done | bytes 524320 | tf_op jit(solution)/shard_map/all_to_all | solution.py:206
  (81 shorter events, 28.3 us)
Async XLA Ops:
  0.0 125.1 %copy-start = (bf16[256,2048]{1,0:T(8,128)(2,1)S(1)}, bf16[256,2048]{1,0:T(8,128)(2,1)}, u32[]{:S(2)}) copy-start(bf16[256,2048]{1,0:T(8,128)(2,1)} %param.16) | copy-start | bytes 3145732
  0.0 3.5 %copy-start.4 = (bf16[32,32,2048]{2,1,0:T(8,128)(2,1)S(1)}, bf16[32,32,2048]{2,1,0:T(8,128)(2,1)}, u32[]{:S(2)}) copy-start(bf16[32,32,2048]{2,1,0:T(8,128)(2,1)} %param.12) | copy-start | bytes 12582916
  4.8 2.7 %copy-start.11 = (s32[32]{0:T(128)S(1)}, s32[32]{0:T(128)}, u32[]{:S(2)}) copy-start(s32[32]{0:T(128)} %param.20) | copy-start | bytes 388
  4.8 3.5 %copy-start.1 = (s32[32]{0:T(128)S(1)}, s32[32]{0:T(128)}, u32[]{:S(2)}) copy-start(s32[32]{0:T(128)} %param.21) | copy-start | bytes 388
  4.8 4.2 %copy-start.2 = (s32[32]{0:T(128)S(1)}, s32[32]{0:T(128)}, u32[]{:S(2)}) copy-start(s32[32]{0:T(128)} %param.22) | copy-start | bytes 388
  4.8 5.0 %copy-start.7 = (bf16[2048,256]{1,0:T(8,128)(2,1)S(1)}, bf16[2048,256]{1,0:T(8,128)(2,1)}, u32[]{:S(2)}) copy-start(bf16[2048,256]{1,0:T(8,128)(2,1)} %param.14) | copy-start | bytes 3145732
  7.4 3.9 %copy-start.8 = (bf16[2048,256]{1,0:T(8,128)(2,1)S(1)}, bf16[2048,256]{1,0:T(8,128)(2,1)}, u32[]{:S(2)}) copy-start(bf16[2048,256]{1,0:T(8,128)(2,1)} %param.13) | copy-start | bytes 3145732
  12.0 3.9 %copy-start.6 = (bf16[32,32,2048]{2,1,0:T(8,128)(2,1)S(1)}, bf16[32,32,2048]{2,1,0:T(8,128)(2,1)}, u32[]{:S(2)}) copy-start(bf16[32,32,2048]{2,1,0:T(8,128)(2,1)} %multiply_convert_fusion) | copy-start | bytes 12582916
  17.2 2.2 copy-start.5
  19.4 1.3 copy-start.10
  27.1 16.0 %copy-start.9 = (s32[1,256]{1,0:T(1,128)S(1)}, s32[1,256]{1,0:T(1,128)}, u32[]{:S(2)}) copy-start(s32[1,256]{1,0:T(1,128)} %param.23) | copy-start | bytes 3076
  27.1 49.5 %all-to-all-start = ((bf16[32,32,768]{2,1,0:T(8,128)(2,1)}), bf16[32,32,768]{2,1,0:T(8,128)(2,1)S(1)}, u32[]{:S(2)}, u32[]{:S(2)}) async-start(bf16[32,32,768]{2,1,0:T(8,128)(2,1)} %broadcast_select_fusion), calls=%async_computation | async-start | bytes 3145728 | tf_op jit(solution)/shard_map/all_to_all | solution.py:145
  38.3 77.9 %collective-permute-start = (bf16[2,2048,256]{2,1,0:T(8,128)(2,1)}, bf16[2,2048,256]{2,1,0:T(8,128)(2,1)}, u32[]{:S(2)}, u32[]{:S(2)}) collective-permute-start(bf16[2,2048,256]{2,1,0:T(8,128)(2,1)} %bitcast.82), channel_id=1, source_target_pairs={{0,128},{8,136},{16,144},{24,152},{32,160},{40,168},{48,176},{56,1... | collective-permute-start | bytes 6291464 | tf_op jit(solution)/shard_map/ppermute | solution.py:77
  76.6 5.2 %copy-start.3 = (bf16[32,32,768]{2,1,0:T(8,128)(2,1)}, bf16[32,32,768]{2,1,0:T(8,128)(2,1)S(1)}, u32[]{:S(2)}) copy-start(bf16[32,32,768]{2,1,0:T(8,128)(2,1)S(1)} %all-to-all-done) | copy-start | bytes 4718596
  172.0 51.4 %all-to-all-start.2 = ((bf16[32,32,256]{2,1,0:T(8,128)(2,1)}), bf16[32,32,256]{2,1,0:T(8,128)(2,1)S(1)}, u32[]{:S(2)}, u32[]{:S(2)}) async-start(bf16[32,32,256]{2,1,0:T(8,128)(2,1)} %bitcast.23), calls=%async_computation.2 | async-start | bytes 1048576 | tf_op jit(solution)/shard_map/all_to_all | solution.py:206

commit v3 on v2

--- a/solution.py
+++ b/solution.py
@@ -37,7 +37,7 @@
         m_out[...] = m_new
 
 
-def attend(state, flags, qrow, rank, q_src, k_src, k_map, v_src, v_map, key_count, heads, block_len):
+def attend(state, flags, qrow, rank, q_src, q_block, k_src, k_map, v_src, v_map, key_count, heads, block_len):
     query_count = qrow.shape[0]
     state_spec = pl.BlockSpec((query_count, HEAD_DIM), lambda h, kb, f: (0, h))
     k_block = (block_len, HEAD_DIM) if k_src.ndim == 2 else (None, block_len, HEAD_DIM)
@@ -48,7 +48,7 @@
         in_specs=[
             pl.BlockSpec((query_count, 1), lambda h, kb, f: (0, 0)),
             pl.BlockSpec((1, block_len), lambda h, kb, f: (0, kb)),
-            pl.BlockSpec((query_count, HEAD_DIM), lambda h, kb, f: (0, h)),
+            pl.BlockSpec((query_count, HEAD_DIM), lambda h, kb, f: (q_block, h)),
             pl.BlockSpec(k_block, lambda h, kb, f: k_map(h, kb)),
             pl.BlockSpec(v_block, lambda h, kb, f: v_map(h, kb)),
             state_spec,
@@ -156,56 +156,67 @@
     replaced = jnp.zeros((own_cache.shape[2],), jnp.bool_).at[rec_positions].set(True)
 
     heads = local_heads
-    query_rows = jnp.arange(span_len, dtype=jnp.int32)[:, None]
+    chunks = 2
+    piece = local_rows // chunks
+    chunk_len = span_len // chunks
+    order = dealt.reshape(groups, chunks, piece, -1).transpose(1, 0, 2, 3).reshape(span_len, -1)
+    row_of = (
+        jnp.arange(span_len, dtype=jnp.int32).reshape(groups, chunks, piece).transpose(1, 0, 2).reshape(-1)
+    )
+    rec_count = rec_keys.shape[0]
+    fresh = jnp.concatenate(
+        [order[:, local_width:], jnp.concatenate([rec_keys, rec_values], axis=1)], axis=0
+    )
+    fresh_rank = jnp.concatenate([row_of, jnp.full((rec_count,), -1, jnp.int32)])[None, :]
+    fresh_count = span_len + rec_count
     never = jnp.int32(1 << 30)
-    state = (
-        jnp.full((span_len, local_width), FLOOR, jnp.float32),
-        jnp.zeros((span_len, local_width), jnp.float32),
-        jnp.zeros((span_len, local_width), jnp.float32),
-    )
-    state = attend(
-        state, jnp.ones((2,), jnp.int32), query_rows,
-        jnp.arange(span_len, dtype=jnp.int32)[None, :],
-        dealt, dealt, lambda h, kb: (kb, heads + h), dealt, lambda h, kb: (kb, 2 * heads + h),
-        span_len, heads, span_len // 2,
-    )
-    rec_count = rec_keys.shape[0]
-    state = attend(
-        state, jnp.ones((1,), jnp.int32), query_rows, jnp.full((1, rec_count), -1, jnp.int32),
-        dealt, rec_keys, lambda h, kb: (kb, h), rec_values, lambda h, kb: (kb, h),
-        rec_count, heads, rec_count,
-    )
     cap = own_cache.shape[2]
     block_len = 512
     key_rows = jnp.arange(cap, dtype=jnp.int32)
     own_rank = jnp.where((key_rows < own_count) & ~replaced, -1, never)[None, :]
     own_flags = (jnp.arange(cap // block_len, dtype=jnp.int32) * block_len < own_count).astype(jnp.int32)
-    state = attend(
-        state, own_flags, query_rows, own_rank,
-        dealt, own_cache[0], lambda h, kb: (0, kb, h), own_cache[0], lambda h, kb: (1, kb, h),
-        cap, heads, block_len,
-    )
     gcap = fetched.shape[1]
     guest_rows = jnp.arange(gcap, dtype=jnp.int32)
     guest_rank = jnp.where(guest_rows < guest_count, -1, never)[None, :]
     guest_flags = (jnp.arange(gcap // block_len, dtype=jnp.int32) * block_len < guest_count).astype(jnp.int32)
-    state = attend(
-        state, guest_flags, query_rows, guest_rank,
-        dealt, fetched, lambda h, kb: (0, kb, h), fetched, lambda h, kb: (1, kb, h),
-        gcap, heads, block_len,
-    )
-    attended = (state[2] / state[1]).astype(jnp.bfloat16)
-    partial_value = jnp.dot(attended, w_out, preferred_element_type=jnp.float32).astype(
-        jnp.bfloat16
-    )
     blocks = lax.axis_size("tp")
-    exchanged = lax.all_to_all(
-        partial_value.reshape(span_len, blocks, -1), "tp", split_axis=1, concat_axis=1, tiled=True
-    )
-    mixed_rows = exchanged.astype(jnp.float32).sum(axis=1).astype(jnp.bfloat16)
-    returned_rows = lax.all_to_all(
-        mixed_rows.reshape(groups, local_rows, -1), "grp", split_axis=0, concat_axis=0, tiled=True
-    )
+    out_by_block = w_out.reshape(local_width, blocks, -1)
+
+    returned = []
+    for chunk in range(chunks):
+        query_rows = row_of[chunk * chunk_len : (chunk + 1) * chunk_len][:, None]
+        state = (
+            jnp.full((chunk_len, local_width), FLOOR, jnp.float32),
+            jnp.zeros((chunk_len, local_width), jnp.float32),
+            jnp.zeros((chunk_len, local_width), jnp.float32),
+        )
+        state = attend(
+            state, jnp.ones((2,), jnp.int32), query_rows, fresh_rank, order, chunk,
+            fresh, lambda h, kb: (kb, h), fresh, lambda h, kb: (kb, heads + h),
+            fresh_count, heads, fresh_count // 2,
+        )
+        state = attend(
+            state, own_flags, query_rows, own_rank, order, chunk,
+            own_cache[0], lambda h, kb: (0, kb, h), own_cache[0], lambda h, kb: (1, kb, h),
+            cap, heads, block_len,
+        )
+        state = attend(
+            state, guest_flags, query_rows, guest_rank, order, chunk,
+            fetched, lambda h, kb: (0, kb, h), fetched, lambda h, kb: (1, kb, h),
+            gcap, heads, block_len,
+        )
+        attended = (state[2] / state[1]).astype(jnp.bfloat16)
+        partial_value = jnp.einsum(
+            "qc,ctd->tqd", attended, out_by_block, preferred_element_type=jnp.float32
+        ).astype(jnp.bfloat16)
+        exchanged = lax.all_to_all(partial_value, "tp", split_axis=0, concat_axis=0, tiled=True)
+        mixed_rows = exchanged.astype(jnp.float32).sum(axis=0).astype(jnp.bfloat16)
+        returned.append(
+            lax.all_to_all(
+                mixed_rows.reshape(groups, piece, -1), "grp", split_axis=0, concat_axis=0, tiled=True
+            )
+        )
+    returned_rows = jnp.stack(returned, axis=1).reshape(groups, local_rows, -1)
     return jnp.take(returned_rows, server, axis=0)
 
 

time: 226 us -> 234 us (1.035)
  blocking collectives: 40 us -> 0 us
  waiting for transfers between devices: 36.6 us -> 61.1 us
  Pallas kernels: 40.2 us -> 49.8 us
  starting transfers between devices: 47.7 us -> 56.5 us
  matrix products: 14.1 us -> 16.9 us
    all_to_all x1 -> x0, blocking collectives: 40 us -> none  [shards(): lax.all_to_all(partial_value.reshape(span_len, blocks, -1), 'tp', split_a...]
    all_to_all x1 -> x4, waiting for transfers between devices: 16.6 us -> 37.9 us  [the longest x2 21.3 us: shards(): lax.all_to_all(mixed_rows.reshape(groups, piece, -1), 'grp', split_axis=0...]
    pallas_call x4 -> x6, Pallas kernels: 40.2 us -> 49.8 us  [attend(): pl.pallas_call(flash_step, grid_spec=grid_spec, out_shape=[shape, shape,...]
    all_to_all x1 -> x4, starting transfers between devices: 34.8 us -> 43.7 us  [the longest x2 30.7 us: shards(): lax.all_to_all(mixed_rows.reshape(groups, piece, -1), 'grp', split_axis=0...]
    dot_general x1 -> x2, matrix products: 2.8 us -> 6.84 us  [shards(): jnp.einsum('qc,ctd->tqd', attended, out_by_block, preferred_element_type=...]
    iota x5 -> x0, local copies, waits for them, and re-layouts: 3.98 us -> none  [the longest x4 3.38 us: shards(): query_rows = jnp.arange(span_len, dtype=jnp.int32)[:, None]]
    ppermute x1, waiting for transfers between devices: 0.01 us -> 3.13 us  [swapped(): return lax.ppermute(value, axis, pairs)]
    another operation x3 -> x7, local copies, waits for them, and re-layouts: 2.67 us -> 5.58 us
  transfers between devices with their start and end apart: 3 -> 6, of which waited for: 2 -> 5; matrix products, arithmetic and copies ran while one was open for 11% -> 14% of each run, Pallas kernels for 14% -> 18%
where the time goes in v3:
time: 234 us; the launch traced here: 233 us
  waiting for transfers between devices  61.1 us (26%)
  starting transfers between devices  56.5 us (24%)
  Pallas kernels  49.8 us (21%)
  other arithmetic  25.4 us (11%)
  local copies, waits for them, and re-layouts  23 us (10%)
  matrix products  16.9 us (7%)
    pallas_call x6, Pallas kernels, attend(): pl.pallas_call(flash_step, grid_spec=grid_spec, out_shape=[shape, shape,...  49.8 us
    all_to_all x2, starting transfers between devices, shards(): lax.all_to_all(mixed_rows.reshape(groups, piece, -1), 'grp', split_axis=0...  30.7 us
    all_to_all x2, waiting for transfers between devices, shards(): lax.all_to_all(mixed_rows.reshape(groups, piece, -1), 'grp', split_axis=0...  21.3 us
    all_to_all x1, waiting for transfers between devices, shards(): lax.all_to_all(arranged, 'grp', split_axis=0, concat_axis=1, tiled=True)[0]  20.1 us
    all_to_all x2, waiting for transfers between devices, shards(): lax.all_to_all(partial_value, 'tp', split_axis=0, concat_axis=0, tiled=True)  16.6 us
    all_to_all x2, starting transfers between devices, shards(): lax.all_to_all(partial_value, 'tp', split_axis=0, concat_axis=0, tiled=True)  13 us
    all_to_all x1, starting transfers between devices, shards(): lax.all_to_all(arranged, 'grp', split_axis=0, concat_axis=1, tiled=True)[0]  11.2 us
    dot_general x2, matrix products, shards(): jnp.einsum('qc,ctd->tqd', attended, out_by_block, preferred_element_type=...  6.84 us
  transfers between devices with their start and end apart: 6, of which 5 were waited for; matrix products, arithmetic and copies ran while one was open for 14% of the time, Pallas kernels for 18%

profile of v3, /device:TPU:1, one launch (start us, length us, event | category | flops | bytes accessed | tf_op | source)
XLA Modules:
  0.0 233.1 jit_solution(15143299128489465235)
XLA Ops:
  0.0 3.0 %convert_reduce_fusion = f32[32,32]{1,0:T(8,128)S(1)} fusion(bf16[32,32,2048]{2,1,0:T(8,128)(2,1)} %param.12), kind=kLoop, calls=%fused_computation.11 | loop fusion | flops 4193280 | bytes 4198400 | tf_op jit(solution)/shard_map/reduce_sum | solution.py:82
  4.9 2.6 %multiply_convert_fusion = bf16[32,32,2048]{2,1,0:T(8,128)(2,1)} fusion(bf16[32,32,2048]{2,1,0:T(8,128)(2,1)S(1)} %copy-done.4, f32[32,32]{1,0:T(8,128)S(1)} %add_rsqrt_fusion, f32[32,32]{1,0:T(8,128)S(1)} %broadcast_multiply_fusion), kind=kLoop, calls=%fused_computation.9 | loop fusion | flops 8388608 | bytes 8396800 | tf_op jit(solution)/shard_map/convert_element_type | solution.py:133
  12.8 3.6 %fusion.32 = f32[1024,2,128]{0,2,1:T(8,128)S(1)} fusion(bf16[1024,2048,1]{1,0,2:T(8,128)(2,1)} %bitcast.89, bf16[2,128,2048]{2,1,0:T(8,128)(2,1)S(1)} %bitcast.97), kind=kOutput, calls=%fused_computation.92 | convolution fusion | flops 1073741824 | bytes 6291456 | tf_op jit(solution)/shard_map/dot_general | solution.py:138
  25.4 2.1 gather_fusion.2
  28.8 11.2 %all-to-all-start = ((bf16[32,32,768]{2,1,0:T(8,128)(2,1)}), bf16[32,32,768]{2,1,0:T(8,128)(2,1)S(1)}, u32[]{:S(2)}, u32[]{:S(2)}) async-start(bf16[32,32,768]{2,1,0:T(8,128)(2,1)} %broadcast_select_fusion), calls=%async_computation | async-start | bytes 3145728 | tf_op jit(solution)/shard_map/all_to_all | solution.py:145
  45.1 2.1 fusion.11
  58.2 20.1 %all-to-all-done = bf16[32,32,768]{2,1,0:T(8,128)(2,1)S(1)} async-done(((bf16[32,32,768]{2,1,0:T(8,128)(2,1)}), bf16[32,32,768]{2,1,0:T(8,128)(2,1)S(1)}, u32[]{:S(2)}, u32[]{:S(2)}) %all-to-all-start) | async-done | bytes 1572896 | tf_op jit(solution)/shard_map/all_to_all | solution.py:145
  83.1 8.3 %shard_map.118 = (f32[512,256]{1,0:T(8,128)}, f32[512,256]{1,0:T(8,128)}, f32[512,256]{1,0:T(8,128)}) custom-call(s32[2]{0:T(128)} %broadcast_12_flags_ref.2.flags_ref, s32[512,1]{1,0:T(8,128)} %broadcast_in_dim.107.qrow_ref, s32[1,1280]{1,0:T(1,128)} %broadcast_in_dim.104.rank_ref, ...), custom_call_target="tpu_custom_call", output_to_operand_aliasing={{0}: (6, {}), {1}: (7, {}), {2}: (8, {})} | custom-call | tf_op jit(solution)/shard_map/pallas_call | solution.py:61
  91.4 9.6 %shard_map.119 = (f32[512,256]{1,0:T(8,128)}, f32[512,256]{1,0:T(8,128)}, f32[512,256]{1,0:T(8,128)}) custom-call(s32[4]{0:T(128)} %compare_convert_fusion.flags_ref, s32[512,1]{1,0:T(8,128)} %broadcast_in_dim.107.qrow_ref, s32[1,2048]{1,0:T(1,128)} %bitcast.102, ...), custom_call_target="tpu_custom_call", output_to_operand_aliasing={{0}: (6, {}), {1}: (7, {}), {2}: (8, {})} | custom-call | tf_op jit(solution)/shard_map/pallas_call | solution.py:61
  101.0 3.1 %collective-permute-done.k_ref.v_ref = bf16[2,2048,256]{2,1,0:T(8,128)(2,1)} collective-permute-done((bf16[2,2048,256]{2,1,0:T(8,128)(2,1)}, bf16[2,2048,256]{2,1,0:T(8,128)(2,1)}, u32[]{:S(2)}, u32[]{:S(2)}) %collective-permute-start) | collective-permute-done | bytes 2097184 | tf_op jit(solution)/shard_map/ppermute | solution.py:77
  104.2 7.0 %shard_map.120 = (f32[512,256]{1,0:T(8,128)}, f32[512,256]{1,0:T(8,128)}, f32[512,256]{1,0:T(8,128)}) custom-call(s32[4]{0:T(128)} %compare_convert_fusion.1.flags_ref, s32[512,1]{1,0:T(8,128)} %broadcast_in_dim.107.qrow_ref, s32[1,2048]{1,0:T(1,128)} %compare_select_fusion.rank_ref, ...), custom_call_target="tpu_custom_call", output_to_operand_aliasing={{0}: (6, {}), {1}: (7, {}), {2}: (8, {})} | custom-call | tf_op jit(solution)/shard_map/pallas_call | solution.py:61
  111.2 3.2 %convert_bitcast_fusion.2 = bf16[8,512,256]{2,1,0:T(8,128)(2,1)} fusion(bf16[32,8,8,256]{3,2,1,0:T(8,128)(2,1)S(1)} %bitcast.108, f32[512,256]{1,0:T(8,128)} %get-tuple-element.27, f32[512,256]{1,0:T(8,128)} %get-tuple-element.28), kind=kOutput, calls=%fused_computation.23 | convolution fusion | flops 538181632 | bytes 4194304 | tf_op jit(solution)/shard_map/qc,ctd->tqd/dot_general | solution.py:209
  114.5 6.4 %all-to-all-start.1 = ((bf16[8,512,256]{2,1,0:T(8,128)(2,1)}), bf16[8,512,256]{2,1,0:T(8,128)(2,1)S(1)}, u32[]{:S(2)}, u32[]{:S(2)}) async-start(bf16[8,512,256]{2,1,0:T(8,128)(2,1)} %convert_bitcast_fusion.2), calls=%async_computation.1 | async-start | bytes 4194304 | tf_op jit(solution)/shard_map/all_to_all | solution.py:212
  124.2 8.3 %shard_map.121 = (f32[512,256]{1,0:T(8,128)}, f32[512,256]{1,0:T(8,128)}, f32[512,256]{1,0:T(8,128)}) custom-call(s32[2]{0:T(128)} %broadcast_12_flags_ref.2.flags_ref, s32[512,1]{1,0:T(8,128)} %broadcast_in_dim.108.qrow_ref, s32[1,1280]{1,0:T(1,128)} %broadcast_in_dim.104.rank_ref, ...), custom_call_target="tpu_custom_call", output_to_operand_aliasing={{0}: (6, {}), {1}: (7, {}), {2}: (8, {})} | custom-call | tf_op jit(solution)/shard_map/pallas_call | solution.py:61
  132.6 9.6 %shard_map.122 = (f32[512,256]{1,0:T(8,128)}, f32[512,256]{1,0:T(8,128)}, f32[512,256]{1,0:T(8,128)}) custom-call(s32[4]{0:T(128)} %compare_convert_fusion.flags_ref, s32[512,1]{1,0:T(8,128)} %broadcast_in_dim.108.qrow_ref, s32[1,2048]{1,0:T(1,128)} %bitcast.103, ...), custom_call_target="tpu_custom_call", output_to_operand_aliasing={{0}: (6, {}), {1}: (7, {}), {2}: (8, {})} | custom-call | tf_op jit(solution)/shard_map/pallas_call | solution.py:61
  142.1 6.9 %shard_map.123 = (f32[512,256]{1,0:T(8,128)}, f32[512,256]{1,0:T(8,128)}, f32[512,256]{1,0:T(8,128)}) custom-call(s32[4]{0:T(128)} %compare_convert_fusion.1.flags_ref, s32[512,1]{1,0:T(8,128)} %broadcast_in_dim.108.qrow_ref, s32[1,2048]{1,0:T(1,128)} %compare_select_fusion.rank_ref, ...), custom_call_target="tpu_custom_call", output_to_operand_aliasing={{0}: (6, {}), {1}: (7, {}), {2}: (8, {})} | custom-call | tf_op jit(solution)/shard_map/pallas_call | solution.py:61
  149.1 3.6 %convert_bitcast_fusion.1 = bf16[8,512,256]{2,1,0:T(8,128)(2,1)} fusion(bf16[32,8,8,256]{3,2,1,0:T(8,128)(2,1)} %bitcast.107, f32[512,256]{1,0:T(8,128)} %get-tuple-element.35, f32[512,256]{1,0:T(8,128)} %get-tuple-element.36), kind=kOutput, calls=%fused_computation.22 | convolution fusion | flops 538181632 | bytes 4194304 | tf_op jit(solution)/shard_map/qc,ctd->tqd/dot_general | solution.py:209
  152.7 6.6 %all-to-all-start.3 = ((bf16[8,512,256]{2,1,0:T(8,128)(2,1)}), bf16[8,512,256]{2,1,0:T(8,128)(2,1)}, u32[]{:S(2)}, u32[]{:S(2)}) async-start(bf16[8,512,256]{2,1,0:T(8,128)(2,1)} %convert_bitcast_fusion.1), calls=%async_computation.3 | async-start | bytes 4194304 | tf_op jit(solution)/shard_map/all_to_all | solution.py:212
  160.3 16.6 %all-to-all-done.3 = bf16[8,512,256]{2,1,0:T(8,128)(2,1)} async-done(((bf16[8,512,256]{2,1,0:T(8,128)(2,1)}), bf16[8,512,256]{2,1,0:T(8,128)(2,1)}, u32[]{:S(2)}, u32[]{:S(2)}) %all-to-all-start.3) | async-done | bytes 2097184 | tf_op jit(solution)/shard_map/all_to_all | solution.py:212
  176.9 25.6 %all-to-all-start.2 = ((bf16[32,16,256]{2,1,0:T(8,128)(2,1)}), bf16[32,16,256]{2,1,0:T(8,128)(2,1)S(1)}, u32[]{:S(2)}, u32[]{:S(2)}) async-start(bf16[32,16,256]{2,1,0:T(8,128)(2,1)} %bitcast.27), calls=%async_computation.2 | async-start | bytes 524288 | tf_op jit(solution)/shard_map/all_to_all | solution.py:215
  202.6 2.7 %reduce_sum.65 = bf16[512,256]{1,0:T(8,128)(2,1)} reduce(bf16[8,512,256]{2,1,0:T(8,128)(2,1)} %all-to-all-done.3, bf16[]{:T(256)} %constant.98.clone.1), dimensions={0}, to_apply=%region_7.8 | reduce | flops 917504 | bytes 2359298 | tf_op jit(solution)/shard_map/reduce_sum | solution.py:213
  205.2 9.3 %all-to-all-done.2 = bf16[32,16,256]{2,1,0:T(8,128)(2,1)S(1)} async-done(((bf16[32,16,256]{2,1,0:T(8,128)(2,1)}), bf16[32,16,256]{2,1,0:T(8,128)(2,1)S(1)}, u32[]{:S(2)}, u32[]{:S(2)}) %all-to-all-start.2) | async-done | bytes 262176 | tf_op jit(solution)/shard_map/all_to_all | solution.py:215
  214.5 5.0 %all-to-all-start.4 = ((bf16[32,16,256]{2,1,0:T(8,128)(2,1)}), bf16[32,16,256]{2,1,0:T(8,128)(2,1)S(1)}, u32[]{:S(2)}, u32[]{:S(2)}) async-start(bf16[32,16,256]{2,1,0:T(8,128)(2,1)} %bitcast.31), calls=%async_computation.4 | async-start | bytes 524288 | tf_op jit(solution)/shard_map/all_to_all | solution.py:215
  219.5 12.0 %all-to-all-done.4 = bf16[32,16,256]{2,1,0:T(8,128)(2,1)S(1)} async-done(((bf16[32,16,256]{2,1,0:T(8,128)(2,1)}), bf16[32,16,256]{2,1,0:T(8,128)(2,1)S(1)}, u32[]{:S(2)}, u32[]{:S(2)}) %all-to-all-start.4) | async-done | bytes 262176 | tf_op jit(solution)/shard_map/all_to_all | solution.py:215
  (101 shorter events, 44.1 us)
Async XLA Ops:
  0.0 22.3 %copy-start = (bf16[2048,256]{1,0:T(8,128)(2,1)S(1)}, bf16[2048,256]{1,0:T(8,128)(2,1)}, u32[]{:S(2)}) copy-start(bf16[2048,256]{1,0:T(8,128)(2,1)} %param.15) | copy-start | bytes 3145732
  0.0 3.5 %copy-start.4 = (bf16[32,32,2048]{2,1,0:T(8,128)(2,1)S(1)}, bf16[32,32,2048]{2,1,0:T(8,128)(2,1)}, u32[]{:S(2)}) copy-start(bf16[32,32,2048]{2,1,0:T(8,128)(2,1)} %param.12) | copy-start | bytes 12582916
  4.8 2.8 %copy-start.13 = (s32[32]{0:T(128)S(1)}, s32[32]{0:T(128)}, u32[]{:S(2)}) copy-start(s32[32]{0:T(128)} %param.20) | copy-start | bytes 388
  4.8 3.5 %copy-start.1 = (s32[32]{0:T(128)S(1)}, s32[32]{0:T(128)}, u32[]{:S(2)}) copy-start(s32[32]{0:T(128)} %param.21) | copy-start | bytes 388
  4.8 4.2 %copy-start.2 = (s32[32]{0:T(128)S(1)}, s32[32]{0:T(128)}, u32[]{:S(2)}) copy-start(s32[32]{0:T(128)} %param.22) | copy-start | bytes 388
  4.8 5.1 %copy-start.7 = (bf16[2048,256]{1,0:T(8,128)(2,1)S(1)}, bf16[2048,256]{1,0:T(8,128)(2,1)}, u32[]{:S(2)}) copy-start(bf16[2048,256]{1,0:T(8,128)(2,1)} %param.14) | copy-start | bytes 3145732
  7.4 3.9 %copy-start.8 = (bf16[2048,256]{1,0:T(8,128)(2,1)S(1)}, bf16[2048,256]{1,0:T(8,128)(2,1)}, u32[]{:S(2)}) copy-start(bf16[2048,256]{1,0:T(8,128)(2,1)} %param.13) | copy-start | bytes 3145732
  11.3 1.4 copy-start.9
  12.8 3.6 %copy-start.6 = (bf16[32,32,2048]{2,1,0:T(8,128)(2,1)S(1)}, bf16[32,32,2048]{2,1,0:T(8,128)(2,1)}, u32[]{:S(2)}) copy-start(bf16[32,32,2048]{2,1,0:T(8,128)(2,1)} %multiply_convert_fusion) | copy-start | bytes 12582916
  12.8 3.7 %copy-start.10 = (bf16[256,2048]{1,0:T(8,128)(2,1)S(1)}, bf16[256,2048]{1,0:T(8,128)(2,1)}, u32[]{:S(2)}) copy-start(bf16[256,2048]{1,0:T(8,128)(2,1)} %copy.54) | copy-start | bytes 3145732
  18.8 2.2 copy-start.5
  28.8 14.3 %copy-start.11 = (s32[1,256]{1,0:T(1,128)S(1)}, s32[1,256]{1,0:T(1,128)}, u32[]{:S(2)}) copy-start(s32[1,256]{1,0:T(1,128)} %param.23) | copy-start | bytes 3076
  28.8 49.5 %all-to-all-start = ((bf16[32,32,768]{2,1,0:T(8,128)(2,1)}), bf16[32,32,768]{2,1,0:T(8,128)(2,1)S(1)}, u32[]{:S(2)}, u32[]{:S(2)}) async-start(bf16[32,32,768]{2,1,0:T(8,128)(2,1)} %broadcast_select_fusion), calls=%async_computation | async-start | bytes 3145728 | tf_op jit(solution)/shard_map/all_to_all | solution.py:145
  40.0 64.2 %collective-permute-start = (bf16[2,2048,256]{2,1,0:T(8,128)(2,1)}, bf16[2,2048,256]{2,1,0:T(8,128)(2,1)}, u32[]{:S(2)}, u32[]{:S(2)}) collective-permute-start(bf16[2,2048,256]{2,1,0:T(8,128)(2,1)} %bitcast.106), channel_id=1, source_target_pairs={{0,128},{8,136},{16,144},{24,152},{32,160},{40,168},{48,176},{56,1... | collective-permute-start | bytes 6291464 | tf_op jit(solution)/shard_map/ppermute | solution.py:77
  78.4 1.6 copy-start.3
  104.2 7.0 %copy-start.12 = (bf16[256,2048]{1,0:T(8,128)(2,1)S(1)}, bf16[256,2048]{1,0:T(8,128)(2,1)}, u32[]{:S(2)}) copy-start(bf16[256,2048]{1,0:T(8,128)(2,1)} %param.16) | copy-start | bytes 3145732
  114.5 38.2 %all-to-all-start.1 = ((bf16[8,512,256]{2,1,0:T(8,128)(2,1)}), bf16[8,512,256]{2,1,0:T(8,128)(2,1)S(1)}, u32[]{:S(2)}, u32[]{:S(2)}) async-start(bf16[8,512,256]{2,1,0:T(8,128)(2,1)} %convert_bitcast_fusion.2), calls=%async_computation.1 | async-start | bytes 4194304 | tf_op jit(solution)/shard_map/all_to_all | solution.py:212
  152.7 24.3 %all-to-all-start.3 = ((bf16[8,512,256]{2,1,0:T(8,128)(2,1)}), bf16[8,512,256]{2,1,0:T(8,128)(2,1)}, u32[]{:S(2)}, u32[]{:S(2)}) async-start(bf16[8,512,256]{2,1,0:T(8,128)(2,1)} %convert_bitcast_fusion.1), calls=%async_computation.3 | async-start | bytes 4194304 | tf_op jit(solution)/shard_map/all_to_all | solution.py:212
  176.9 37.6 %all-to-all-start.2 = ((bf16[32,16,256]{2,1,0:T(8,128)(2,1)}), bf16[32,16,256]{2,1,0:T(8,128)(2,1)S(1)}, u32[]{:S(2)}, u32[]{:S(2)}) async-start(bf16[32,16,256]{2,1,0:T(8,128)(2,1)} %bitcast.27), calls=%async_computation.2 | async-start | bytes 524288 | tf_op jit(solution)/shard_map/all_to_all | solution.py:215
  214.5 17.1 %all-to-all-start.4 = ((bf16[32,16,256]{2,1,0:T(8,128)(2,1)}), bf16[32,16,256]{2,1,0:T(8,128)(2,1)S(1)}, u32[]{:S(2)}, u32[]{:S(2)}) async-start(bf16[32,16,256]{2,1,0:T(8,128)(2,1)} %bitcast.31), calls=%async_computation.4 | async-start | bytes 524288 | tf_op jit(solution)/shard_map/all_to_all | solution.py:215

commit v4 on v3

--- a/solution.py
+++ b/solution.py
@@ -138,12 +138,15 @@
         jnp.dot(normed, w_key, preferred_element_type=jnp.float32), local_positions, HEAD_DIM
     ).astype(jnp.bfloat16)
     new_values = jnp.dot(normed, w_value, preferred_element_type=jnp.float32).astype(jnp.bfloat16)
-    projected = jnp.concatenate([queries, new_keys, new_values], axis=-1).reshape(
-        requests, local_rows, 3 * local_width
-    )
-    arranged = jnp.take(projected, deal_order, axis=0)
-    dealt = lax.all_to_all(arranged, "grp", split_axis=0, concat_axis=1, tiled=True)[0]
-    span_len = dealt.shape[0]
+    fresh_kv = jnp.concatenate([new_keys, new_values], axis=-1).reshape(requests, local_rows, -1)
+    dealt_q = lax.all_to_all(
+        jnp.take(queries.reshape(requests, local_rows, -1), deal_order, axis=0),
+        "grp", split_axis=0, concat_axis=1, tiled=True,
+    )[0]
+    dealt_kv = lax.all_to_all(
+        jnp.take(fresh_kv, deal_order, axis=0), "grp", split_axis=0, concat_axis=1, tiled=True
+    )[0]
+    span_len = dealt_q.shape[0]
 
     own_count = own_len[group_id]
     guest_count = guest_len[partner_id]
@@ -159,13 +162,16 @@
     chunks = 2
     piece = local_rows // chunks
     chunk_len = span_len // chunks
-    order = dealt.reshape(groups, chunks, piece, -1).transpose(1, 0, 2, 3).reshape(span_len, -1)
+    def chunk_major(rows):
+        return rows.reshape(groups, chunks, piece, -1).transpose(1, 0, 2, 3).reshape(span_len, -1)
+
+    order = chunk_major(dealt_q)
     row_of = (
         jnp.arange(span_len, dtype=jnp.int32).reshape(groups, chunks, piece).transpose(1, 0, 2).reshape(-1)
     )
     rec_count = rec_keys.shape[0]
     fresh = jnp.concatenate(
-        [order[:, local_width:], jnp.concatenate([rec_keys, rec_values], axis=1)], axis=0
+        [chunk_major(dealt_kv), jnp.concatenate([rec_keys, rec_values], axis=1)], axis=0
     )
     fresh_rank = jnp.concatenate([row_of, jnp.full((rec_count,), -1, jnp.int32)])[None, :]
     fresh_count = span_len + rec_count
@@ -191,11 +197,6 @@
             jnp.zeros((chunk_len, local_width), jnp.float32),
         )
         state = attend(
-            state, jnp.ones((2,), jnp.int32), query_rows, fresh_rank, order, chunk,
-            fresh, lambda h, kb: (kb, h), fresh, lambda h, kb: (kb, heads + h),
-            fresh_count, heads, fresh_count // 2,
-        )
-        state = attend(
             state, own_flags, query_rows, own_rank, order, chunk,
             own_cache[0], lambda h, kb: (0, kb, h), own_cache[0], lambda h, kb: (1, kb, h),
             cap, heads, block_len,
@@ -204,6 +205,11 @@
             state, guest_flags, query_rows, guest_rank, order, chunk,
             fetched, lambda h, kb: (0, kb, h), fetched, lambda h, kb: (1, kb, h),
             gcap, heads, block_len,
+        )
+        state = attend(
+            state, jnp.ones((2,), jnp.int32), query_rows, fresh_rank, order, chunk,
+            fresh, lambda h, kb: (kb, h), fresh, lambda h, kb: (kb, heads + h),
+            fresh_count, heads, fresh_count // 2,
         )
         attended = (state[2] / state[1]).astype(jnp.bfloat16)
         partial_value = jnp.einsum(

time: 234 us -> 240 us (1.026)
  waiting for transfers between devices: 61.1 us -> 49.3 us
  other arithmetic: 25.4 us -> 32 us
  starting transfers between devices: 56.5 us -> 62.2 us
  local copies, waits for them, and re-layouts: 23 us -> 27.7 us
    all_to_all x1 -> x2, waiting for transfers between devices: 20.1 us -> 11.5 us  [the longest x1 11.5 us: shards(): lax.all_to_all(jnp.take(fresh_kv, deal_order, axis=0), 'grp', split_axis=...]
    all_to_all x1 -> x2, starting transfers between devices: 11.2 us -> 18.6 us  [the longest x1 11.1 us: shards(): lax.all_to_all(jnp.take(queries.reshape(requests, local_rows, -1), deal_o...]
    ppermute x1, waiting for transfers between devices: 3.13 us -> 0.01 us  [swapped(): return lax.ppermute(value, axis, pairs)]
    transpose x1 -> x2, local copies, waits for them, and re-layouts: 0.11 us -> 3.17 us  [chunk_major(): rows.reshape(groups, chunks, piece, -1).transpose(1, 0, 2, 3)]
  transfers between devices with their start and end apart: 6 -> 7, of which waited for: 5 -> 4; matrix products, arithmetic and copies ran while one was open for 14% -> 20% of each run, Pallas kernels for 18% -> 14%
where the time goes in v4:
time: 240 us; the launch traced here: 238 us
  starting transfers between devices  62.2 us (26%)
  Pallas kernels  49.7 us (21%)
  waiting for transfers between devices  49.3 us (21%)
  other arithmetic  32 us (13%)
  local copies, waits for them, and re-layouts  27.7 us (12%)
  matrix products  16.8 us (7%)
    pallas_call x6, Pallas kernels, attend(): pl.pallas_call(flash_step, grid_spec=grid_spec, out_shape=[shape, shape,...  49.7 us
    all_to_all x2, starting transfers between devices, shards(): lax.all_to_all(mixed_rows.reshape(groups, piece, -1), 'grp', split_axis=0...  28.9 us
    all_to_all x2, waiting for transfers between devices, shards(): lax.all_to_all(mixed_rows.reshape(groups, piece, -1), 'grp', split_axis=0...  21.3 us
    all_to_all x2, waiting for transfers between devices, shards(): lax.all_to_all(partial_value, 'tp', split_axis=0, concat_axis=0, tiled=True)  16.6 us
    all_to_all x2, starting transfers between devices, shards(): lax.all_to_all(partial_value, 'tp', split_axis=0, concat_axis=0, tiled=True)  13 us
    all_to_all x1, waiting for transfers between devices, shards(): lax.all_to_all(jnp.take(fresh_kv, deal_order, axis=0), 'grp', split_axis=...  11.5 us
    all_to_all x1, starting transfers between devices, shards(): lax.all_to_all(jnp.take(queries.reshape(requests, local_rows, -1), deal_o...  11.1 us
    all_to_all x1, starting transfers between devices, shards(): lax.all_to_all(jnp.take(fresh_kv, deal_order, axis=0), 'grp', split_axis=...  7.53 us
  transfers between devices with their start and end apart: 7, of which 4 were waited for; matrix products, arithmetic and copies ran while one was open for 20% of the time, Pallas kernels for 14%

profile of v4, /device:TPU:1, one launch (start us, length us, event | category | flops | bytes accessed | tf_op | source)
XLA Modules:
  0.0 238.1 jit_solution(17533826789236896135)
XLA Ops:
  1.8 2.8 %convert_reduce_fusion = f32[32,32]{1,0:T(8,128)S(1)} fusion(bf16[32,32,2048]{2,1,0:T(8,128)(2,1)} %param.14), kind=kLoop, calls=%fused_computation.12 | loop fusion | flops 4193280 | bytes 4198400 | tf_op jit(solution)/shard_map/reduce_sum | solution.py:82
  5.9 2.6 %multiply_convert_fusion = bf16[32,32,2048]{2,1,0:T(8,128)(2,1)} fusion(bf16[32,32,2048]{2,1,0:T(8,128)(2,1)S(1)} %copy-done.3, f32[32,32]{1,0:T(8,128)S(1)} %add_rsqrt_fusion, f32[32,32]{1,0:T(8,128)S(1)} %broadcast_multiply_fusion), kind=kLoop, calls=%fused_computation.10 | loop fusion | flops 8388608 | bytes 8396800 | tf_op jit(solution)/shard_map/convert_element_type | solution.py:133
  13.7 3.6 %fusion.32 = f32[1024,2,128]{0,2,1:T(8,128)S(1)} fusion(bf16[1024,2048,1]{1,0,2:T(8,128)(2,1)} %bitcast.90, bf16[2,128,2048]{2,1,0:T(8,128)(2,1)S(1)} %bitcast.98), kind=kOutput, calls=%fused_computation.94 | convolution fusion | flops 1073741824 | bytes 6291456 | tf_op jit(solution)/shard_map/dot_general | solution.py:138
  23.1 11.1 %all-to-all-start = ((bf16[32,32,256]{2,1,0:T(8,128)(2,1)}), bf16[32,32,256]{2,1,0:T(8,128)(2,1)}, u32[]{:S(2)}, u32[]{:S(2)}) async-start(bf16[32,32,256]{2,1,0:T(8,128)(2,1)} %broadcast_select_fusion.2), calls=%async_computation | async-start | bytes 1048576 | tf_op jit(solution)/shard_map/all_to_all | solution.py:142
  37.5 2.8 %fusion.1 = bf16[1024,2048]{1,0:T(8,128)(2,1)S(1)} fusion(bf16[32,32,2048]{2,1,0:T(8,128)(2,1)} %param.14, f32[1024]{0:T(1024)S(1)} %rsqrt.21, f32[1024]{0:T(1024)S(1)} %div.33), kind=kLoop, calls=%fused_computation.9 | loop fusion | flops 8388608 | bytes 8396800 | tf_op jit(solution)/shard_map/convert_element_type | solution.py:133
  45.1 2.8 %gather_fusion.2 = bf16[32,32,512]{2,1,0:T(8,128)(2,1)} fusion(bf16[32,32,512]{2,1,0:T(8,128)(2,1)} %bitcast.89, s32[1024]{0:T(1024)S(1)} %pad_clamp_fusion), kind=kCustom, calls=%fused_computation.4 | custom fusion | bytes 2097280 | tf_op jit(solution)/shard_map/jit(_take)/gather | solution.py:147
  52.3 7.5 %all-to-all-start.1 = ((bf16[32,32,512]{2,1,0:T(8,128)(2,1)}), bf16[32,32,512]{2,1,0:T(8,128)(2,1)}, u32[]{:S(2)}, u32[]{:S(2)}) async-start(bf16[32,32,512]{2,1,0:T(8,128)(2,1)} %broadcast_select_fusion), calls=%async_computation.1 | async-start | bytes 2097152 | tf_op jit(solution)/shard_map/all_to_all | solution.py:146
  77.2 9.6 %shard_map.121 = (f32[512,256]{1,0:T(8,128)}, f32[512,256]{1,0:T(8,128)}, f32[512,256]{1,0:T(8,128)}) custom-call(s32[4]{0:T(128)} %compare_convert_fusion.flags_ref, s32[512,1]{1,0:T(8,128)} %broadcast_in_dim.112.qrow_ref, s32[1,2048]{1,0:T(1,128)} %bitcast.103, ...), custom_call_target="tpu_custom_call", output_to_operand_aliasing={{0}: (6, {}), {1}: (7, {}), {2}: (8, {})} | custom-call | tf_op jit(solution)/shard_map/pallas_call | solution.py:61
  86.8 11.5 %all-to-all-done.1 = bf16[32,32,512]{2,1,0:T(8,128)(2,1)} async-done(((bf16[32,32,512]{2,1,0:T(8,128)(2,1)}), bf16[32,32,512]{2,1,0:T(8,128)(2,1)}, u32[]{:S(2)}, u32[]{:S(2)}) %all-to-all-start.1) | async-done | bytes 1048608 | tf_op jit(solution)/shard_map/all_to_all | solution.py:146
  102.1 6.9 %shard_map.122 = (f32[512,256]{1,0:T(8,128)}, f32[512,256]{1,0:T(8,128)}, f32[512,256]{1,0:T(8,128)}) custom-call(s32[4]{0:T(128)} %compare_convert_fusion.1.flags_ref, s32[512,1]{1,0:T(8,128)} %broadcast_in_dim.112.qrow_ref, s32[1,2048]{1,0:T(1,128)} %compare_select_fusion.rank_ref, ...), custom_call_target="tpu_custom_call", output_to_operand_aliasing={{0}: (6, {}), {1}: (7, {}), {2}: (8, {})} | custom-call | tf_op jit(solution)/shard_map/pallas_call | solution.py:61
  109.6 8.4 %shard_map.123 = (f32[512,256]{1,0:T(8,128)}, f32[512,256]{1,0:T(8,128)}, f32[512,256]{1,0:T(8,128)}) custom-call(s32[2]{0:T(128)} %broadcast_12_flags_ref.2.flags_ref, s32[512,1]{1,0:T(8,128)} %broadcast_in_dim.112.qrow_ref, s32[1,1280]{1,0:T(1,128)} %broadcast_in_dim.90.rank_ref, ...), custom_call_target="tpu_custom_call", output_to_operand_aliasing={{0}: (6, {}), {1}: (7, {}), {2}: (8, {})} | custom-call | tf_op jit(solution)/shard_map/pallas_call | solution.py:61
  118.0 3.3 %convert_bitcast_fusion.1 = bf16[8,512,256]{2,1,0:T(8,128)(2,1)} fusion(bf16[32,8,8,256]{3,2,1,0:T(8,128)(2,1)S(1)} %bitcast.109, f32[512,256]{1,0:T(8,128)} %get-tuple-element.36, f32[512,256]{1,0:T(8,128)} %get-tuple-element.37), kind=kOutput, calls=%fused_computation.23 | convolution fusion | flops 538181632 | bytes 4194304 | tf_op jit(solution)/shard_map/qc,ctd->tqd/dot_general | solution.py:215
  121.2 6.4 %all-to-all-start.4 = ((bf16[8,512,256]{2,1,0:T(8,128)(2,1)}), bf16[8,512,256]{2,1,0:T(8,128)(2,1)S(1)}, u32[]{:S(2)}, u32[]{:S(2)}) async-start(bf16[8,512,256]{2,1,0:T(8,128)(2,1)} %convert_bitcast_fusion.1), calls=%async_computation.4 | async-start | bytes 4194304 | tf_op jit(solution)/shard_map/all_to_all | solution.py:218
  131.0 9.6 %shard_map.118 = (f32[512,256]{1,0:T(8,128)}, f32[512,256]{1,0:T(8,128)}, f32[512,256]{1,0:T(8,128)}) custom-call(s32[4]{0:T(128)} %compare_convert_fusion.flags_ref, s32[512,1]{1,0:T(8,128)} %broadcast_in_dim.111.qrow_ref, s32[1,2048]{1,0:T(1,128)} %bitcast.104, ...), custom_call_target="tpu_custom_call", output_to_operand_aliasing={{0}: (6, {}), {1}: (7, {}), {2}: (8, {})} | custom-call | tf_op jit(solution)/shard_map/pallas_call | solution.py:61
  140.5 6.9 %shard_map.119 = (f32[512,256]{1,0:T(8,128)}, f32[512,256]{1,0:T(8,128)}, f32[512,256]{1,0:T(8,128)}) custom-call(s32[4]{0:T(128)} %compare_convert_fusion.1.flags_ref, s32[512,1]{1,0:T(8,128)} %broadcast_in_dim.111.qrow_ref, s32[1,2048]{1,0:T(1,128)} %compare_select_fusion.rank_ref, ...), custom_call_target="tpu_custom_call", output_to_operand_aliasing={{0}: (6, {}), {1}: (7, {}), {2}: (8, {})} | custom-call | tf_op jit(solution)/shard_map/pallas_call | solution.py:61
  147.5 8.3 %shard_map.120 = (f32[512,256]{1,0:T(8,128)}, f32[512,256]{1,0:T(8,128)}, f32[512,256]{1,0:T(8,128)}) custom-call(s32[2]{0:T(128)} %broadcast_12_flags_ref.2.flags_ref, s32[512,1]{1,0:T(8,128)} %broadcast_in_dim.111.qrow_ref, s32[1,1280]{1,0:T(1,128)} %broadcast_in_dim.90.rank_ref, ...), custom_call_target="tpu_custom_call", output_to_operand_aliasing={{0}: (6, {}), {1}: (7, {}), {2}: (8, {})} | custom-call | tf_op jit(solution)/shard_map/pallas_call | solution.py:61
  155.8 3.6 %convert_bitcast_fusion.2 = bf16[8,512,256]{2,1,0:T(8,128)(2,1)} fusion(bf16[32,8,8,256]{3,2,1,0:T(8,128)(2,1)} %bitcast.108, f32[512,256]{1,0:T(8,128)} %get-tuple-element.28, f32[512,256]{1,0:T(8,128)} %get-tuple-element.29), kind=kOutput, calls=%fused_computation.24 | convolution fusion | flops 538181632 | bytes 4194304 | tf_op jit(solution)/shard_map/qc,ctd->tqd/dot_general | solution.py:215
  159.4 6.6 %all-to-all-start.2 = ((bf16[8,512,256]{2,1,0:T(8,128)(2,1)}), bf16[8,512,256]{2,1,0:T(8,128)(2,1)}, u32[]{:S(2)}, u32[]{:S(2)}) async-start(bf16[8,512,256]{2,1,0:T(8,128)(2,1)} %convert_bitcast_fusion.2), calls=%async_computation.2 | async-start | bytes 4194304 | tf_op jit(solution)/shard_map/all_to_all | solution.py:218
  167.1 16.6 %all-to-all-done.2 = bf16[8,512,256]{2,1,0:T(8,128)(2,1)} async-done(((bf16[8,512,256]{2,1,0:T(8,128)(2,1)}), bf16[8,512,256]{2,1,0:T(8,128)(2,1)}, u32[]{:S(2)}, u32[]{:S(2)}) %all-to-all-start.2) | async-done | bytes 2097184 | tf_op jit(solution)/shard_map/all_to_all | solution.py:218
  183.7 23.9 %all-to-all-start.5 = ((bf16[32,16,256]{2,1,0:T(8,128)(2,1)}), bf16[32,16,256]{2,1,0:T(8,128)(2,1)S(1)}, u32[]{:S(2)}, u32[]{:S(2)}) async-start(bf16[32,16,256]{2,1,0:T(8,128)(2,1)} %bitcast.33), calls=%async_computation.5 | async-start | bytes 524288 | tf_op jit(solution)/shard_map/all_to_all | solution.py:221
  207.6 2.7 %reduce_sum.64 = bf16[512,256]{1,0:T(8,128)(2,1)} reduce(bf16[8,512,256]{2,1,0:T(8,128)(2,1)} %all-to-all-done.2, bf16[]{:T(256)} %constant.96.clone.1), dimensions={0}, to_apply=%region_6.8 | reduce | flops 917504 | bytes 2359298 | tf_op jit(solution)/shard_map/reduce_sum | solution.py:219
  210.3 9.3 %all-to-all-done.5 = bf16[32,16,256]{2,1,0:T(8,128)(2,1)S(1)} async-done(((bf16[32,16,256]{2,1,0:T(8,128)(2,1)}), bf16[32,16,256]{2,1,0:T(8,128)(2,1)S(1)}, u32[]{:S(2)}, u32[]{:S(2)}) %all-to-all-start.5) | async-done | bytes 262176 | tf_op jit(solution)/shard_map/all_to_all | solution.py:221
  219.5 5.0 %all-to-all-start.3 = ((bf16[32,16,256]{2,1,0:T(8,128)(2,1)}), bf16[32,16,256]{2,1,0:T(8,128)(2,1)S(1)}, u32[]{:S(2)}, u32[]{:S(2)}) async-start(bf16[32,16,256]{2,1,0:T(8,128)(2,1)} %bitcast.29), calls=%async_computation.3 | async-start | bytes 524288 | tf_op jit(solution)/shard_map/all_to_all | solution.py:221
  224.6 12.0 %all-to-all-done.3 = bf16[32,16,256]{2,1,0:T(8,128)(2,1)S(1)} async-done(((bf16[32,16,256]{2,1,0:T(8,128)(2,1)}), bf16[32,16,256]{2,1,0:T(8,128)(2,1)S(1)}, u32[]{:S(2)}, u32[]{:S(2)}) %all-to-all-start.3) | async-done | bytes 262176 | tf_op jit(solution)/shard_map/all_to_all | solution.py:221
  (105 shorter events, 53.9 us)
Async XLA Ops:
  0.0 40.3 %copy-start = (bf16[2048,256]{1,0:T(8,128)(2,1)S(1)}, bf16[2048,256]{1,0:T(8,128)(2,1)}, u32[]{:S(2)}) copy-start(bf16[2048,256]{1,0:T(8,128)(2,1)} %param.17) | copy-start | bytes 3145732
  0.0 4.6 %copy-start.3 = (bf16[32,32,2048]{2,1,0:T(8,128)(2,1)S(1)}, bf16[32,32,2048]{2,1,0:T(8,128)(2,1)}, u32[]{:S(2)}) copy-start(bf16[32,32,2048]{2,1,0:T(8,128)(2,1)} %param.14) | copy-start | bytes 12582916
  5.9 2.6 %copy-start.7 = (bf16[2048,256]{1,0:T(8,128)(2,1)S(1)}, bf16[2048,256]{1,0:T(8,128)(2,1)}, u32[]{:S(2)}) copy-start(bf16[2048,256]{1,0:T(8,128)(2,1)} %param.16) | copy-start | bytes 3145732
  5.9 4.8 %copy-start.2 = (s32[32]{0:T(128)S(1)}, s32[32]{0:T(128)}, u32[]{:S(2)}) copy-start(s32[32]{0:T(128)} %param.23) | copy-start | bytes 388
  8.4 2.9 %copy-start.1 = (s32[32]{0:T(128)S(1)}, s32[32]{0:T(128)}, u32[]{:S(2)}) copy-start(s32[32]{0:T(128)} %param.24) | copy-start | bytes 388
  8.4 3.8 %copy-start.8 = (bf16[2048,256]{1,0:T(8,128)(2,1)S(1)}, bf16[2048,256]{1,0:T(8,128)(2,1)}, u32[]{:S(2)}) copy-start(bf16[2048,256]{1,0:T(8,128)(2,1)} %param.15) | copy-start | bytes 3145732
  9.9 3.8 %copy-start.9 = (bf16[256,2048]{1,0:T(8,128)(2,1)S(1)}, bf16[256,2048]{1,0:T(8,128)(2,1)}, u32[]{:S(2)}) copy-start(bf16[256,2048]{1,0:T(8,128)(2,1)} %copy.58) | copy-start | bytes 3145732
  13.7 3.6 %copy-start.5 = (bf16[32,32,2048]{2,1,0:T(8,128)(2,1)S(1)}, bf16[32,32,2048]{2,1,0:T(8,128)(2,1)}, u32[]{:S(2)}) copy-start(bf16[32,32,2048]{2,1,0:T(8,128)(2,1)} %multiply_convert_fusion) | copy-start | bytes 12582916
  13.7 3.7 %copy-start.10 = (bf16[256,2048]{1,0:T(8,128)(2,1)S(1)}, bf16[256,2048]{1,0:T(8,128)(2,1)}, u32[]{:S(2)}) copy-start(bf16[256,2048]{1,0:T(8,128)(2,1)} %copy.56) | copy-start | bytes 3145732
  21.2 16.2 %copy-start.11 = (s32[1,256]{1,0:T(1,128)S(1)}, s32[1,256]{1,0:T(1,128)}, u32[]{:S(2)}) copy-start(s32[1,256]{1,0:T(1,128)} %param.25) | copy-start | bytes 3076
  23.1 29.2 %all-to-all-start = ((bf16[32,32,256]{2,1,0:T(8,128)(2,1)}), bf16[32,32,256]{2,1,0:T(8,128)(2,1)}, u32[]{:S(2)}, u32[]{:S(2)}) async-start(bf16[32,32,256]{2,1,0:T(8,128)(2,1)} %broadcast_select_fusion.2), calls=%async_computation | async-start | bytes 1048576 | tf_op jit(solution)/shard_map/all_to_all | solution.py:142
  34.2 66.6 %collective-permute-start = (bf16[2,2048,256]{2,1,0:T(8,128)(2,1)}, bf16[2,2048,256]{2,1,0:T(8,128)(2,1)S(1)}, u32[]{:S(2)}, u32[]{:S(2)}) collective-permute-start(bf16[2,2048,256]{2,1,0:T(8,128)(2,1)} %bitcast.107), channel_id=1, source_target_pairs={{0,128},{8,136},{16,144},{24,152},{32,160},{40,168},{48,176},{56,1... | collective-permute-start | bytes 6291464 | tf_op jit(solution)/shard_map/ppermute | solution.py:77
  40.3 1.3 copy-start.6
  52.3 46.0 %all-to-all-start.1 = ((bf16[32,32,512]{2,1,0:T(8,128)(2,1)}), bf16[32,32,512]{2,1,0:T(8,128)(2,1)}, u32[]{:S(2)}, u32[]{:S(2)}) async-start(bf16[32,32,512]{2,1,0:T(8,128)(2,1)} %broadcast_select_fusion), calls=%async_computation.1 | async-start | bytes 2097152 | tf_op jit(solution)/shard_map/all_to_all | solution.py:146
  100.8 1.3 copy-start.4
  109.0 8.9 %copy-start.12 = (bf16[256,2048]{1,0:T(8,128)(2,1)S(1)}, bf16[256,2048]{1,0:T(8,128)(2,1)}, u32[]{:S(2)}) copy-start(bf16[256,2048]{1,0:T(8,128)(2,1)} %param.18) | copy-start | bytes 3145732
  121.2 38.2 %all-to-all-start.4 = ((bf16[8,512,256]{2,1,0:T(8,128)(2,1)}), bf16[8,512,256]{2,1,0:T(8,128)(2,1)S(1)}, u32[]{:S(2)}, u32[]{:S(2)}) async-start(bf16[8,512,256]{2,1,0:T(8,128)(2,1)} %convert_bitcast_fusion.1), calls=%async_computation.4 | async-start | bytes 4194304 | tf_op jit(solution)/shard_map/all_to_all | solution.py:218
  159.4 24.3 %all-to-all-start.2 = ((bf16[8,512,256]{2,1,0:T(8,128)(2,1)}), bf16[8,512,256]{2,1,0:T(8,128)(2,1)}, u32[]{:S(2)}, u32[]{:S(2)}) async-start(bf16[8,512,256]{2,1,0:T(8,128)(2,1)} %convert_bitcast_fusion.2), calls=%async_computation.2 | async-start | bytes 4194304 | tf_op jit(solution)/shard_map/all_to_all | solution.py:218
  183.7 35.9 %all-to-all-start.5 = ((bf16[32,16,256]{2,1,0:T(8,128)(2,1)}), bf16[32,16,256]{2,1,0:T(8,128)(2,1)S(1)}, u32[]{:S(2)}, u32[]{:S(2)}) async-start(bf16[32,16,256]{2,1,0:T(8,128)(2,1)} %bitcast.33), calls=%async_computation.5 | async-start | bytes 524288 | tf_op jit(solution)/shard_map/all_to_all | solution.py:221
  219.5 17.1 %all-to-all-start.3 = ((bf16[32,16,256]{2,1,0:T(8,128)(2,1)}), bf16[32,16,256]{2,1,0:T(8,128)(2,1)S(1)}, u32[]{:S(2)}, u32[]{:S(2)}) async-start(bf16[32,16,256]{2,1,0:T(8,128)(2,1)} %bitcast.29), calls=%async_computation.3 | async-start | bytes 524288 | tf_op jit(solution)/shard_map/all_to_all | solution.py:221

commit v5 on v2

--- a/solution.py
+++ b/solution.py
@@ -1,3 +1,5 @@
+import functools
+
 import jax
 import jax.numpy as jnp
 from jax import lax
@@ -65,6 +67,61 @@
         input_output_aliases={6: 0, 7: 1, 8: 2},
         compiler_params=pltpu.CompilerParams(dimension_semantics=("arbitrary", "arbitrary")),
     )(flags, qrow, rank, q_src, k_src, v_src, *state)
+
+
+def exchange_step(axis, count, x_ref, y_ref, local_sem, send_sem, recv_sem):
+    me = lax.axis_index(axis)
+    barrier = pltpu.get_barrier_semaphore()
+    for step in range(1, count):
+        pl.semaphore_signal(
+            barrier, inc=1, device_id={axis: lax.rem(me + step, count)},
+            device_id_type=pl.DeviceIdType.MESH,
+        )
+    pl.semaphore_wait(barrier, count - 1)
+    own = pltpu.make_async_copy(x_ref.at[me], y_ref.at[me], local_sem)
+    own.start()
+    sends = []
+    for step in range(1, count):
+        target = lax.rem(me + step, count)
+        copy = pltpu.make_async_remote_copy(
+            src_ref=x_ref.at[target],
+            dst_ref=y_ref.at[me],
+            send_sem=send_sem.at[step],
+            recv_sem=recv_sem.at[me],
+            device_id={axis: target},
+            device_id_type=pl.DeviceIdType.MESH,
+        )
+        copy.start()
+        sends.append(copy)
+    for copy in sends:
+        copy.wait_send()
+    for step in range(1, count):
+        source = lax.rem(me + count - step, count)
+        pltpu.make_async_remote_copy(
+            src_ref=x_ref.at[source],
+            dst_ref=y_ref.at[source],
+            send_sem=send_sem.at[step],
+            recv_sem=recv_sem.at[source],
+            device_id={axis: source},
+            device_id_type=pl.DeviceIdType.MESH,
+        ).wait_recv()
+    own.wait()
+
+
+def exchange(blocks, axis, collective):
+    count = blocks.shape[0]
+    return pl.pallas_call(
+        functools.partial(exchange_step, axis, count),
+        out_shape=jax.ShapeDtypeStruct(blocks.shape, blocks.dtype),
+        in_specs=[pl.BlockSpec(memory_space=pl.ANY)],
+        out_specs=pl.BlockSpec(memory_space=pl.ANY),
+        scratch_shapes=[
+            pltpu.SemaphoreType.DMA(()),
+            pltpu.SemaphoreType.DMA((count,)),
+            pltpu.SemaphoreType.DMA((count,)),
+        ],
+        compiler_params=pltpu.CompilerParams(collective_id=collective, has_side_effects=True),
+    )(blocks)
 
 
 rope_base = 10000.0
@@ -195,17 +252,13 @@
         gcap, heads, block_len,
     )
     attended = (state[2] / state[1]).astype(jnp.bfloat16)
-    partial_value = jnp.dot(attended, w_out, preferred_element_type=jnp.float32).astype(
-        jnp.bfloat16
-    )
     blocks = lax.axis_size("tp")
-    exchanged = lax.all_to_all(
-        partial_value.reshape(span_len, blocks, -1), "tp", split_axis=1, concat_axis=1, tiled=True
-    )
-    mixed_rows = exchanged.astype(jnp.float32).sum(axis=1).astype(jnp.bfloat16)
-    returned_rows = lax.all_to_all(
-        mixed_rows.reshape(groups, local_rows, -1), "grp", split_axis=0, concat_axis=0, tiled=True
-    )
+    partial_value = jnp.einsum(
+        "qc,ctd->tqd", attended, w_out.reshape(local_width, blocks, -1), preferred_element_type=jnp.float32
+    ).astype(jnp.bfloat16)
+    exchanged = exchange(partial_value, "tp", 0)
+    mixed_rows = exchanged.astype(jnp.float32).sum(axis=0).astype(jnp.bfloat16)
+    returned_rows = exchange(mixed_rows.reshape(groups, local_rows, -1), "grp", 1)
     return jnp.take(returned_rows, server, axis=0)
 
 

time: 226 us -> 225 us (level)
  Pallas kernels: 40.2 us -> 128 us
  blocking collectives: 40 us -> 0 us
  starting transfers between devices: 47.7 us -> 12.7 us
  waiting for transfers between devices: 36.6 us -> 20.3 us
    pallas_call x0 -> x2, Pallas kernels: none -> 82.8 us  [exchange(): pl.pallas_call(functools.partial(exchange_step, axis, count), out_shape=j...]
    all_to_all x1 -> x0, blocking collectives: 40 us -> none  [shards(): lax.all_to_all(partial_value.reshape(span_len, blocks, -1), 'tp', split_a...]
    all_to_all x1 -> x0, starting transfers between devices: 34.8 us -> none  [shards(): lax.all_to_all(mixed_rows.reshape(groups, local_rows, -1), 'grp', split_a...]
    all_to_all x1 -> x0, waiting for transfers between devices: 16.6 us -> none  [shards(): lax.all_to_all(mixed_rows.reshape(groups, local_rows, -1), 'grp', split_a...]
    pallas_call x4, Pallas kernels: 40.2 us -> 45.3 us  [attend(): pl.pallas_call(flash_step, grid_spec=grid_spec, out_shape=[shape, shape,...]
  transfers between devices with their start and end apart: 3 -> 2, of which waited for: 2 -> 1; matrix products, arithmetic and copies ran while one was open for 11% -> 11% of each run, Pallas kernels for 14% -> 17%
where the time goes in v5:
time: 225 us; the launch traced here: 224 us
  Pallas kernels  128 us (57%)
  other arithmetic  24.1 us (11%)
  local copies, waits for them, and re-layouts  22.7 us (10%)
  waiting for transfers between devices  20.3 us (9%)
  matrix products  15.8 us (7%)
  starting transfers between devices  12.7 us (6%)
    pallas_call x2, Pallas kernels, exchange(): pl.pallas_call(functools.partial(exchange_step, axis, count), out_shape=j...  82.8 us
    pallas_call x4, Pallas kernels, attend(): pl.pallas_call(flash_step, grid_spec=grid_spec, out_shape=[shape, shape,...  45.3 us
    all_to_all x1, waiting for transfers between devices, shards(): lax.all_to_all(arranged, 'grp', split_axis=0, concat_axis=1, tiled=True)[0]  20.3 us
    all_to_all x1, starting transfers between devices, shards(): lax.all_to_all(arranged, 'grp', split_axis=0, concat_axis=1, tiled=True)[0]  11 us
    dot_general x1, matrix products, shards(): jnp.einsum('qc,ctd->tqd', attended, w_out.reshape(local_width, blocks, -1...  4.76 us
  transfers between devices with their start and end apart: 2, of which 1 were waited for; matrix products, arithmetic and copies ran while one was open for 11% of the time, Pallas kernels for 17%

profile of v5, /device:TPU:1, one launch (start us, length us, event | category | flops | bytes accessed | tf_op | source)
XLA Modules:
  0.0 224.1 jit_solution(4425227527948079041)
XLA Ops:
  0.0 3.0 %convert_reduce_fusion = f32[32,32]{1,0:T(8,128)S(1)} fusion(bf16[32,32,2048]{2,1,0:T(8,128)(2,1)} %param.12), kind=kLoop, calls=%fused_computation.11 | loop fusion | flops 4193280 | bytes 4198400 | tf_op jit(solution)/shard_map/reduce_sum | solution.py:139
  4.9 2.5 %multiply_convert_fusion = bf16[32,32,2048]{2,1,0:T(8,128)(2,1)} fusion(bf16[32,32,2048]{2,1,0:T(8,128)(2,1)S(1)} %copy-done.4, f32[32,32]{1,0:T(8,128)S(1)} %add_rsqrt_fusion, f32[32,32]{1,0:T(8,128)S(1)} %broadcast_multiply_fusion), kind=kLoop, calls=%fused_computation.9 | loop fusion | flops 8388608 | bytes 8396800 | tf_op jit(solution)/shard_map/convert_element_type | solution.py:190
  9.9 1.4 copy.38
  12.0 3.9 %fusion.28 = f32[1024,2,128]{0,2,1:T(8,128)S(1)} fusion(bf16[1024,2048,1]{1,0,2:T(8,128)(2,1)} %bitcast.71, bf16[2,128,2048]{2,1,0:T(8,128)(2,1)} %bitcast.78), kind=kOutput, calls=%fused_computation.83 | convolution fusion | flops 1073741824 | bytes 6291456 | tf_op jit(solution)/shard_map/dot_general | solution.py:195
  15.9 1.4 fusion.27
  22.2 1.6 copy.32
  23.8 2.1 gather_fusion.2
  27.2 11.0 %all-to-all-start = ((bf16[32,32,768]{2,1,0:T(8,128)(2,1)}), bf16[32,32,768]{2,1,0:T(8,128)(2,1)S(1)}, u32[]{:S(2)}, u32[]{:S(2)}) async-start(bf16[32,32,768]{2,1,0:T(8,128)(2,1)} %broadcast_select_fusion), calls=%async_computation | async-start | bytes 3145728 | tf_op jit(solution)/shard_map/all_to_all | solution.py:202
  38.3 1.7 collective-permute-start
  40.0 1.4 convert_reduce_fusion.1
  41.4 1.6 fusion.7
  43.4 2.1 fusion.11
  47.6 1.5 scatter_custom_fusion.1
  54.0 2.4 %convolution_convert_fusion.1.v_ref = bf16[256,256]{1,0:T(8,128)(2,1)} fusion(bf16[2048,256]{1,0:T(8,128)(2,1)S(1)} %copy-done, bf16[1,256,2048]{2,1,0:T(8,128)(2,1)} %param.19, f32[256]{0:T(256)S(1)} %add_rsqrt_fusion.1, f32[256]{0:T(256)S(1)} %broadcast_multiply_fusion.1), kind=kOutput, calls=%fused_computation.26 | convolution fusion | flops 270598144 | bytes 2230272 | tf_op jit(solution)/shard_map/dot_general | solution.py:212
  56.3 20.3 %all-to-all-done = bf16[32,32,768]{2,1,0:T(8,128)(2,1)S(1)} async-done(((bf16[32,32,768]{2,1,0:T(8,128)(2,1)}), bf16[32,32,768]{2,1,0:T(8,128)(2,1)S(1)}, u32[]{:S(2)}, u32[]{:S(2)}) %all-to-all-start) | async-done | bytes 1572896 | tf_op jit(solution)/shard_map/all_to_all | solution.py:202
  81.9 11.4 %shard_map.118 = (f32[1024,256]{1,0:T(8,128)}, f32[1024,256]{1,0:T(8,128)}, f32[1024,256]{1,0:T(8,128)}) custom-call(s32[2]{0:T(128)} %broadcast_12_flags_ref.2.flags_ref, s32[1024,1]{1,0:T(8,128)} %iota.51.qrow_ref, s32[1,1024]{1,0:T(1,128)} %iota.52.rank_ref, ...), custom_call_target="tpu_custom_call", output_to_operand_aliasing={{0}: (6, {}), {1}: (7, {}), {2}: (8, {})} | custom-call | tf_op jit(solution)/shard_map/pallas_call | solution.py:63
  94.7 6.7 %shard_map.119 = (f32[1024,256]{1,0:T(8,128)}, f32[1024,256]{1,0:T(8,128)}, f32[1024,256]{1,0:T(8,128)}) custom-call(s32[1]{0:T(128)} %constant.94.clone.1.flags_ref, s32[1024,1]{1,0:T(8,128)} %iota.50.qrow_ref, s32[1,256]{1,0:T(1,128)} %broadcast_in_dim.93.rank_ref, ...), custom_call_target="tpu_custom_call", output_to_operand_aliasing={{0}: (6, {}), {1}: (7, {}), {2}: (8, {})} | custom-call | tf_op jit(solution)/shard_map/pallas_call | solution.py:63
  102.2 18.9 %shard_map.120 = (f32[1024,256]{1,0:T(8,128)}, f32[1024,256]{1,0:T(8,128)}, f32[1024,256]{1,0:T(8,128)}) custom-call(s32[4]{0:T(128)} %compare_convert_fusion.flags_ref, s32[1024,1]{1,0:T(8,128)} %iota.48.qrow_ref, s32[1,2048]{1,0:T(1,128)} %bitcast.82, bf16[1024,768]{1,0:T(8,128)(2,1)} %bitcast.66, ...), custom_call_target="tpu_custom_call", output_to_operand_aliasing={{0}: (6, {}), {1}: (7, {}), {2}: (8, {})} | custom-call | tf_op jit(solution)/shard_map/pallas_call | solution.py:63
  122.0 8.3 %shard_map.121 = (f32[1024,256]{1,0:T(8,128)}, f32[1024,256]{1,0:T(8,128)}, f32[1024,256]{1,0:T(8,128)}) custom-call(s32[4]{0:T(128)} %compare_convert_fusion.1.flags_ref, s32[1024,1]{1,0:T(8,128)} %iota.45.qrow_ref, s32[1,2048]{1,0:T(1,128)} %compare_select_fusion.rank_ref, ...), custom_call_target="tpu_custom_call", output_to_operand_aliasing={{0}: (6, {}), {1}: (7, {}), {2}: (8, {})} | custom-call | tf_op jit(solution)/shard_map/pallas_call | solution.py:63
  130.3 4.8 %convert_bitcast_fusion.x_ref = bf16[8,1024,256]{2,1,0:T(8,128)(2,1)} fusion(bf16[32,8,8,256]{3,2,1,0:T(8,128)(2,1)S(1)} %bitcast.86, f32[1024,256]{1,0:T(8,128)} %get-tuple-element.25, f32[1024,256]{1,0:T(8,128)} %get-tuple-element.26), kind=kOutput, calls=%fused_computation.12 | convolution fusion | flops 1076363264 | bytes 7340032 | tf_op jit(solution)/shard_map/qc,ctd->tqd/dot_general | solution.py:256
  135.0 51.5 %shard_map.122 = bf16[8,1024,256]{2,1,0:T(8,128)(2,1)} custom-call(bf16[8,1024,256]{2,1,0:T(8,128)(2,1)} %convert_bitcast_fusion.x_ref), custom_call_target="tpu_custom_call" | custom-call | tf_op jit(solution)/shard_map/pallas_call | solution.py:113
  186.6 3.7 %reduce_sum.52 = bf16[1024,256]{1,0:T(8,128)(2,1)} reduce(bf16[8,1024,256]{2,1,0:T(8,128)(2,1)} %shard_map.122, bf16[]{:T(256)} %constant.97.clone.1), dimensions={0}, to_apply=%region_6.7 | reduce | flops 1835008 | bytes 4718594 | tf_op jit(solution)/shard_map/reduce_sum | solution.py:260
  190.3 31.3 %shard_map.123 = bf16[32,32,256]{2,1,0:T(8,128)(2,1)} custom-call(bf16[32,32,256]{2,1,0:T(8,128)(2,1)} %bitcast.73), custom_call_target="tpu_custom_call" | custom-call | tf_op jit(solution)/shard_map/pallas_call | solution.py:113
  221.6 1.6 gather_fusion.3
  (79 shorter events, 27.6 us)
Async XLA Ops:
  0.0 20.8 %copy-start = (bf16[2048,256]{1,0:T(8,128)(2,1)S(1)}, bf16[2048,256]{1,0:T(8,128)(2,1)}, u32[]{:S(2)}) copy-start(bf16[2048,256]{1,0:T(8,128)(2,1)} %param.15) | copy-start | bytes 3145732
  0.0 3.5 %copy-start.4 = (bf16[32,32,2048]{2,1,0:T(8,128)(2,1)S(1)}, bf16[32,32,2048]{2,1,0:T(8,128)(2,1)}, u32[]{:S(2)}) copy-start(bf16[32,32,2048]{2,1,0:T(8,128)(2,1)} %param.12) | copy-start | bytes 12582916
  4.8 2.7 %copy-start.11 = (s32[32]{0:T(128)S(1)}, s32[32]{0:T(128)}, u32[]{:S(2)}) copy-start(s32[32]{0:T(128)} %param.20) | copy-start | bytes 388
  4.8 3.5 %copy-start.1 = (s32[32]{0:T(128)S(1)}, s32[32]{0:T(128)}, u32[]{:S(2)}) copy-start(s32[32]{0:T(128)} %param.21) | copy-start | bytes 388
  4.8 4.2 %copy-start.2 = (s32[32]{0:T(128)S(1)}, s32[32]{0:T(128)}, u32[]{:S(2)}) copy-start(s32[32]{0:T(128)} %param.22) | copy-start | bytes 388
  4.8 5.0 %copy-start.7 = (bf16[2048,256]{1,0:T(8,128)(2,1)S(1)}, bf16[2048,256]{1,0:T(8,128)(2,1)}, u32[]{:S(2)}) copy-start(bf16[2048,256]{1,0:T(8,128)(2,1)} %param.14) | copy-start | bytes 3145732
  7.4 3.9 %copy-start.8 = (bf16[2048,256]{1,0:T(8,128)(2,1)S(1)}, bf16[2048,256]{1,0:T(8,128)(2,1)}, u32[]{:S(2)}) copy-start(bf16[2048,256]{1,0:T(8,128)(2,1)} %param.13) | copy-start | bytes 3145732
  12.0 3.9 %copy-start.6 = (bf16[32,32,2048]{2,1,0:T(8,128)(2,1)S(1)}, bf16[32,32,2048]{2,1,0:T(8,128)(2,1)}, u32[]{:S(2)}) copy-start(bf16[32,32,2048]{2,1,0:T(8,128)(2,1)} %multiply_convert_fusion) | copy-start | bytes 12582916
  17.3 2.2 copy-start.5
  25.9 14.1 %copy-start.9 = (s32[1,256]{1,0:T(1,128)S(1)}, s32[1,256]{1,0:T(1,128)}, u32[]{:S(2)}) copy-start(s32[1,256]{1,0:T(1,128)} %param.23) | copy-start | bytes 3076
  27.2 49.4 %all-to-all-start = ((bf16[32,32,768]{2,1,0:T(8,128)(2,1)}), bf16[32,32,768]{2,1,0:T(8,128)(2,1)S(1)}, u32[]{:S(2)}, u32[]{:S(2)}) async-start(bf16[32,32,768]{2,1,0:T(8,128)(2,1)} %broadcast_select_fusion), calls=%async_computation | async-start | bytes 3145728 | tf_op jit(solution)/shard_map/all_to_all | solution.py:202
  38.3 82.8 %collective-permute-start = (bf16[2,2048,256]{2,1,0:T(8,128)(2,1)}, bf16[2,2048,256]{2,1,0:T(8,128)(2,1)}, u32[]{:S(2)}, u32[]{:S(2)}) collective-permute-start(bf16[2,2048,256]{2,1,0:T(8,128)(2,1)} %bitcast.85), channel_id=1, source_target_pairs={{0,128},{8,136},{16,144},{24,152},{32,160},{40,168},{48,176},{56,1... | collective-permute-start | bytes 6291464 | tf_op jit(solution)/shard_map/ppermute | solution.py:134
  76.6 5.3 %copy-start.3 = (bf16[32,32,768]{2,1,0:T(8,128)(2,1)}, bf16[32,32,768]{2,1,0:T(8,128)(2,1)S(1)}, u32[]{:S(2)}) copy-start(bf16[32,32,768]{2,1,0:T(8,128)(2,1)S(1)} %all-to-all-done) | copy-start | bytes 4718596
  122.0 8.3 %copy-start.10 = (bf16[256,2048]{1,0:T(8,128)(2,1)S(1)}, bf16[256,2048]{1,0:T(8,128)(2,1)}, u32[]{:S(2)}) copy-start(bf16[256,2048]{1,0:T(8,128)(2,1)} %param.16) | copy-start | bytes 3145732

commit v6 on v3

--- a/solution.py
+++ b/solution.py
@@ -1,3 +1,5 @@
+import functools
+
 import jax
 import jax.numpy as jnp
 from jax import lax
@@ -65,6 +67,61 @@
         input_output_aliases={6: 0, 7: 1, 8: 2},
         compiler_params=pltpu.CompilerParams(dimension_semantics=("arbitrary", "arbitrary")),
     )(flags, qrow, rank, q_src, k_src, v_src, *state)
+
+
+def exchange_step(axis, count, x_ref, y_ref, local_sem, send_sem, recv_sem):
+    me = lax.axis_index(axis)
+    barrier = pltpu.get_barrier_semaphore()
+    for step in range(1, count):
+        pl.semaphore_signal(
+            barrier, inc=1, device_id={axis: lax.rem(me + step, count)},
+            device_id_type=pl.DeviceIdType.MESH,
+        )
+    pl.semaphore_wait(barrier, count - 1)
+    own = pltpu.make_async_copy(x_ref.at[me], y_ref.at[me], local_sem)
+    own.start()
+    sends = []
+    for step in range(1, count):
+        target = lax.rem(me + step, count)
+        copy = pltpu.make_async_remote_copy(
+            src_ref=x_ref.at[target],
+            dst_ref=y_ref.at[me],
+            send_sem=send_sem.at[step],
+            recv_sem=recv_sem.at[me],
+            device_id={axis: target},
+            device_id_type=pl.DeviceIdType.MESH,
+        )
+        copy.start()
+        sends.append(copy)
+    for copy in sends:
+        copy.wait_send()
+    for step in range(1, count):
+        source = lax.rem(me + count - step, count)
+        pltpu.make_async_remote_copy(
+            src_ref=x_ref.at[source],
+            dst_ref=y_ref.at[source],
+            send_sem=send_sem.at[step],
+            recv_sem=recv_sem.at[source],
+            device_id={axis: source},
+            device_id_type=pl.DeviceIdType.MESH,
+        ).wait_recv()
+    own.wait()
+
+
+def exchange(blocks, axis, collective):
+    count = blocks.shape[0]
+    return pl.pallas_call(
+        functools.partial(exchange_step, axis, count),
+        out_shape=jax.ShapeDtypeStruct(blocks.shape, blocks.dtype),
+        in_specs=[pl.BlockSpec(memory_space=pl.ANY)],
+        out_specs=pl.BlockSpec(memory_space=pl.ANY),
+        scratch_shapes=[
+            pltpu.SemaphoreType.DMA(()),
+            pltpu.SemaphoreType.DMA((count,)),
+            pltpu.SemaphoreType.DMA((count,)),
+        ],
+        compiler_params=pltpu.CompilerParams(collective_id=collective, has_side_effects=True),
+    )(blocks)
 
 
 rope_base = 10000.0
@@ -211,12 +268,8 @@
         ).astype(jnp.bfloat16)
         exchanged = lax.all_to_all(partial_value, "tp", split_axis=0, concat_axis=0, tiled=True)
         mixed_rows = exchanged.astype(jnp.float32).sum(axis=0).astype(jnp.bfloat16)
-        returned.append(
-            lax.all_to_all(
-                mixed_rows.reshape(groups, piece, -1), "grp", split_axis=0, concat_axis=0, tiled=True
-            )
-        )
-    returned_rows = jnp.stack(returned, axis=1).reshape(groups, local_rows, -1)
+        returned.append(mixed_rows.reshape(groups, piece, -1))
+    returned_rows = exchange(jnp.stack(returned, axis=1).reshape(groups, local_rows, -1), "grp", 1)
     return jnp.take(returned_rows, server, axis=0)
 
 

time: 234 us -> 225 us (0.962)
  Pallas kernels: 49.8 us -> 84.4 us
  starting transfers between devices: 56.5 us -> 25.9 us
  waiting for transfers between devices: 61.1 us -> 47.6 us
    all_to_all x2 -> x0, starting transfers between devices: 30.7 us -> none  [shards(): lax.all_to_all(mixed_rows.reshape(groups, piece, -1), 'grp', split_axis=0...]
    pallas_call x0 -> x1, Pallas kernels: none -> 21.4 us  [exchange(): pl.pallas_call(functools.partial(exchange_step, axis, count), out_shape=j...]
    all_to_all x2 -> x0, waiting for transfers between devices: 21.3 us -> none  [shards(): lax.all_to_all(mixed_rows.reshape(groups, piece, -1), 'grp', split_axis=0...]
    pallas_call x6, Pallas kernels: 49.8 us -> 63.1 us  [attend(): pl.pallas_call(flash_step, grid_spec=grid_spec, out_shape=[shape, shape,...]
    all_to_all x2, waiting for transfers between devices: 16.6 us -> 26.5 us  [shards(): lax.all_to_all(partial_value, 'tp', split_axis=0, concat_axis=0, tiled=True)]
  transfers between devices with their start and end apart: 6 -> 4, of which waited for: 5 -> 3; matrix products, arithmetic and copies ran while one was open for 14% -> 13% of each run, Pallas kernels for 18% -> 23%
where the time goes in v6:
time: 225 us; the launch traced here: 224 us
  Pallas kernels  84.4 us (38%)
  waiting for transfers between devices  47.6 us (21%)
  starting transfers between devices  25.9 us (12%)
  other arithmetic  24.9 us (11%)
  local copies, waits for them, and re-layouts  24.1 us (11%)
  matrix products  16.8 us (7%)
    pallas_call x6, Pallas kernels, attend(): pl.pallas_call(flash_step, grid_spec=grid_spec, out_shape=[shape, shape,...  63.1 us
    all_to_all x2, waiting for transfers between devices, shards(): lax.all_to_all(partial_value, 'tp', split_axis=0, concat_axis=0, tiled=True)  26.5 us
    pallas_call x1, Pallas kernels, exchange(): pl.pallas_call(functools.partial(exchange_step, axis, count), out_shape=j...  21.4 us
    all_to_all x1, waiting for transfers between devices, shards(): lax.all_to_all(arranged, 'grp', split_axis=0, concat_axis=1, tiled=True)[0]  20 us
    all_to_all x2, starting transfers between devices, shards(): lax.all_to_all(partial_value, 'tp', split_axis=0, concat_axis=0, tiled=True)  13 us
    all_to_all x1, starting transfers between devices, shards(): lax.all_to_all(arranged, 'grp', split_axis=0, concat_axis=1, tiled=True)[0]  11.2 us
    dot_general x2, matrix products, shards(): jnp.einsum('qc,ctd->tqd', attended, out_by_block, preferred_element_type=...  6.82 us
    another operation x7, local copies, waits for them, and re-layouts  5.55 us
  transfers between devices with their start and end apart: 4, of which 3 were waited for; matrix products, arithmetic and copies ran while one was open for 13% of the time, Pallas kernels for 23%

profile of v6, /device:TPU:1, one launch (start us, length us, event | category | flops | bytes accessed | tf_op | source)
XLA Modules:
  0.0 224.1 jit_solution(14601229669392440163)
XLA Ops:
  0.0 3.0 %convert_reduce_fusion = f32[32,32]{1,0:T(8,128)S(1)} fusion(bf16[32,32,2048]{2,1,0:T(8,128)(2,1)} %param.12), kind=kLoop, calls=%fused_computation.11 | loop fusion | flops 4193280 | bytes 4198400 | tf_op jit(solution)/shard_map/reduce_sum | solution.py:139
  4.9 2.6 %multiply_convert_fusion = bf16[32,32,2048]{2,1,0:T(8,128)(2,1)} fusion(bf16[32,32,2048]{2,1,0:T(8,128)(2,1)S(1)} %copy-done.4, f32[32,32]{1,0:T(8,128)S(1)} %add_rsqrt_fusion, f32[32,32]{1,0:T(8,128)S(1)} %broadcast_multiply_fusion), kind=kLoop, calls=%fused_computation.9 | loop fusion | flops 8388608 | bytes 8396800 | tf_op jit(solution)/shard_map/convert_element_type | solution.py:190
  12.8 3.6 %fusion.32 = f32[1024,2,128]{0,2,1:T(8,128)S(1)} fusion(bf16[1024,2048,1]{1,0,2:T(8,128)(2,1)} %bitcast.87, bf16[2,128,2048]{2,1,0:T(8,128)(2,1)S(1)} %bitcast.95), kind=kOutput, calls=%fused_computation.92 | convolution fusion | flops 1073741824 | bytes 6291456 | tf_op jit(solution)/shard_map/dot_general | solution.py:195
  19.3 1.7 copy-done.5
  25.3 2.1 gather_fusion.2
  28.7 11.2 %all-to-all-start = ((bf16[32,32,768]{2,1,0:T(8,128)(2,1)}), bf16[32,32,768]{2,1,0:T(8,128)(2,1)S(1)}, u32[]{:S(2)}, u32[]{:S(2)}) async-start(bf16[32,32,768]{2,1,0:T(8,128)(2,1)} %broadcast_select_fusion), calls=%async_computation | async-start | bytes 3145728 | tf_op jit(solution)/shard_map/all_to_all | solution.py:202
  39.9 1.7 collective-permute-start
  43.1 1.6 fusion.7
  45.1 2.1 fusion.11
  56.6 1.7 convolution_convert_fusion.1
  58.3 20.0 %all-to-all-done = bf16[32,32,768]{2,1,0:T(8,128)(2,1)S(1)} async-done(((bf16[32,32,768]{2,1,0:T(8,128)(2,1)}), bf16[32,32,768]{2,1,0:T(8,128)(2,1)S(1)}, u32[]{:S(2)}, u32[]{:S(2)}) %all-to-all-start) | async-done | bytes 1572896 | tf_op jit(solution)/shard_map/all_to_all | solution.py:202
  83.0 8.3 %shard_map.118 = (f32[512,256]{1,0:T(8,128)}, f32[512,256]{1,0:T(8,128)}, f32[512,256]{1,0:T(8,128)}) custom-call(s32[2]{0:T(128)} %broadcast_12_flags_ref.2.flags_ref, s32[512,1]{1,0:T(8,128)} %broadcast_in_dim.107.qrow_ref, s32[1,1280]{1,0:T(1,128)} %broadcast_in_dim.104.rank_ref, ...), custom_call_target="tpu_custom_call", output_to_operand_aliasing={{0}: (6, {}), {1}: (7, {}), {2}: (8, {})} | custom-call | tf_op jit(solution)/shard_map/pallas_call | solution.py:63
  91.3 11.6 %shard_map.119 = (f32[512,256]{1,0:T(8,128)}, f32[512,256]{1,0:T(8,128)}, f32[512,256]{1,0:T(8,128)}) custom-call(s32[4]{0:T(128)} %compare_convert_fusion.flags_ref, s32[512,1]{1,0:T(8,128)} %broadcast_in_dim.107.qrow_ref, s32[1,2048]{1,0:T(1,128)} %bitcast.100, ...), custom_call_target="tpu_custom_call", output_to_operand_aliasing={{0}: (6, {}), {1}: (7, {}), {2}: (8, {})} | custom-call | tf_op jit(solution)/shard_map/pallas_call | solution.py:63
  104.1 11.7 %shard_map.120 = (f32[512,256]{1,0:T(8,128)}, f32[512,256]{1,0:T(8,128)}, f32[512,256]{1,0:T(8,128)}) custom-call(s32[4]{0:T(128)} %compare_convert_fusion.1.flags_ref, s32[512,1]{1,0:T(8,128)} %broadcast_in_dim.107.qrow_ref, s32[1,2048]{1,0:T(1,128)} %compare_select_fusion.rank_ref, ...), custom_call_target="tpu_custom_call", output_to_operand_aliasing={{0}: (6, {}), {1}: (7, {}), {2}: (8, {})} | custom-call | tf_op jit(solution)/shard_map/pallas_call | solution.py:63
  115.8 3.2 %convert_bitcast_fusion.2 = bf16[8,512,256]{2,1,0:T(8,128)(2,1)} fusion(bf16[32,8,8,256]{3,2,1,0:T(8,128)(2,1)S(1)} %bitcast.106, f32[512,256]{1,0:T(8,128)} %get-tuple-element.27, f32[512,256]{1,0:T(8,128)} %get-tuple-element.28), kind=kOutput, calls=%fused_computation.23 | convolution fusion | flops 538181632 | bytes 4194304 | tf_op jit(solution)/shard_map/qc,ctd->tqd/dot_general | solution.py:266
  119.1 6.4 %all-to-all-start.1 = ((bf16[8,512,256]{2,1,0:T(8,128)(2,1)}), bf16[8,512,256]{2,1,0:T(8,128)(2,1)S(1)}, u32[]{:S(2)}, u32[]{:S(2)}) async-start(bf16[8,512,256]{2,1,0:T(8,128)(2,1)} %convert_bitcast_fusion.2), calls=%async_computation.1 | async-start | bytes 4194304 | tf_op jit(solution)/shard_map/all_to_all | solution.py:269
  128.8 8.3 %shard_map.121 = (f32[512,256]{1,0:T(8,128)}, f32[512,256]{1,0:T(8,128)}, f32[512,256]{1,0:T(8,128)}) custom-call(s32[2]{0:T(128)} %broadcast_12_flags_ref.2.flags_ref, s32[512,1]{1,0:T(8,128)} %broadcast_in_dim.108.qrow_ref, s32[1,1280]{1,0:T(1,128)} %broadcast_in_dim.104.rank_ref, ...), custom_call_target="tpu_custom_call", output_to_operand_aliasing={{0}: (6, {}), {1}: (7, {}), {2}: (8, {})} | custom-call | tf_op jit(solution)/shard_map/pallas_call | solution.py:63
  137.1 11.5 %shard_map.122 = (f32[512,256]{1,0:T(8,128)}, f32[512,256]{1,0:T(8,128)}, f32[512,256]{1,0:T(8,128)}) custom-call(s32[4]{0:T(128)} %compare_convert_fusion.flags_ref, s32[512,1]{1,0:T(8,128)} %broadcast_in_dim.108.qrow_ref, s32[1,2048]{1,0:T(1,128)} %bitcast.101, ...), custom_call_target="tpu_custom_call", output_to_operand_aliasing={{0}: (6, {}), {1}: (7, {}), {2}: (8, {})} | custom-call | tf_op jit(solution)/shard_map/pallas_call | solution.py:63
  148.7 11.5 %shard_map.123 = (f32[512,256]{1,0:T(8,128)}, f32[512,256]{1,0:T(8,128)}, f32[512,256]{1,0:T(8,128)}) custom-call(s32[4]{0:T(128)} %compare_convert_fusion.1.flags_ref, s32[512,1]{1,0:T(8,128)} %broadcast_in_dim.108.qrow_ref, s32[1,2048]{1,0:T(1,128)} %compare_select_fusion.rank_ref, ...), custom_call_target="tpu_custom_call", output_to_operand_aliasing={{0}: (6, {}), {1}: (7, {}), {2}: (8, {})} | custom-call | tf_op jit(solution)/shard_map/pallas_call | solution.py:63
  160.2 3.6 %convert_bitcast_fusion.1 = bf16[8,512,256]{2,1,0:T(8,128)(2,1)} fusion(bf16[32,8,8,256]{3,2,1,0:T(8,128)(2,1)} %bitcast.105, f32[512,256]{1,0:T(8,128)} %get-tuple-element.35, f32[512,256]{1,0:T(8,128)} %get-tuple-element.36), kind=kOutput, calls=%fused_computation.22 | convolution fusion | flops 538181632 | bytes 4194304 | tf_op jit(solution)/shard_map/qc,ctd->tqd/dot_general | solution.py:266
  163.8 6.6 %all-to-all-start.2 = ((bf16[8,512,256]{2,1,0:T(8,128)(2,1)}), bf16[8,512,256]{2,1,0:T(8,128)(2,1)}, u32[]{:S(2)}, u32[]{:S(2)}) async-start(bf16[8,512,256]{2,1,0:T(8,128)(2,1)} %convert_bitcast_fusion.1), calls=%async_computation.2 | async-start | bytes 4194304 | tf_op jit(solution)/shard_map/all_to_all | solution.py:269
  170.9 26.5 %all-to-all-done.2 = bf16[8,512,256]{2,1,0:T(8,128)(2,1)} async-done(((bf16[8,512,256]{2,1,0:T(8,128)(2,1)}), bf16[8,512,256]{2,1,0:T(8,128)(2,1)}, u32[]{:S(2)}, u32[]{:S(2)}) %all-to-all-start.2) | async-done | bytes 2097184 | tf_op jit(solution)/shard_map/all_to_all | solution.py:269
  197.4 2.0 reduce_sum.65
  200.2 21.4 %shard_map.124 = bf16[32,32,256]{2,1,0:T(8,128)(2,1)} custom-call(bf16[32,32,256]{2,1,0:T(8,128)(2,1)} %bitcast.89), custom_call_target="tpu_custom_call" | custom-call | tf_op jit(solution)/shard_map/pallas_call | solution.py:113
  (98 shorter events, 39.8 us)
Async XLA Ops:
  0.0 22.2 %copy-start = (bf16[2048,256]{1,0:T(8,128)(2,1)S(1)}, bf16[2048,256]{1,0:T(8,128)(2,1)}, u32[]{:S(2)}) copy-start(bf16[2048,256]{1,0:T(8,128)(2,1)} %param.15) | copy-start | bytes 3145732
  0.0 3.5 %copy-start.4 = (bf16[32,32,2048]{2,1,0:T(8,128)(2,1)S(1)}, bf16[32,32,2048]{2,1,0:T(8,128)(2,1)}, u32[]{:S(2)}) copy-start(bf16[32,32,2048]{2,1,0:T(8,128)(2,1)} %param.12) | copy-start | bytes 12582916
  4.8 2.8 %copy-start.13 = (s32[32]{0:T(128)S(1)}, s32[32]{0:T(128)}, u32[]{:S(2)}) copy-start(s32[32]{0:T(128)} %param.20) | copy-start | bytes 388
  4.8 3.5 %copy-start.1 = (s32[32]{0:T(128)S(1)}, s32[32]{0:T(128)}, u32[]{:S(2)}) copy-start(s32[32]{0:T(128)} %param.21) | copy-start | bytes 388
  4.8 4.2 %copy-start.2 = (s32[32]{0:T(128)S(1)}, s32[32]{0:T(128)}, u32[]{:S(2)}) copy-start(s32[32]{0:T(128)} %param.22) | copy-start | bytes 388
  4.8 5.0 %copy-start.7 = (bf16[2048,256]{1,0:T(8,128)(2,1)S(1)}, bf16[2048,256]{1,0:T(8,128)(2,1)}, u32[]{:S(2)}) copy-start(bf16[2048,256]{1,0:T(8,128)(2,1)} %param.14) | copy-start | bytes 3145732
  7.4 3.9 %copy-start.8 = (bf16[2048,256]{1,0:T(8,128)(2,1)S(1)}, bf16[2048,256]{1,0:T(8,128)(2,1)}, u32[]{:S(2)}) copy-start(bf16[2048,256]{1,0:T(8,128)(2,1)} %param.13) | copy-start | bytes 3145732
  11.3 1.4 copy-start.9
  12.8 3.6 %copy-start.6 = (bf16[32,32,2048]{2,1,0:T(8,128)(2,1)S(1)}, bf16[32,32,2048]{2,1,0:T(8,128)(2,1)}, u32[]{:S(2)}) copy-start(bf16[32,32,2048]{2,1,0:T(8,128)(2,1)} %multiply_convert_fusion) | copy-start | bytes 12582916
  12.8 3.7 %copy-start.10 = (bf16[256,2048]{1,0:T(8,128)(2,1)S(1)}, bf16[256,2048]{1,0:T(8,128)(2,1)}, u32[]{:S(2)}) copy-start(bf16[256,2048]{1,0:T(8,128)(2,1)} %copy.54) | copy-start | bytes 3145732
  18.8 2.2 copy-start.5
  28.7 14.3 %copy-start.11 = (s32[1,256]{1,0:T(1,128)S(1)}, s32[1,256]{1,0:T(1,128)}, u32[]{:S(2)}) copy-start(s32[1,256]{1,0:T(1,128)} %param.23) | copy-start | bytes 3076
  28.7 49.5 %all-to-all-start = ((bf16[32,32,768]{2,1,0:T(8,128)(2,1)}), bf16[32,32,768]{2,1,0:T(8,128)(2,1)S(1)}, u32[]{:S(2)}, u32[]{:S(2)}) async-start(bf16[32,32,768]{2,1,0:T(8,128)(2,1)} %broadcast_select_fusion), calls=%async_computation | async-start | bytes 3145728 | tf_op jit(solution)/shard_map/all_to_all | solution.py:202
  39.9 64.2 %collective-permute-start = (bf16[2,2048,256]{2,1,0:T(8,128)(2,1)}, bf16[2,2048,256]{2,1,0:T(8,128)(2,1)}, u32[]{:S(2)}, u32[]{:S(2)}) collective-permute-start(bf16[2,2048,256]{2,1,0:T(8,128)(2,1)} %bitcast.104), channel_id=1, source_target_pairs={{0,128},{8,136},{16,144},{24,152},{32,160},{40,168},{48,176},{56,1... | collective-permute-start | bytes 6291464 | tf_op jit(solution)/shard_map/ppermute | solution.py:134
  78.4 1.6 copy-start.3
  104.1 11.7 %copy-start.12 = (bf16[256,2048]{1,0:T(8,128)(2,1)S(1)}, bf16[256,2048]{1,0:T(8,128)(2,1)}, u32[]{:S(2)}) copy-start(bf16[256,2048]{1,0:T(8,128)(2,1)} %param.16) | copy-start | bytes 3145732
  119.1 44.8 %all-to-all-start.1 = ((bf16[8,512,256]{2,1,0:T(8,128)(2,1)}), bf16[8,512,256]{2,1,0:T(8,128)(2,1)S(1)}, u32[]{:S(2)}, u32[]{:S(2)}) async-start(bf16[8,512,256]{2,1,0:T(8,128)(2,1)} %convert_bitcast_fusion.2), calls=%async_computation.1 | async-start | bytes 4194304 | tf_op jit(solution)/shard_map/all_to_all | solution.py:269
  163.8 33.5 %all-to-all-start.2 = ((bf16[8,512,256]{2,1,0:T(8,128)(2,1)}), bf16[8,512,256]{2,1,0:T(8,128)(2,1)}, u32[]{:S(2)}, u32[]{:S(2)}) async-start(bf16[8,512,256]{2,1,0:T(8,128)(2,1)} %convert_bitcast_fusion.1), calls=%async_computation.2 | async-start | bytes 4194304 | tf_op jit(solution)/shard_map/all_to_all | solution.py:269

commit v7 on v6

--- a/solution.py
+++ b/solution.py
@@ -124,6 +124,53 @@
     )(blocks)
 
 
+def project_step(turned, x_ref, cos_ref, sin_ref, *refs):
+    weights, out_ref = refs[:-1], refs[-1]
+    widened = x_ref[...].astype(jnp.float32)
+    centred = widened - jnp.mean(widened, axis=-1, keepdims=True)
+    variance = jnp.mean(centred * centred, axis=-1, keepdims=True)
+    normed = (centred * lax.rsqrt(variance + norm_eps)).astype(jnp.bfloat16)
+    cosine = cos_ref[...]
+    sine = sin_ref[...]
+    for index, weight in enumerate(weights):
+        width = weight.shape[1]
+        product = jnp.dot(normed, weight[...], preferred_element_type=jnp.float32)
+        if turned[index]:
+            pieces = []
+            for head in range(width // HEAD_DIM):
+                part = product[:, head * HEAD_DIM : (head + 1) * HEAD_DIM]
+                pieces.append(part * cosine + pltpu.roll(part, HEAD_DIM // 2, 1) * sine)
+            product = jnp.concatenate(pieces, axis=1)
+        out_ref[:, index * width : (index + 1) * width] = product.astype(out_ref.dtype)
+
+
+def rope_tables(positions):
+    half_dim = HEAD_DIM // 2
+    frequency = jnp.exp(-jnp.log(rope_base) * jnp.arange(half_dim, dtype=jnp.float32) / half_dim)
+    angles = positions.astype(jnp.float32)[:, None] * frequency[None, :]
+    cosine = jnp.cos(angles)
+    sine = jnp.sin(angles)
+    return jnp.concatenate([cosine, cosine], axis=1), jnp.concatenate([-sine, sine], axis=1)
+
+
+def project(rows, positions, weights, turned, block_rows):
+    count, width = rows.shape
+    cosine, sine = rope_tables(positions)
+    out_width = sum(w.shape[1] for w in weights)
+    return pl.pallas_call(
+        functools.partial(project_step, tuple(turned)),
+        grid=(count // block_rows,),
+        in_specs=[
+            pl.BlockSpec((block_rows, width), lambda i: (i, 0)),
+            pl.BlockSpec((block_rows, HEAD_DIM), lambda i: (i, 0)),
+            pl.BlockSpec((block_rows, HEAD_DIM), lambda i: (i, 0)),
+        ]
+        + [pl.BlockSpec(w.shape, lambda i: (0, 0)) for w in weights],
+        out_specs=pl.BlockSpec((block_rows, out_width), lambda i: (i, 0)),
+        out_shape=jax.ShapeDtypeStruct((count, out_width), jnp.bfloat16),
+    )(rows, cosine, sine, *weights)
+
+
 rope_base = 10000.0
 norm_eps = 1e-05
 
@@ -132,29 +179,6 @@
     mask = 2**apart
     pairs = [(source, source ^ mask) for source in range(lax.axis_size(axis))]
     return lax.ppermute(value, axis, pairs)
-
-
-def layer_norm(token_rows):
-    widened = token_rows.astype(jnp.float32)
-    centred = widened - jnp.mean(widened, axis=-1, keepdims=True)
-    variance = jnp.mean(centred * centred, axis=-1, keepdims=True)
-    return centred * lax.rsqrt(variance + norm_eps)
-
-
-def rotate(projected, positions, head_dim):
-    half_dim = head_dim // 2
-    frequency = jnp.exp(-jnp.log(rope_base) * jnp.arange(half_dim, dtype=jnp.float32) / half_dim)
-    angles = positions.astype(jnp.float32)[:, None] * frequency[None, :]
-    cosine = jnp.cos(angles)[:, None, :]
-    sine_part = jnp.sin(angles)[:, None, :]
-    shaped = projected.reshape(projected.shape[0], -1, head_dim)
-    first_half = shaped[..., :half_dim]
-    second = shaped[..., half_dim:]
-    turned = jnp.concatenate(
-        [first_half * cosine - second * sine_part, second * cosine + first_half * sine_part],
-        axis=-1,
-    )
-    return turned.reshape(projected.shape)
 
 
 def shards(
@@ -187,29 +211,18 @@
         start_of[:, None] + group_id * local_rows + jnp.arange(local_rows, dtype=jnp.int32)[None, :]
     ).reshape(-1)
 
-    normed = layer_norm(tokens.reshape(-1, model_width)).astype(jnp.bfloat16)
-    queries = rotate(
-        jnp.dot(normed, w_query, preferred_element_type=jnp.float32), local_positions, HEAD_DIM
-    ).astype(jnp.bfloat16)
-    new_keys = rotate(
-        jnp.dot(normed, w_key, preferred_element_type=jnp.float32), local_positions, HEAD_DIM
-    ).astype(jnp.bfloat16)
-    new_values = jnp.dot(normed, w_value, preferred_element_type=jnp.float32).astype(jnp.bfloat16)
-    projected = jnp.concatenate([queries, new_keys, new_values], axis=-1).reshape(
-        requests, local_rows, 3 * local_width
-    )
+    projected = project(
+        tokens.reshape(-1, model_width), local_positions, [w_query, w_key, w_value],
+        [True, True, False], 256,
+    ).reshape(requests, local_rows, -1)
     arranged = jnp.take(projected, deal_order, axis=0)
     dealt = lax.all_to_all(arranged, "grp", split_axis=0, concat_axis=1, tiled=True)[0]
     span_len = dealt.shape[0]
 
     own_count = own_len[group_id]
     guest_count = guest_len[partner_id]
-    rec_rows = layer_norm(rec_hidden[0]).astype(jnp.bfloat16)
     rec_positions = rec_index[0]
-    rec_keys = rotate(
-        jnp.dot(rec_rows, w_key, preferred_element_type=jnp.float32), rec_positions, HEAD_DIM
-    ).astype(jnp.bfloat16)
-    rec_values = jnp.dot(rec_rows, w_value, preferred_element_type=jnp.float32).astype(jnp.bfloat16)
+    recomputed = project(rec_hidden[0], rec_positions, [w_key, w_value], [True, False], 256)
     replaced = jnp.zeros((own_cache.shape[2],), jnp.bool_).at[rec_positions].set(True)
 
     heads = local_heads
@@ -220,9 +233,9 @@
     row_of = (
         jnp.arange(span_len, dtype=jnp.int32).reshape(groups, chunks, piece).transpose(1, 0, 2).reshape(-1)
     )
-    rec_count = rec_keys.shape[0]
+    rec_count = recomputed.shape[0]
     fresh = jnp.concatenate(
-        [order[:, local_width:], jnp.concatenate([rec_keys, rec_values], axis=1)], axis=0
+        [order[:, local_width:], recomputed], axis=0
     )
     fresh_rank = jnp.concatenate([row_of, jnp.full((rec_count,), -1, jnp.int32)])[None, :]
     fresh_count = span_len + rec_count

time: 225 us -> 217 us (0.964)
  Pallas kernels: 84.4 us -> 104 us
  matrix products: 16.8 us -> 6.52 us
  other arithmetic: 24.9 us -> 17.9 us
  local copies, waits for them, and re-layouts: 24.1 us -> 19.2 us
  waiting for transfers between devices: 47.6 us -> 43 us
    pallas_call x1, Pallas kernels: 21.4 us -> 42.2 us  [exchange(): pl.pallas_call(functools.partial(exchange_step, axis, count), out_shape=j...]
    pallas_call x6, Pallas kernels: 63.1 us -> 48.1 us  [attend(): pl.pallas_call(flash_step, grid_spec=grid_spec, out_shape=[shape, shape,...]
    pallas_call x0 -> x2, Pallas kernels: none -> 13.4 us  [project(): pl.pallas_call(functools.partial(project_step, tuple(turned)), grid=(coun...]
    dot_general x5 -> x0, matrix products: 10 us -> none  [the longest x1 3.62 us: shards(): jnp.dot(normed, w_key, preferred_element_type=jnp.float32)]
    all_to_all x2, waiting for transfers between devices: 26.5 us -> 17.2 us  [shards(): lax.all_to_all(partial_value, 'tp', split_axis=0, concat_axis=0, tiled=True)]
    reduce_sum x4 -> x0, other arithmetic: 7.31 us -> none  [the longest x2 4.42 us: layer_norm(): centred = widened - jnp.mean(widened, axis=-1, keepdims=True)]
    convert_element_type x4 -> x2, other arithmetic: 3.9 us -> 0.08 us  [rope_tables(): angles = positions.astype(jnp.float32)[:, None] * frequency[None, :]]
    dot_general x2 -> x0, local copies, waits for them, and re-layouts: 2.85 us -> none  [the longest x1 1.43 us: shards(): jnp.dot(normed, w_key, preferred_element_type=jnp.float32)]
  transfers between devices with their start and end apart: 4 -> 4, of which waited for: 3 -> 3; matrix products, arithmetic and copies ran while one was open for 13% -> 10% of each run, Pallas kernels for 23% -> 21%
where the time goes in v7:
time: 217 us; the launch traced here: 216 us
  Pallas kernels  104 us (48%)
  waiting for transfers between devices  43 us (20%)
  starting transfers between devices  25.7 us (12%)
  local copies, waits for them, and re-layouts  19.2 us (9%)
  other arithmetic  17.9 us (8%)
  matrix products  6.52 us (3%)
    pallas_call x6, Pallas kernels, attend(): pl.pallas_call(flash_step, grid_spec=grid_spec, out_shape=[shape, shape,...  48.1 us
    pallas_call x1, Pallas kernels, exchange(): pl.pallas_call(functools.partial(exchange_step, axis, count), out_shape=j...  42.2 us
    all_to_all x1, waiting for transfers between devices, shards(): lax.all_to_all(arranged, 'grp', split_axis=0, concat_axis=1, tiled=True)[0]  22.6 us
    all_to_all x2, waiting for transfers between devices, shards(): lax.all_to_all(partial_value, 'tp', split_axis=0, concat_axis=0, tiled=True)  17.2 us
    pallas_call x2, Pallas kernels, project(): pl.pallas_call(functools.partial(project_step, tuple(turned)), grid=(coun...  13.4 us
    all_to_all x2, starting transfers between devices, shards(): lax.all_to_all(partial_value, 'tp', split_axis=0, concat_axis=0, tiled=True)  13 us
    all_to_all x1, starting transfers between devices, shards(): lax.all_to_all(arranged, 'grp', split_axis=0, concat_axis=1, tiled=True)[0]  11.2 us
    dot_general x2, matrix products, shards(): jnp.einsum('qc,ctd->tqd', attended, out_by_block, preferred_element_type=...  6.52 us
  transfers between devices with their start and end apart: 4, of which 3 were waited for; matrix products, arithmetic and copies ran while one was open for 10% of the time, Pallas kernels for 21%

profile of v7, /device:TPU:1, one launch (start us, length us, event | category | flops | bytes accessed | tf_op | source)
XLA Modules:
  0.0 216.2 jit_solution(14549938976625030819)
XLA Ops:
  4.9 1.9 fusion.6
  8.9 9.4 %shard_map.118 = bf16[1024,768]{1,0:T(8,128)(2,1)} custom-call(bf16[1024,2048]{1,0:T(8,128)(2,1)} %bitcast.50, f32[1024,128]{1,0:T(8,128)} %pad_maximum_fusion.1.cos_ref, f32[1024,128]{1,0:T(8,128)} %pad_maximum_fusion.2.sin_ref, bf16[2048,256]{1,0:T(8,128)(2,1)} %refs_0_.2, bf16[2048,256]{1,0:T(8,128)(2,1)} %refs_0_.3, bf16[2048,256]{1,0:T(8,128)(2,1)} %refs_1_.3), custom_call_target="tpu_custom_call" | custom-call | tf_op jit(solution)/shard_map/pallas_call | solution.py:160
  18.3 2.1 gather_fusion.2
  20.4 1.4 broadcast_select_fusion
  21.7 11.2 %all-to-all-start = ((bf16[32,32,768]{2,1,0:T(8,128)(2,1)}), bf16[32,32,768]{2,1,0:T(8,128)(2,1)S(1)}, u32[]{:S(2)}, u32[]{:S(2)}) async-start(bf16[32,32,768]{2,1,0:T(8,128)(2,1)} %broadcast_select_fusion), calls=%async_computation | async-start | bytes 3145728 | tf_op jit(solution)/shard_map/all_to_all | solution.py:219
  32.9 1.5 collective-permute-start
  37.2 1.7 scatter_custom_fusion.1
  40.2 4.0 %shard_map.119 = bf16[256,512]{1,0:T(8,128)(2,1)} custom-call(bf16[256,2048]{1,0:T(8,128)(2,1)} %bitcast.52, f32[256,128]{1,0:T(8,128)} %get-tuple-element.49.cos_ref, f32[256,128]{1,0:T(8,128)} %get-tuple-element.50.sin_ref, bf16[2048,256]{1,0:T(8,128)(2,1)} %refs_0_.3, bf16[2048,256]{1,0:T(8,128)(2,1)} %refs_1_.3), custom_call_target="tpu_custom_call" | custom-call | tf_op jit(solution)/shard_map/pallas_call | solution.py:160
  48.7 22.6 %all-to-all-done = bf16[32,32,768]{2,1,0:T(8,128)(2,1)S(1)} async-done(((bf16[32,32,768]{2,1,0:T(8,128)(2,1)}), bf16[32,32,768]{2,1,0:T(8,128)(2,1)S(1)}, u32[]{:S(2)}, u32[]{:S(2)}) %all-to-all-start) | async-done | bytes 1572896 | tf_op jit(solution)/shard_map/all_to_all | solution.py:219
  76.8 8.3 %shard_map.123 = (f32[512,256]{1,0:T(8,128)}, f32[512,256]{1,0:T(8,128)}, f32[512,256]{1,0:T(8,128)}) custom-call(s32[2]{0:T(128)} %broadcast_10_flags_ref.2.flags_ref, s32[512,1]{1,0:T(8,128)} %broadcast_in_dim.96.qrow_ref, s32[1,1280]{1,0:T(1,128)} %broadcast_in_dim.92.rank_ref, ...), custom_call_target="tpu_custom_call", output_to_operand_aliasing={{0}: (6, {}), {1}: (7, {}), {2}: (8, {})} | custom-call | tf_op jit(solution)/shard_map/pallas_call | solution.py:63
  85.1 8.8 %shard_map.124 = (f32[512,256]{1,0:T(8,128)}, f32[512,256]{1,0:T(8,128)}, f32[512,256]{1,0:T(8,128)}) custom-call(s32[4]{0:T(128)} %compare_convert_fusion.flags_ref, s32[512,1]{1,0:T(8,128)} %broadcast_in_dim.96.qrow_ref, s32[1,2048]{1,0:T(1,128)} %bitcast.55, ...), custom_call_target="tpu_custom_call", output_to_operand_aliasing={{0}: (6, {}), {1}: (7, {}), {2}: (8, {})} | custom-call | tf_op jit(solution)/shard_map/pallas_call | solution.py:63
  93.9 3.2 %collective-permute-done.k_ref.v_ref = bf16[2,2048,256]{2,1,0:T(8,128)(2,1)} collective-permute-done((bf16[2,2048,256]{2,1,0:T(8,128)(2,1)}, bf16[2,2048,256]{2,1,0:T(8,128)(2,1)}, u32[]{:S(2)}, u32[]{:S(2)}) %collective-permute-start) | collective-permute-done | bytes 2097184 | tf_op jit(solution)/shard_map/ppermute | solution.py:181
  97.1 7.0 %shard_map.125 = (f32[512,256]{1,0:T(8,128)}, f32[512,256]{1,0:T(8,128)}, f32[512,256]{1,0:T(8,128)}) custom-call(s32[4]{0:T(128)} %compare_convert_fusion.1.flags_ref, s32[512,1]{1,0:T(8,128)} %broadcast_in_dim.96.qrow_ref, s32[1,2048]{1,0:T(1,128)} %compare_select_fusion.rank_ref, ...), custom_call_target="tpu_custom_call", output_to_operand_aliasing={{0}: (6, {}), {1}: (7, {}), {2}: (8, {})} | custom-call | tf_op jit(solution)/shard_map/pallas_call | solution.py:63
  104.2 3.3 %convert_bitcast_fusion = bf16[8,512,256]{2,1,0:T(8,128)(2,1)} fusion(bf16[32,8,8,256]{3,2,1,0:T(8,128)(2,1)S(1)} %bitcast.60, f32[512,256]{1,0:T(8,128)} %get-tuple-element.35, f32[512,256]{1,0:T(8,128)} %get-tuple-element.36), kind=kOutput, calls=%fused_computation.6 | convolution fusion | flops 538181632 | bytes 4194304 | tf_op jit(solution)/shard_map/qc,ctd->tqd/dot_general | solution.py:279
  107.4 6.3 %all-to-all-start.2 = ((bf16[8,512,256]{2,1,0:T(8,128)(2,1)}), bf16[8,512,256]{2,1,0:T(8,128)(2,1)S(1)}, u32[]{:S(2)}, u32[]{:S(2)}) async-start(bf16[8,512,256]{2,1,0:T(8,128)(2,1)} %convert_bitcast_fusion), calls=%async_computation.2 | async-start | bytes 4194304 | tf_op jit(solution)/shard_map/all_to_all | solution.py:282
  117.1 8.3 %shard_map.120 = (f32[512,256]{1,0:T(8,128)}, f32[512,256]{1,0:T(8,128)}, f32[512,256]{1,0:T(8,128)}) custom-call(s32[2]{0:T(128)} %broadcast_10_flags_ref.2.flags_ref, s32[512,1]{1,0:T(8,128)} %broadcast_in_dim.95.qrow_ref, s32[1,1280]{1,0:T(1,128)} %broadcast_in_dim.92.rank_ref, ...), custom_call_target="tpu_custom_call", output_to_operand_aliasing={{0}: (6, {}), {1}: (7, {}), {2}: (8, {})} | custom-call | tf_op jit(solution)/shard_map/pallas_call | solution.py:63
  125.4 8.8 %shard_map.121 = (f32[512,256]{1,0:T(8,128)}, f32[512,256]{1,0:T(8,128)}, f32[512,256]{1,0:T(8,128)}) custom-call(s32[4]{0:T(128)} %compare_convert_fusion.flags_ref, s32[512,1]{1,0:T(8,128)} %broadcast_in_dim.95.qrow_ref, s32[1,2048]{1,0:T(1,128)} %bitcast.56, ...), custom_call_target="tpu_custom_call", output_to_operand_aliasing={{0}: (6, {}), {1}: (7, {}), {2}: (8, {})} | custom-call | tf_op jit(solution)/shard_map/pallas_call | solution.py:63
  134.2 6.9 %shard_map.122 = (f32[512,256]{1,0:T(8,128)}, f32[512,256]{1,0:T(8,128)}, f32[512,256]{1,0:T(8,128)}) custom-call(s32[4]{0:T(128)} %compare_convert_fusion.1.flags_ref, s32[512,1]{1,0:T(8,128)} %broadcast_in_dim.95.qrow_ref, s32[1,2048]{1,0:T(1,128)} %compare_select_fusion.rank_ref, ...), custom_call_target="tpu_custom_call", output_to_operand_aliasing={{0}: (6, {}), {1}: (7, {}), {2}: (8, {})} | custom-call | tf_op jit(solution)/shard_map/pallas_call | solution.py:63
  141.1 3.3 %convert_bitcast_fusion.1 = bf16[8,512,256]{2,1,0:T(8,128)(2,1)} fusion(bf16[32,8,8,256]{3,2,1,0:T(8,128)(2,1)S(1)} %bitcast.61, f32[512,256]{1,0:T(8,128)} %get-tuple-element.27, f32[512,256]{1,0:T(8,128)} %get-tuple-element.28), kind=kOutput, calls=%fused_computation.7 | convolution fusion | flops 538181632 | bytes 4194304 | tf_op jit(solution)/shard_map/qc,ctd->tqd/dot_general | solution.py:279
  144.4 6.6 %all-to-all-start.1 = ((bf16[8,512,256]{2,1,0:T(8,128)(2,1)}), bf16[8,512,256]{2,1,0:T(8,128)(2,1)}, u32[]{:S(2)}, u32[]{:S(2)}) async-start(bf16[8,512,256]{2,1,0:T(8,128)(2,1)} %convert_bitcast_fusion.1), calls=%async_computation.1 | async-start | bytes 4194304 | tf_op jit(solution)/shard_map/all_to_all | solution.py:282
  151.4 17.2 %all-to-all-done.1 = bf16[8,512,256]{2,1,0:T(8,128)(2,1)} async-done(((bf16[8,512,256]{2,1,0:T(8,128)(2,1)}), bf16[8,512,256]{2,1,0:T(8,128)(2,1)}, u32[]{:S(2)}, u32[]{:S(2)}) %all-to-all-start.1) | async-done | bytes 2097184 | tf_op jit(solution)/shard_map/all_to_all | solution.py:282
  168.6 2.0 reduce_sum.24
  171.5 42.2 %shard_map.126 = bf16[32,32,256]{2,1,0:T(8,128)(2,1)} custom-call(bf16[32,32,256]{2,1,0:T(8,128)(2,1)} %bitcast.51), custom_call_target="tpu_custom_call" | custom-call | tf_op jit(solution)/shard_map/pallas_call | solution.py:113
  213.6 1.6 gather_fusion.3
  (60 shorter events, 26.6 us)
Async XLA Ops:
  21.7 12.7 %copy-start = (s32[32]{0:T(128)S(1)}, s32[32]{0:T(128)}, u32[]{:S(2)}) copy-start(s32[32]{0:T(128)} %param.22) | copy-start | bytes 388
  21.7 13.3 %copy-start.1 = (s32[32]{0:T(128)S(1)}, s32[32]{0:T(128)}, u32[]{:S(2)}) copy-start(s32[32]{0:T(128)} %param.21) | copy-start | bytes 388
  21.7 13.9 %copy-start.4 = (s32[1,256]{1,0:T(1,128)S(1)}, s32[1,256]{1,0:T(1,128)}, u32[]{:S(2)}) copy-start(s32[1,256]{1,0:T(1,128)} %param.23) | copy-start | bytes 3076
  21.7 49.5 %all-to-all-start = ((bf16[32,32,768]{2,1,0:T(8,128)(2,1)}), bf16[32,32,768]{2,1,0:T(8,128)(2,1)S(1)}, u32[]{:S(2)}, u32[]{:S(2)}) async-start(bf16[32,32,768]{2,1,0:T(8,128)(2,1)} %broadcast_select_fusion), calls=%async_computation | async-start | bytes 3145728 | tf_op jit(solution)/shard_map/all_to_all | solution.py:219
  32.9 64.2 %collective-permute-start = (bf16[2,2048,256]{2,1,0:T(8,128)(2,1)}, bf16[2,2048,256]{2,1,0:T(8,128)(2,1)}, u32[]{:S(2)}, u32[]{:S(2)}) collective-permute-start(bf16[2,2048,256]{2,1,0:T(8,128)(2,1)} %bitcast.59), channel_id=1, source_target_pairs={{0,128},{8,136},{16,144},{24,152},{32,160},{40,168},{48,176},{56,1... | collective-permute-start | bytes 6291464 | tf_op jit(solution)/shard_map/ppermute | solution.py:181
  71.4 2.4 %copy-start.2 = (bf16[2,32,16,768]{3,2,1,0:T(8,128)(2,1)}, bf16[2,32,16,768]{3,2,1,0:T(8,128)(2,1)S(1)}, u32[]{:S(2)}) copy-start(bf16[2,32,16,768]{3,2,1,0:T(8,128)(2,1)S(1)} %copy.33) | copy-start | bytes 4718596
  71.4 1.1 copy-start.3
  97.1 7.0 %copy-start.5 = (bf16[256,2048]{1,0:T(8,128)(2,1)S(1)}, bf16[256,2048]{1,0:T(8,128)(2,1)}, u32[]{:S(2)}) copy-start(bf16[256,2048]{1,0:T(8,128)(2,1)} %param.16) | copy-start | bytes 3145732
  107.4 37.0 %all-to-all-start.2 = ((bf16[8,512,256]{2,1,0:T(8,128)(2,1)}), bf16[8,512,256]{2,1,0:T(8,128)(2,1)S(1)}, u32[]{:S(2)}, u32[]{:S(2)}) async-start(bf16[8,512,256]{2,1,0:T(8,128)(2,1)} %convert_bitcast_fusion), calls=%async_computation.2 | async-start | bytes 4194304 | tf_op jit(solution)/shard_map/all_to_all | solution.py:282
  144.4 24.3 %all-to-all-start.1 = ((bf16[8,512,256]{2,1,0:T(8,128)(2,1)}), bf16[8,512,256]{2,1,0:T(8,128)(2,1)}, u32[]{:S(2)}, u32[]{:S(2)}) async-start(bf16[8,512,256]{2,1,0:T(8,128)(2,1)} %convert_bitcast_fusion.1), calls=%async_computation.1 | async-start | bytes 4194304 | tf_op jit(solution)/shard_map/all_to_all | solution.py:282

commit v8 on v7

--- a/solution.py
+++ b/solution.py
@@ -253,6 +253,7 @@
     out_by_block = w_out.reshape(local_width, blocks, -1)
 
     returned = []
+    exchanged = []
     for chunk in range(chunks):
         query_rows = row_of[chunk * chunk_len : (chunk + 1) * chunk_len][:, None]
         state = (
@@ -279,10 +280,13 @@
         partial_value = jnp.einsum(
             "qc,ctd->tqd", attended, out_by_block, preferred_element_type=jnp.float32
         ).astype(jnp.bfloat16)
-        exchanged = lax.all_to_all(partial_value, "tp", split_axis=0, concat_axis=0, tiled=True)
-        mixed_rows = exchanged.astype(jnp.float32).sum(axis=0).astype(jnp.bfloat16)
-        returned.append(mixed_rows.reshape(groups, piece, -1))
-    returned_rows = exchange(jnp.stack(returned, axis=1).reshape(groups, local_rows, -1), "grp", 1)
+        exchanged.append(
+            lax.all_to_all(partial_value, "tp", split_axis=0, concat_axis=0, tiled=True)
+        )
+    for chunk in range(chunks):
+        mixed_rows = exchanged[chunk].astype(jnp.float32).sum(axis=0).astype(jnp.bfloat16)
+        returned.append(exchange(mixed_rows.reshape(groups, piece, -1), "grp", 1 + chunk))
+    returned_rows = jnp.stack(returned, axis=1).reshape(groups, local_rows, -1)
     return jnp.take(returned_rows, server, axis=0)
 
 

time: 217 us -> 207 us (0.954)
  waiting for transfers between devices: 43 us -> 24.4 us
  Pallas kernels: 104 us -> 110 us
    all_to_all x2, waiting for transfers between devices: 17.2 us -> 0.01 us  [shards(): lax.all_to_all(partial_value, 'tp', split_axis=0, concat_axis=0, tiled=True)]
    pallas_call x1 -> x2, Pallas kernels: 42.2 us -> 47.1 us  [exchange(): pl.pallas_call(functools.partial(exchange_step, axis, count), out_shape=j...]
    another operation x7 -> x8, local copies, waits for them, and re-layouts: 5.56 us -> 5.63 us
  transfers between devices with their start and end apart: 4 -> 4, of which waited for: 3 -> 2; matrix products, arithmetic and copies ran while one was open for 10% -> 11% of each run, Pallas kernels for 21% -> 36%
where the time goes in v8:
time: 207 us; the launch traced here: 205 us
  Pallas kernels  110 us (53%)
  starting transfers between devices  25.7 us (12%)
  waiting for transfers between devices  24.4 us (12%)
  other arithmetic  19.9 us (10%)
  local copies, waits for them, and re-layouts  18.4 us (9%)
  matrix products  6.53 us (3%)
    pallas_call x6, Pallas kernels, attend(): pl.pallas_call(flash_step, grid_spec=grid_spec, out_shape=[shape, shape,...  49.8 us
    pallas_call x2, Pallas kernels, exchange(): pl.pallas_call(functools.partial(exchange_step, axis, count), out_shape=j...  47.1 us
    all_to_all x1, waiting for transfers between devices, shards(): lax.all_to_all(arranged, 'grp', split_axis=0, concat_axis=1, tiled=True)[0]  22.1 us
    pallas_call x2, Pallas kernels, project(): pl.pallas_call(functools.partial(project_step, tuple(turned)), grid=(coun...  13.4 us
    all_to_all x2, starting transfers between devices, shards(): lax.all_to_all(partial_value, 'tp', split_axis=0, concat_axis=0, tiled=True)  13 us
    all_to_all x1, starting transfers between devices, shards(): lax.all_to_all(arranged, 'grp', split_axis=0, concat_axis=1, tiled=True)[0]  11.2 us
    dot_general x2, matrix products, shards(): jnp.einsum('qc,ctd->tqd', attended, out_by_block, preferred_element_type=...  6.53 us
    another operation x7, local copies, waits for them, and re-layouts  5.58 us
  transfers between devices with their start and end apart: 4, of which 2 were waited for; matrix products, arithmetic and copies ran while one was open for 11% of the time, Pallas kernels for 36%

profile of v8, /device:TPU:1, one launch (start us, length us, event | category | flops | bytes accessed | tf_op | source)
XLA Modules:
  0.0 205.4 jit_solution(1173007651062200247)
XLA Ops:
  3.4 1.4 gather_fusion
  4.9 1.9 fusion.6
  8.9 9.4 %shard_map.118 = bf16[1024,768]{1,0:T(8,128)(2,1)} custom-call(bf16[1024,2048]{1,0:T(8,128)(2,1)} %bitcast.52, f32[1024,128]{1,0:T(8,128)} %pad_maximum_fusion.1.cos_ref, f32[1024,128]{1,0:T(8,128)} %pad_maximum_fusion.2.sin_ref, bf16[2048,256]{1,0:T(8,128)(2,1)} %refs_0_.2, bf16[2048,256]{1,0:T(8,128)(2,1)} %refs_0_.3, bf16[2048,256]{1,0:T(8,128)(2,1)} %refs_1_.3), custom_call_target="tpu_custom_call" | custom-call | tf_op jit(solution)/shard_map/pallas_call | solution.py:160
  18.3 2.1 gather_fusion.2
  20.4 1.4 broadcast_select_fusion
  21.8 11.2 %all-to-all-start = ((bf16[32,32,768]{2,1,0:T(8,128)(2,1)}), bf16[32,32,768]{2,1,0:T(8,128)(2,1)S(1)}, u32[]{:S(2)}, u32[]{:S(2)}) async-start(bf16[32,32,768]{2,1,0:T(8,128)(2,1)} %broadcast_select_fusion), calls=%async_computation | async-start | bytes 3145728 | tf_op jit(solution)/shard_map/all_to_all | solution.py:219
  32.9 1.5 collective-permute-start
  37.3 1.7 scatter_custom_fusion.1
  40.3 4.0 %shard_map.119 = bf16[256,512]{1,0:T(8,128)(2,1)} custom-call(bf16[256,2048]{1,0:T(8,128)(2,1)} %bitcast.54, f32[256,128]{1,0:T(8,128)} %get-tuple-element.49.cos_ref, f32[256,128]{1,0:T(8,128)} %get-tuple-element.50.sin_ref, bf16[2048,256]{1,0:T(8,128)(2,1)} %refs_0_.3, bf16[2048,256]{1,0:T(8,128)(2,1)} %refs_1_.3), custom_call_target="tpu_custom_call" | custom-call | tf_op jit(solution)/shard_map/pallas_call | solution.py:160
  49.2 22.1 %all-to-all-done = bf16[32,32,768]{2,1,0:T(8,128)(2,1)S(1)} async-done(((bf16[32,32,768]{2,1,0:T(8,128)(2,1)}), bf16[32,32,768]{2,1,0:T(8,128)(2,1)S(1)}, u32[]{:S(2)}, u32[]{:S(2)}) %all-to-all-start) | async-done | bytes 1572896 | tf_op jit(solution)/shard_map/all_to_all | solution.py:219
  76.8 8.3 %shard_map.124 = (f32[512,256]{1,0:T(8,128)}, f32[512,256]{1,0:T(8,128)}, f32[512,256]{1,0:T(8,128)}) custom-call(s32[2]{0:T(128)} %broadcast_10_flags_ref.2.flags_ref, s32[512,1]{1,0:T(8,128)} %broadcast_in_dim.96.qrow_ref, s32[1,1280]{1,0:T(1,128)} %broadcast_in_dim.92.rank_ref, ...), custom_call_target="tpu_custom_call", output_to_operand_aliasing={{0}: (6, {}), {1}: (7, {}), {2}: (8, {})} | custom-call | tf_op jit(solution)/shard_map/pallas_call | solution.py:63
  85.2 9.6 %shard_map.125 = (f32[512,256]{1,0:T(8,128)}, f32[512,256]{1,0:T(8,128)}, f32[512,256]{1,0:T(8,128)}) custom-call(s32[4]{0:T(128)} %compare_convert_fusion.flags_ref, s32[512,1]{1,0:T(8,128)} %broadcast_in_dim.96.qrow_ref, s32[1,2048]{1,0:T(1,128)} %bitcast.59, ...), custom_call_target="tpu_custom_call", output_to_operand_aliasing={{0}: (6, {}), {1}: (7, {}), {2}: (8, {})} | custom-call | tf_op jit(solution)/shard_map/pallas_call | solution.py:63
  94.7 2.4 %collective-permute-done.k_ref.v_ref = bf16[2,2048,256]{2,1,0:T(8,128)(2,1)} collective-permute-done((bf16[2,2048,256]{2,1,0:T(8,128)(2,1)}, bf16[2,2048,256]{2,1,0:T(8,128)(2,1)}, u32[]{:S(2)}, u32[]{:S(2)}) %collective-permute-start) | collective-permute-done | bytes 2097184 | tf_op jit(solution)/shard_map/ppermute | solution.py:181
  97.1 7.0 %shard_map.126 = (f32[512,256]{1,0:T(8,128)}, f32[512,256]{1,0:T(8,128)}, f32[512,256]{1,0:T(8,128)}) custom-call(s32[4]{0:T(128)} %compare_convert_fusion.1.flags_ref, s32[512,1]{1,0:T(8,128)} %broadcast_in_dim.96.qrow_ref, s32[1,2048]{1,0:T(1,128)} %compare_select_fusion.rank_ref, ...), custom_call_target="tpu_custom_call", output_to_operand_aliasing={{0}: (6, {}), {1}: (7, {}), {2}: (8, {})} | custom-call | tf_op jit(solution)/shard_map/pallas_call | solution.py:63
  104.2 3.3 %convert_bitcast_fusion = bf16[8,512,256]{2,1,0:T(8,128)(2,1)} fusion(bf16[32,8,8,256]{3,2,1,0:T(8,128)(2,1)S(1)} %bitcast.64, f32[512,256]{1,0:T(8,128)} %get-tuple-element.35, f32[512,256]{1,0:T(8,128)} %get-tuple-element.36), kind=kOutput, calls=%fused_computation.6 | convolution fusion | flops 538181632 | bytes 4194304 | tf_op jit(solution)/shard_map/qc,ctd->tqd/dot_general | solution.py:280
  107.4 6.4 %all-to-all-start.2 = ((bf16[8,512,256]{2,1,0:T(8,128)(2,1)}), bf16[8,512,256]{2,1,0:T(8,128)(2,1)S(1)}, u32[]{:S(2)}, u32[]{:S(2)}) async-start(bf16[8,512,256]{2,1,0:T(8,128)(2,1)} %convert_bitcast_fusion), calls=%async_computation.2 | async-start | bytes 4194304 | tf_op jit(solution)/shard_map/all_to_all | solution.py:284
  117.2 8.3 %shard_map.120 = (f32[512,256]{1,0:T(8,128)}, f32[512,256]{1,0:T(8,128)}, f32[512,256]{1,0:T(8,128)}) custom-call(s32[2]{0:T(128)} %broadcast_10_flags_ref.2.flags_ref, s32[512,1]{1,0:T(8,128)} %broadcast_in_dim.95.qrow_ref, s32[1,1280]{1,0:T(1,128)} %broadcast_in_dim.92.rank_ref, ...), custom_call_target="tpu_custom_call", output_to_operand_aliasing={{0}: (6, {}), {1}: (7, {}), {2}: (8, {})} | custom-call | tf_op jit(solution)/shard_map/pallas_call | solution.py:63
  125.5 9.6 %shard_map.121 = (f32[512,256]{1,0:T(8,128)}, f32[512,256]{1,0:T(8,128)}, f32[512,256]{1,0:T(8,128)}) custom-call(s32[4]{0:T(128)} %compare_convert_fusion.flags_ref, s32[512,1]{1,0:T(8,128)} %broadcast_in_dim.95.qrow_ref, s32[1,2048]{1,0:T(1,128)} %bitcast.60, ...), custom_call_target="tpu_custom_call", output_to_operand_aliasing={{0}: (6, {}), {1}: (7, {}), {2}: (8, {})} | custom-call | tf_op jit(solution)/shard_map/pallas_call | solution.py:63
  135.1 6.9 %shard_map.122 = (f32[512,256]{1,0:T(8,128)}, f32[512,256]{1,0:T(8,128)}, f32[512,256]{1,0:T(8,128)}) custom-call(s32[4]{0:T(128)} %compare_convert_fusion.1.flags_ref, s32[512,1]{1,0:T(8,128)} %broadcast_in_dim.95.qrow_ref, s32[1,2048]{1,0:T(1,128)} %compare_select_fusion.rank_ref, ...), custom_call_target="tpu_custom_call", output_to_operand_aliasing={{0}: (6, {}), {1}: (7, {}), {2}: (8, {})} | custom-call | tf_op jit(solution)/shard_map/pallas_call | solution.py:63
  142.0 3.3 %convert_bitcast_fusion.1 = bf16[8,512,256]{2,1,0:T(8,128)(2,1)} fusion(bf16[32,8,8,256]{3,2,1,0:T(8,128)(2,1)S(1)} %bitcast.65, f32[512,256]{1,0:T(8,128)} %get-tuple-element.27, f32[512,256]{1,0:T(8,128)} %get-tuple-element.28), kind=kOutput, calls=%fused_computation.7 | convolution fusion | flops 538181632 | bytes 4194304 | tf_op jit(solution)/shard_map/qc,ctd->tqd/dot_general | solution.py:280
  145.3 6.7 %all-to-all-start.1 = ((bf16[8,512,256]{2,1,0:T(8,128)(2,1)}), bf16[8,512,256]{2,1,0:T(8,128)(2,1)}, u32[]{:S(2)}, u32[]{:S(2)}) async-start(bf16[8,512,256]{2,1,0:T(8,128)(2,1)} %convert_bitcast_fusion.1), calls=%async_computation.1 | async-start | bytes 4194304 | tf_op jit(solution)/shard_map/all_to_all | solution.py:284
  153.0 27.8 %shard_map.127 = bf16[32,16,256]{2,1,0:T(8,128)(2,1)} custom-call(bf16[32,16,256]{2,1,0:T(8,128)(2,1)} %bitcast.56), custom_call_target="tpu_custom_call" | custom-call | tf_op jit(solution)/shard_map/pallas_call | solution.py:113
  180.9 2.7 %reduce_sum.24 = bf16[512,256]{1,0:T(8,128)(2,1)} reduce(bf16[8,512,256]{2,1,0:T(8,128)(2,1)} %all-to-all-done.1, bf16[]{:T(256)} %constant.88.clone.1), dimensions={0}, to_apply=%region_2.3 | reduce | flops 917504 | bytes 2359298 | tf_op jit(solution)/shard_map/reduce_sum | solution.py:287
  183.6 19.2 %shard_map.123 = bf16[32,16,256]{2,1,0:T(8,128)(2,1)} custom-call(bf16[32,16,256]{2,1,0:T(8,128)(2,1)} %bitcast.55), custom_call_target="tpu_custom_call" | custom-call | tf_op jit(solution)/shard_map/pallas_call | solution.py:113
  (64 shorter events, 27.2 us)
Async XLA Ops:
  21.7 12.7 %copy-start = (s32[32]{0:T(128)S(1)}, s32[32]{0:T(128)}, u32[]{:S(2)}) copy-start(s32[32]{0:T(128)} %param.22) | copy-start | bytes 388
  21.7 13.3 %copy-start.1 = (s32[32]{0:T(128)S(1)}, s32[32]{0:T(128)}, u32[]{:S(2)}) copy-start(s32[32]{0:T(128)} %param.21) | copy-start | bytes 388
  21.7 13.9 %copy-start.5 = (s32[1,256]{1,0:T(1,128)S(1)}, s32[1,256]{1,0:T(1,128)}, u32[]{:S(2)}) copy-start(s32[1,256]{1,0:T(1,128)} %param.23) | copy-start | bytes 3076
  21.8 49.5 %all-to-all-start = ((bf16[32,32,768]{2,1,0:T(8,128)(2,1)}), bf16[32,32,768]{2,1,0:T(8,128)(2,1)S(1)}, u32[]{:S(2)}, u32[]{:S(2)}) async-start(bf16[32,32,768]{2,1,0:T(8,128)(2,1)} %broadcast_select_fusion), calls=%async_computation | async-start | bytes 3145728 | tf_op jit(solution)/shard_map/all_to_all | solution.py:219
  32.9 64.2 %collective-permute-start = (bf16[2,2048,256]{2,1,0:T(8,128)(2,1)}, bf16[2,2048,256]{2,1,0:T(8,128)(2,1)}, u32[]{:S(2)}, u32[]{:S(2)}) collective-permute-start(bf16[2,2048,256]{2,1,0:T(8,128)(2,1)} %bitcast.63), channel_id=1, source_target_pairs={{0,128},{8,136},{16,144},{24,152},{32,160},{40,168},{48,176},{56,1... | collective-permute-start | bytes 6291464 | tf_op jit(solution)/shard_map/ppermute | solution.py:181
  71.4 2.4 %copy-start.2 = (bf16[2,32,16,768]{3,2,1,0:T(8,128)(2,1)}, bf16[2,32,16,768]{3,2,1,0:T(8,128)(2,1)S(1)}, u32[]{:S(2)}) copy-start(bf16[2,32,16,768]{3,2,1,0:T(8,128)(2,1)S(1)} %copy.33) | copy-start | bytes 4718596
  71.4 1.1 copy-start.3
  97.1 7.1 %copy-start.6 = (bf16[256,2048]{1,0:T(8,128)(2,1)S(1)}, bf16[256,2048]{1,0:T(8,128)(2,1)}, u32[]{:S(2)}) copy-start(bf16[256,2048]{1,0:T(8,128)(2,1)} %param.16) | copy-start | bytes 3145732
  107.4 37.9 %all-to-all-start.2 = ((bf16[8,512,256]{2,1,0:T(8,128)(2,1)}), bf16[8,512,256]{2,1,0:T(8,128)(2,1)S(1)}, u32[]{:S(2)}, u32[]{:S(2)}) async-start(bf16[8,512,256]{2,1,0:T(8,128)(2,1)} %convert_bitcast_fusion), calls=%async_computation.2 | async-start | bytes 4194304 | tf_op jit(solution)/shard_map/all_to_all | solution.py:284
  145.3 35.6 %all-to-all-start.1 = ((bf16[8,512,256]{2,1,0:T(8,128)(2,1)}), bf16[8,512,256]{2,1,0:T(8,128)(2,1)}, u32[]{:S(2)}, u32[]{:S(2)}) async-start(bf16[8,512,256]{2,1,0:T(8,128)(2,1)} %convert_bitcast_fusion.1), calls=%async_computation.1 | async-start | bytes 4194304 | tf_op jit(solution)/shard_map/all_to_all | solution.py:284
  180.9 21.9 %copy-start.4 = (bf16[32,16,256]{2,1,0:T(8,128)(2,1)S(1)}, bf16[32,16,256]{2,1,0:T(8,128)(2,1)}, u32[]{:S(2)}) copy-start(bf16[32,16,256]{2,1,0:T(8,128)(2,1)} %shard_map.127) | copy-start | bytes 786436

commit v9 on v8

--- a/solution.py
+++ b/solution.py
@@ -241,7 +241,7 @@
     fresh_count = span_len + rec_count
     never = jnp.int32(1 << 30)
     cap = own_cache.shape[2]
-    block_len = 512
+    block_len = 1024
     key_rows = jnp.arange(cap, dtype=jnp.int32)
     own_rank = jnp.where((key_rows < own_count) & ~replaced, -1, never)[None, :]
     own_flags = (jnp.arange(cap // block_len, dtype=jnp.int32) * block_len < own_count).astype(jnp.int32)
@@ -262,9 +262,9 @@
             jnp.zeros((chunk_len, local_width), jnp.float32),
         )
         state = attend(
-            state, jnp.ones((2,), jnp.int32), query_rows, fresh_rank, order, chunk,
+            state, jnp.ones((1,), jnp.int32), query_rows, fresh_rank, order, chunk,
             fresh, lambda h, kb: (kb, h), fresh, lambda h, kb: (kb, heads + h),
-            fresh_count, heads, fresh_count // 2,
+            fresh_count, heads, fresh_count,
         )
         state = attend(
             state, own_flags, query_rows, own_rank, order, chunk,

time: 207 us -> 203 us (0.981)
  Pallas kernels: 110 us -> 103 us
  waiting for transfers between devices: 24.4 us -> 29.3 us
    pallas_call x6, Pallas kernels: 49.8 us -> 37.4 us  [attend(): pl.pallas_call(flash_step, grid_spec=grid_spec, out_shape=[shape, shape,...]
    ppermute x1, waiting for transfers between devices: 2.37 us -> 7.24 us  [swapped(): return lax.ppermute(value, axis, pairs)]
    pallas_call x2, Pallas kernels: 47.1 us -> 51.8 us  [exchange(): pl.pallas_call(functools.partial(exchange_step, axis, count), out_shape=j...]
    another operation x7 -> x6, local copies, waits for them, and re-layouts: 5.58 us -> 5.01 us
  transfers between devices with their start and end apart: 4 -> 4, of which waited for: 2 -> 2; matrix products, arithmetic and copies ran while one was open for 11% -> 11% of each run, Pallas kernels for 36% -> 31%
where the time goes in v9:
time: 203 us; the launch traced here: 202 us
  Pallas kernels  103 us (51%)
  waiting for transfers between devices  29.3 us (14%)
  starting transfers between devices  25.7 us (13%)
  other arithmetic  19.9 us (10%)
  local copies, waits for them, and re-layouts  17.8 us (9%)
  matrix products  6.53 us (3%)
    pallas_call x2, Pallas kernels, exchange(): pl.pallas_call(functools.partial(exchange_step, axis, count), out_shape=j...  51.8 us
    pallas_call x6, Pallas kernels, attend(): pl.pallas_call(flash_step, grid_spec=grid_spec, out_shape=[shape, shape,...  37.4 us
    all_to_all x1, waiting for transfers between devices, shards(): lax.all_to_all(arranged, 'grp', split_axis=0, concat_axis=1, tiled=True)[0]  22.1 us
    pallas_call x2, Pallas kernels, project(): pl.pallas_call(functools.partial(project_step, tuple(turned)), grid=(coun...  13.4 us
    all_to_all x2, starting transfers between devices, shards(): lax.all_to_all(partial_value, 'tp', split_axis=0, concat_axis=0, tiled=True)  13 us
    all_to_all x1, starting transfers between devices, shards(): lax.all_to_all(arranged, 'grp', split_axis=0, concat_axis=1, tiled=True)[0]  11.2 us
    ppermute x1, waiting for transfers between devices, swapped(): return lax.ppermute(value, axis, pairs)  7.24 us
    dot_general x2, matrix products, shards(): jnp.einsum('qc,ctd->tqd', attended, out_by_block, preferred_element_type=...  6.53 us
  transfers between devices with their start and end apart: 4, of which 2 were waited for; matrix products, arithmetic and copies ran while one was open for 11% of the time, Pallas kernels for 31%

profile of v9, /device:TPU:1, one launch (start us, length us, event | category | flops | bytes accessed | tf_op | source)
XLA Modules:
  0.0 202.0 jit_solution(4351113599139231682)
XLA Ops:
  3.4 1.4 gather_fusion
  4.9 1.9 fusion.6
  8.9 9.4 %shard_map.118 = bf16[1024,768]{1,0:T(8,128)(2,1)} custom-call(bf16[1024,2048]{1,0:T(8,128)(2,1)} %bitcast.52, f32[1024,128]{1,0:T(8,128)} %pad_maximum_fusion.1.cos_ref, f32[1024,128]{1,0:T(8,128)} %pad_maximum_fusion.2.sin_ref, bf16[2048,256]{1,0:T(8,128)(2,1)} %refs_0_.2, bf16[2048,256]{1,0:T(8,128)(2,1)} %refs_0_.3, bf16[2048,256]{1,0:T(8,128)(2,1)} %refs_1_.3), custom_call_target="tpu_custom_call" | custom-call | tf_op jit(solution)/shard_map/pallas_call | solution.py:160
  18.3 2.1 %gather_fusion.2 = bf16[32,32,768]{2,1,0:T(8,128)(2,1)S(1)} fusion(bf16[32,32,768]{2,1,0:T(8,128)(2,1)} %bitcast.51, s32[1024]{0:T(1024)S(1)} %pad_clamp_fusion), kind=kCustom, calls=%fused_computation.2 | custom fusion | bytes 3145856 | tf_op jit(solution)/shard_map/jit(_take)/gather | solution.py:218
  20.4 1.4 broadcast_select_fusion
  21.8 11.2 %all-to-all-start = ((bf16[32,32,768]{2,1,0:T(8,128)(2,1)}), bf16[32,32,768]{2,1,0:T(8,128)(2,1)S(1)}, u32[]{:S(2)}, u32[]{:S(2)}) async-start(bf16[32,32,768]{2,1,0:T(8,128)(2,1)} %broadcast_select_fusion), calls=%async_computation | async-start | bytes 3145728 | tf_op jit(solution)/shard_map/all_to_all | solution.py:219
  32.9 1.5 collective-permute-start
  37.3 1.7 scatter_custom_fusion.1
  40.3 4.0 %shard_map.119 = bf16[256,512]{1,0:T(8,128)(2,1)} custom-call(bf16[256,2048]{1,0:T(8,128)(2,1)} %bitcast.54, f32[256,128]{1,0:T(8,128)} %get-tuple-element.49.cos_ref, f32[256,128]{1,0:T(8,128)} %get-tuple-element.50.sin_ref, bf16[2048,256]{1,0:T(8,128)(2,1)} %refs_0_.3, bf16[2048,256]{1,0:T(8,128)(2,1)} %refs_1_.3), custom_call_target="tpu_custom_call" | custom-call | tf_op jit(solution)/shard_map/pallas_call | solution.py:160
  49.2 22.1 %all-to-all-done = bf16[32,32,768]{2,1,0:T(8,128)(2,1)S(1)} async-done(((bf16[32,32,768]{2,1,0:T(8,128)(2,1)}), bf16[32,32,768]{2,1,0:T(8,128)(2,1)S(1)}, u32[]{:S(2)}, u32[]{:S(2)}) %all-to-all-start) | async-done | bytes 1572896 | tf_op jit(solution)/shard_map/all_to_all | solution.py:219
  76.2 6.1 %shard_map.124 = (f32[512,256]{1,0:T(8,128)}, f32[512,256]{1,0:T(8,128)}, f32[512,256]{1,0:T(8,128)}) custom-call(s32[1]{0:T(128)} %constant.85.clone.1.flags_ref, s32[512,1]{1,0:T(8,128)} %broadcast_in_dim.96.qrow_ref, s32[1,1280]{1,0:T(1,128)} %broadcast_in_dim.92.rank_ref, ...), custom_call_target="tpu_custom_call", output_to_operand_aliasing={{0}: (6, {}), {1}: (7, {}), {2}: (8, {})} | custom-call | tf_op jit(solution)/shard_map/pallas_call | solution.py:63
  82.3 7.5 %shard_map.125 = (f32[512,256]{1,0:T(8,128)}, f32[512,256]{1,0:T(8,128)}, f32[512,256]{1,0:T(8,128)}) custom-call(s32[2]{0:T(128)} %compare_convert_fusion.flags_ref, s32[512,1]{1,0:T(8,128)} %broadcast_in_dim.96.qrow_ref, s32[1,2048]{1,0:T(1,128)} %bitcast.59, ...), custom_call_target="tpu_custom_call", output_to_operand_aliasing={{0}: (6, {}), {1}: (7, {}), {2}: (8, {})} | custom-call | tf_op jit(solution)/shard_map/pallas_call | solution.py:63
  89.9 7.2 %collective-permute-done.k_ref.v_ref = bf16[2,2048,256]{2,1,0:T(8,128)(2,1)} collective-permute-done((bf16[2,2048,256]{2,1,0:T(8,128)(2,1)}, bf16[2,2048,256]{2,1,0:T(8,128)(2,1)}, u32[]{:S(2)}, u32[]{:S(2)}) %collective-permute-start) | collective-permute-done | bytes 2097184 | tf_op jit(solution)/shard_map/ppermute | solution.py:181
  97.1 5.1 %shard_map.126 = (f32[512,256]{1,0:T(8,128)}, f32[512,256]{1,0:T(8,128)}, f32[512,256]{1,0:T(8,128)}) custom-call(s32[2]{0:T(128)} %compare_convert_fusion.1.flags_ref, s32[512,1]{1,0:T(8,128)} %broadcast_in_dim.96.qrow_ref, s32[1,2048]{1,0:T(1,128)} %compare_select_fusion.rank_ref, ...), custom_call_target="tpu_custom_call", output_to_operand_aliasing={{0}: (6, {}), {1}: (7, {}), {2}: (8, {})} | custom-call | tf_op jit(solution)/shard_map/pallas_call | solution.py:63
  102.2 3.3 %convert_bitcast_fusion = bf16[8,512,256]{2,1,0:T(8,128)(2,1)} fusion(bf16[32,8,8,256]{3,2,1,0:T(8,128)(2,1)S(1)} %bitcast.64, f32[512,256]{1,0:T(8,128)} %get-tuple-element.35, f32[512,256]{1,0:T(8,128)} %get-tuple-element.36), kind=kOutput, calls=%fused_computation.6 | convolution fusion | flops 538181632 | bytes 4194304 | tf_op jit(solution)/shard_map/qc,ctd->tqd/dot_general | solution.py:280
  105.5 6.4 %all-to-all-start.2 = ((bf16[8,512,256]{2,1,0:T(8,128)(2,1)}), bf16[8,512,256]{2,1,0:T(8,128)(2,1)S(1)}, u32[]{:S(2)}, u32[]{:S(2)}) async-start(bf16[8,512,256]{2,1,0:T(8,128)(2,1)} %convert_bitcast_fusion), calls=%async_computation.2 | async-start | bytes 4194304 | tf_op jit(solution)/shard_map/all_to_all | solution.py:284
  115.3 6.1 %shard_map.120 = (f32[512,256]{1,0:T(8,128)}, f32[512,256]{1,0:T(8,128)}, f32[512,256]{1,0:T(8,128)}) custom-call(s32[1]{0:T(128)} %constant.85.clone.1.flags_ref, s32[512,1]{1,0:T(8,128)} %broadcast_in_dim.95.qrow_ref, s32[1,1280]{1,0:T(1,128)} %broadcast_in_dim.92.rank_ref, ...), custom_call_target="tpu_custom_call", output_to_operand_aliasing={{0}: (6, {}), {1}: (7, {}), {2}: (8, {})} | custom-call | tf_op jit(solution)/shard_map/pallas_call | solution.py:63
  121.4 7.5 %shard_map.121 = (f32[512,256]{1,0:T(8,128)}, f32[512,256]{1,0:T(8,128)}, f32[512,256]{1,0:T(8,128)}) custom-call(s32[2]{0:T(128)} %compare_convert_fusion.flags_ref, s32[512,1]{1,0:T(8,128)} %broadcast_in_dim.95.qrow_ref, s32[1,2048]{1,0:T(1,128)} %bitcast.60, ...), custom_call_target="tpu_custom_call", output_to_operand_aliasing={{0}: (6, {}), {1}: (7, {}), {2}: (8, {})} | custom-call | tf_op jit(solution)/shard_map/pallas_call | solution.py:63
  128.9 5.0 %shard_map.122 = (f32[512,256]{1,0:T(8,128)}, f32[512,256]{1,0:T(8,128)}, f32[512,256]{1,0:T(8,128)}) custom-call(s32[2]{0:T(128)} %compare_convert_fusion.1.flags_ref, s32[512,1]{1,0:T(8,128)} %broadcast_in_dim.95.qrow_ref, s32[1,2048]{1,0:T(1,128)} %compare_select_fusion.rank_ref, ...), custom_call_target="tpu_custom_call", output_to_operand_aliasing={{0}: (6, {}), {1}: (7, {}), {2}: (8, {})} | custom-call | tf_op jit(solution)/shard_map/pallas_call | solution.py:63
  133.9 3.3 %convert_bitcast_fusion.1 = bf16[8,512,256]{2,1,0:T(8,128)(2,1)} fusion(bf16[32,8,8,256]{3,2,1,0:T(8,128)(2,1)S(1)} %bitcast.65, f32[512,256]{1,0:T(8,128)} %get-tuple-element.27, f32[512,256]{1,0:T(8,128)} %get-tuple-element.28), kind=kOutput, calls=%fused_computation.7 | convolution fusion | flops 538181632 | bytes 4194304 | tf_op jit(solution)/shard_map/qc,ctd->tqd/dot_general | solution.py:280
  137.2 6.6 %all-to-all-start.1 = ((bf16[8,512,256]{2,1,0:T(8,128)(2,1)}), bf16[8,512,256]{2,1,0:T(8,128)(2,1)}, u32[]{:S(2)}, u32[]{:S(2)}) async-start(bf16[8,512,256]{2,1,0:T(8,128)(2,1)} %convert_bitcast_fusion.1), calls=%async_computation.1 | async-start | bytes 4194304 | tf_op jit(solution)/shard_map/all_to_all | solution.py:284
  144.9 27.0 %shard_map.127 = bf16[32,16,256]{2,1,0:T(8,128)(2,1)} custom-call(bf16[32,16,256]{2,1,0:T(8,128)(2,1)} %bitcast.56), custom_call_target="tpu_custom_call" | custom-call | tf_op jit(solution)/shard_map/pallas_call | solution.py:113
  172.0 2.7 %reduce_sum.24 = bf16[512,256]{1,0:T(8,128)(2,1)} reduce(bf16[8,512,256]{2,1,0:T(8,128)(2,1)} %all-to-all-done.1, bf16[]{:T(256)} %constant.88.clone.1), dimensions={0}, to_apply=%region_2.3 | reduce | flops 917504 | bytes 2359298 | tf_op jit(solution)/shard_map/reduce_sum | solution.py:287
  174.7 24.7 %shard_map.123 = bf16[32,16,256]{2,1,0:T(8,128)(2,1)} custom-call(bf16[32,16,256]{2,1,0:T(8,128)(2,1)} %bitcast.55), custom_call_target="tpu_custom_call" | custom-call | tf_op jit(solution)/shard_map/pallas_call | solution.py:113
  (63 shorter events, 26.7 us)
Async XLA Ops:
  21.7 12.7 %copy-start = (s32[32]{0:T(128)S(1)}, s32[32]{0:T(128)}, u32[]{:S(2)}) copy-start(s32[32]{0:T(128)} %param.22) | copy-start | bytes 388
  21.7 13.3 %copy-start.1 = (s32[32]{0:T(128)S(1)}, s32[32]{0:T(128)}, u32[]{:S(2)}) copy-start(s32[32]{0:T(128)} %param.21) | copy-start | bytes 388
  21.7 13.9 %copy-start.5 = (s32[1,256]{1,0:T(1,128)S(1)}, s32[1,256]{1,0:T(1,128)}, u32[]{:S(2)}) copy-start(s32[1,256]{1,0:T(1,128)} %param.23) | copy-start | bytes 3076
  21.8 49.5 %all-to-all-start = ((bf16[32,32,768]{2,1,0:T(8,128)(2,1)}), bf16[32,32,768]{2,1,0:T(8,128)(2,1)S(1)}, u32[]{:S(2)}, u32[]{:S(2)}) async-start(bf16[32,32,768]{2,1,0:T(8,128)(2,1)} %broadcast_select_fusion), calls=%async_computation | async-start | bytes 3145728 | tf_op jit(solution)/shard_map/all_to_all | solution.py:219
  32.9 64.2 %collective-permute-start = (bf16[2,2048,256]{2,1,0:T(8,128)(2,1)}, bf16[2,2048,256]{2,1,0:T(8,128)(2,1)}, u32[]{:S(2)}, u32[]{:S(2)}) collective-permute-start(bf16[2,2048,256]{2,1,0:T(8,128)(2,1)} %bitcast.63), channel_id=1, source_target_pairs={{0,128},{8,136},{16,144},{24,152},{32,160},{40,168},{48,176},{56,1... | collective-permute-start | bytes 6291464 | tf_op jit(solution)/shard_map/ppermute | solution.py:181
  71.4 2.4 %copy-start.2 = (bf16[2,32,16,768]{3,2,1,0:T(8,128)(2,1)}, bf16[2,32,16,768]{3,2,1,0:T(8,128)(2,1)S(1)}, u32[]{:S(2)}) copy-start(bf16[2,32,16,768]{3,2,1,0:T(8,128)(2,1)S(1)} %copy.33) | copy-start | bytes 4718596
  71.4 1.1 copy-start.3
  97.1 5.1 %copy-start.6 = (bf16[256,2048]{1,0:T(8,128)(2,1)S(1)}, bf16[256,2048]{1,0:T(8,128)(2,1)}, u32[]{:S(2)}) copy-start(bf16[256,2048]{1,0:T(8,128)(2,1)} %param.16) | copy-start | bytes 3145732
  105.5 31.7 %all-to-all-start.2 = ((bf16[8,512,256]{2,1,0:T(8,128)(2,1)}), bf16[8,512,256]{2,1,0:T(8,128)(2,1)S(1)}, u32[]{:S(2)}, u32[]{:S(2)}) async-start(bf16[8,512,256]{2,1,0:T(8,128)(2,1)} %convert_bitcast_fusion), calls=%async_computation.2 | async-start | bytes 4194304 | tf_op jit(solution)/shard_map/all_to_all | solution.py:284
  137.2 34.8 %all-to-all-start.1 = ((bf16[8,512,256]{2,1,0:T(8,128)(2,1)}), bf16[8,512,256]{2,1,0:T(8,128)(2,1)}, u32[]{:S(2)}, u32[]{:S(2)}) async-start(bf16[8,512,256]{2,1,0:T(8,128)(2,1)} %convert_bitcast_fusion.1), calls=%async_computation.1 | async-start | bytes 4194304 | tf_op jit(solution)/shard_map/all_to_all | solution.py:284
  172.0 27.4 %copy-start.4 = (bf16[32,16,256]{2,1,0:T(8,128)(2,1)S(1)}, bf16[32,16,256]{2,1,0:T(8,128)(2,1)}, u32[]{:S(2)}) copy-start(bf16[32,16,256]{2,1,0:T(8,128)(2,1)} %shard_map.127) | copy-start | bytes 786436

commit v10 on v9

--- a/solution.py
+++ b/solution.py
@@ -241,7 +241,7 @@
     fresh_count = span_len + rec_count
     never = jnp.int32(1 << 30)
     cap = own_cache.shape[2]
-    block_len = 1024
+    block_len = 2048
     key_rows = jnp.arange(cap, dtype=jnp.int32)
     own_rank = jnp.where((key_rows < own_count) & ~replaced, -1, never)[None, :]
     own_flags = (jnp.arange(cap // block_len, dtype=jnp.int32) * block_len < own_count).astype(jnp.int32)

time: 203 us -> 194 us (0.956)
  Pallas kernels: 103 us -> 93.5 us
  other arithmetic: 19.9 us -> 17.5 us
    pallas_call x2, Pallas kernels: 51.8 us -> 47.1 us  [exchange(): pl.pallas_call(functools.partial(exchange_step, axis, count), out_shape=j...]
    pallas_call x6, Pallas kernels: 37.4 us -> 33.1 us  [attend(): pl.pallas_call(flash_step, grid_spec=grid_spec, out_shape=[shape, shape,...]
    convert_element_type x2 -> x0, other arithmetic: 2.41 us -> none  [the longest x1 1.26 us: shards(): (jnp.arange(cap // block_len, dtype=jnp.int32) * block_len < own_count).a...]
  transfers between devices with their start and end apart: 4 -> 4, of which waited for: 2 -> 2; matrix products, arithmetic and copies ran while one was open for 11% -> 10% of each run, Pallas kernels for 31% -> 31%
where the time goes in v10:
time: 194 us; the launch traced here: 193 us
  Pallas kernels  93.5 us (48%)
  waiting for transfers between devices  30.7 us (16%)
  starting transfers between devices  25.7 us (13%)
  local copies, waits for them, and re-layouts  17.8 us (9%)
  other arithmetic  17.5 us (9%)
  matrix products  6.53 us (3%)
    pallas_call x2, Pallas kernels, exchange(): pl.pallas_call(functools.partial(exchange_step, axis, count), out_shape=j...  47.1 us
    pallas_call x6, Pallas kernels, attend(): pl.pallas_call(flash_step, grid_spec=grid_spec, out_shape=[shape, shape,...  33.1 us
    all_to_all x1, waiting for transfers between devices, shards(): lax.all_to_all(arranged, 'grp', split_axis=0, concat_axis=1, tiled=True)[0]  23.1 us
    pallas_call x2, Pallas kernels, project(): pl.pallas_call(functools.partial(project_step, tuple(turned)), grid=(coun...  13.4 us
    all_to_all x2, starting transfers between devices, shards(): lax.all_to_all(partial_value, 'tp', split_axis=0, concat_axis=0, tiled=True)  13 us
    all_to_all x1, starting transfers between devices, shards(): lax.all_to_all(arranged, 'grp', split_axis=0, concat_axis=1, tiled=True)[0]  11.2 us
    ppermute x1, waiting for transfers between devices, swapped(): return lax.ppermute(value, axis, pairs)  7.54 us
    dot_general x2, matrix products, shards(): jnp.einsum('qc,ctd->tqd', attended, out_by_block, preferred_element_type=...  6.53 us
  transfers between devices with their start and end apart: 4, of which 2 were waited for; matrix products, arithmetic and copies ran while one was open for 10% of the time, Pallas kernels for 31%

profile of v10, /device:TPU:1, one launch (start us, length us, event | category | flops | bytes accessed | tf_op | source)
XLA Modules:
  0.0 193.2 jit_solution(10178070593842418247)
XLA Ops:
  3.4 1.4 gather_fusion
  4.9 1.9 fusion.6
  8.9 9.4 %shard_map.118 = bf16[1024,768]{1,0:T(8,128)(2,1)} custom-call(bf16[1024,2048]{1,0:T(8,128)(2,1)} %bitcast.52, f32[1024,128]{1,0:T(8,128)} %pad_maximum_fusion.1.cos_ref, f32[1024,128]{1,0:T(8,128)} %pad_maximum_fusion.2.sin_ref, bf16[2048,256]{1,0:T(8,128)(2,1)} %refs_0_.2, bf16[2048,256]{1,0:T(8,128)(2,1)} %refs_0_.3, bf16[2048,256]{1,0:T(8,128)(2,1)} %refs_1_.3), custom_call_target="tpu_custom_call" | custom-call | tf_op jit(solution)/shard_map/pallas_call | solution.py:160
  18.3 2.1 %gather_fusion.2 = bf16[32,32,768]{2,1,0:T(8,128)(2,1)S(1)} fusion(bf16[32,32,768]{2,1,0:T(8,128)(2,1)} %bitcast.51, s32[1024]{0:T(1024)S(1)} %pad_clamp_fusion), kind=kCustom, calls=%fused_computation.2 | custom fusion | bytes 3145856 | tf_op jit(solution)/shard_map/jit(_take)/gather | solution.py:218
  20.4 1.4 broadcast_select_fusion
  21.8 11.2 %all-to-all-start = ((bf16[32,32,768]{2,1,0:T(8,128)(2,1)}), bf16[32,32,768]{2,1,0:T(8,128)(2,1)S(1)}, u32[]{:S(2)}, u32[]{:S(2)}) async-start(bf16[32,32,768]{2,1,0:T(8,128)(2,1)} %broadcast_select_fusion), calls=%async_computation | async-start | bytes 3145728 | tf_op jit(solution)/shard_map/all_to_all | solution.py:219
  32.9 1.5 collective-permute-start
  38.6 1.7 scatter_custom_fusion.1
  41.7 4.0 %shard_map.119 = bf16[256,512]{1,0:T(8,128)(2,1)} custom-call(bf16[256,2048]{1,0:T(8,128)(2,1)} %bitcast.54, f32[256,128]{1,0:T(8,128)} %get-tuple-element.49.cos_ref, f32[256,128]{1,0:T(8,128)} %get-tuple-element.50.sin_ref, bf16[2048,256]{1,0:T(8,128)(2,1)} %refs_0_.3, bf16[2048,256]{1,0:T(8,128)(2,1)} %refs_1_.3), custom_call_target="tpu_custom_call" | custom-call | tf_op jit(solution)/shard_map/pallas_call | solution.py:160
  48.1 23.1 %all-to-all-done = bf16[32,32,768]{2,1,0:T(8,128)(2,1)S(1)} async-done(((bf16[32,32,768]{2,1,0:T(8,128)(2,1)}), bf16[32,32,768]{2,1,0:T(8,128)(2,1)S(1)}, u32[]{:S(2)}, u32[]{:S(2)}) %all-to-all-start) | async-done | bytes 1572896 | tf_op jit(solution)/shard_map/all_to_all | solution.py:219
  76.2 6.1 %shard_map.124 = (f32[512,256]{1,0:T(8,128)}, f32[512,256]{1,0:T(8,128)}, f32[512,256]{1,0:T(8,128)}) custom-call(s32[1]{0:T(128)} %constant.85.clone.1.flags_ref, s32[512,1]{1,0:T(8,128)} %broadcast_in_dim.96.qrow_ref, s32[1,1280]{1,0:T(1,128)} %broadcast_in_dim.92.rank_ref, ...), custom_call_target="tpu_custom_call", output_to_operand_aliasing={{0}: (6, {}), {1}: (7, {}), {2}: (8, {})} | custom-call | tf_op jit(solution)/shard_map/pallas_call | solution.py:63
  82.3 7.2 %shard_map.125 = (f32[512,256]{1,0:T(8,128)}, f32[512,256]{1,0:T(8,128)}, f32[512,256]{1,0:T(8,128)}) custom-call(s32[1]{0:T(128)S(6)} %convert_element_type.51.flags_ref, s32[512,1]{1,0:T(8,128)} %broadcast_in_dim.96.qrow_ref, s32[1,2048]{1,0:T(1,128)} %bitcast.59, ...), custom_call_target="tpu_custom_call", output_to_operand_aliasing={{0}: (6, {}), {1}: (7, {}), {2}: (8, {})} | custom-call | tf_op jit(solution)/shard_map/pallas_call | solution.py:63
  89.6 7.5 %collective-permute-done.k_ref.v_ref = bf16[2,2048,256]{2,1,0:T(8,128)(2,1)} collective-permute-done((bf16[2,2048,256]{2,1,0:T(8,128)(2,1)}, bf16[2,2048,256]{2,1,0:T(8,128)(2,1)}, u32[]{:S(2)}, u32[]{:S(2)}) %collective-permute-start) | collective-permute-done | bytes 2097184 | tf_op jit(solution)/shard_map/ppermute | solution.py:181
  97.1 3.2 %shard_map.126 = (f32[512,256]{1,0:T(8,128)}, f32[512,256]{1,0:T(8,128)}, f32[512,256]{1,0:T(8,128)}) custom-call(s32[1]{0:T(128)S(6)} %convert_element_type.48.flags_ref, s32[512,1]{1,0:T(8,128)} %broadcast_in_dim.96.qrow_ref, s32[1,2048]{1,0:T(1,128)} %compare_select_fusion.rank_ref, ...), custom_call_target="tpu_custom_call", output_to_operand_aliasing={{0}: (6, {}), {1}: (7, {}), {2}: (8, {})} | custom-call | tf_op jit(solution)/shard_map/pallas_call | solution.py:63
  100.3 3.3 %convert_bitcast_fusion = bf16[8,512,256]{2,1,0:T(8,128)(2,1)} fusion(bf16[32,8,8,256]{3,2,1,0:T(8,128)(2,1)S(1)} %bitcast.64, f32[512,256]{1,0:T(8,128)} %get-tuple-element.35, f32[512,256]{1,0:T(8,128)} %get-tuple-element.36), kind=kOutput, calls=%fused_computation.6 | convolution fusion | flops 538181632 | bytes 4194304 | tf_op jit(solution)/shard_map/qc,ctd->tqd/dot_general | solution.py:280
  103.6 6.4 %all-to-all-start.2 = ((bf16[8,512,256]{2,1,0:T(8,128)(2,1)}), bf16[8,512,256]{2,1,0:T(8,128)(2,1)S(1)}, u32[]{:S(2)}, u32[]{:S(2)}) async-start(bf16[8,512,256]{2,1,0:T(8,128)(2,1)} %convert_bitcast_fusion), calls=%async_computation.2 | async-start | bytes 4194304 | tf_op jit(solution)/shard_map/all_to_all | solution.py:284
  113.4 6.1 %shard_map.120 = (f32[512,256]{1,0:T(8,128)}, f32[512,256]{1,0:T(8,128)}, f32[512,256]{1,0:T(8,128)}) custom-call(s32[1]{0:T(128)} %constant.85.clone.1.flags_ref, s32[512,1]{1,0:T(8,128)} %broadcast_in_dim.95.qrow_ref, s32[1,1280]{1,0:T(1,128)} %broadcast_in_dim.92.rank_ref, ...), custom_call_target="tpu_custom_call", output_to_operand_aliasing={{0}: (6, {}), {1}: (7, {}), {2}: (8, {})} | custom-call | tf_op jit(solution)/shard_map/pallas_call | solution.py:63
  119.5 7.3 %shard_map.121 = (f32[512,256]{1,0:T(8,128)}, f32[512,256]{1,0:T(8,128)}, f32[512,256]{1,0:T(8,128)}) custom-call(s32[1]{0:T(128)S(6)} %convert_element_type.51.flags_ref, s32[512,1]{1,0:T(8,128)} %broadcast_in_dim.95.qrow_ref, s32[1,2048]{1,0:T(1,128)} %bitcast.60, ...), custom_call_target="tpu_custom_call", output_to_operand_aliasing={{0}: (6, {}), {1}: (7, {}), {2}: (8, {})} | custom-call | tf_op jit(solution)/shard_map/pallas_call | solution.py:63
  126.8 3.1 %shard_map.122 = (f32[512,256]{1,0:T(8,128)}, f32[512,256]{1,0:T(8,128)}, f32[512,256]{1,0:T(8,128)}) custom-call(s32[1]{0:T(128)S(6)} %convert_element_type.48.flags_ref, s32[512,1]{1,0:T(8,128)} %broadcast_in_dim.95.qrow_ref, s32[1,2048]{1,0:T(1,128)} %compare_select_fusion.rank_ref, ...), custom_call_target="tpu_custom_call", output_to_operand_aliasing={{0}: (6, {}), {1}: (7, {}), {2}: (8, {})} | custom-call | tf_op jit(solution)/shard_map/pallas_call | solution.py:63
  129.9 3.3 %convert_bitcast_fusion.1 = bf16[8,512,256]{2,1,0:T(8,128)(2,1)} fusion(bf16[32,8,8,256]{3,2,1,0:T(8,128)(2,1)S(1)} %bitcast.65, f32[512,256]{1,0:T(8,128)} %get-tuple-element.27, f32[512,256]{1,0:T(8,128)} %get-tuple-element.28), kind=kOutput, calls=%fused_computation.7 | convolution fusion | flops 538181632 | bytes 4194304 | tf_op jit(solution)/shard_map/qc,ctd->tqd/dot_general | solution.py:280
  133.2 6.6 %all-to-all-start.1 = ((bf16[8,512,256]{2,1,0:T(8,128)(2,1)}), bf16[8,512,256]{2,1,0:T(8,128)(2,1)}, u32[]{:S(2)}, u32[]{:S(2)}) async-start(bf16[8,512,256]{2,1,0:T(8,128)(2,1)} %convert_bitcast_fusion.1), calls=%async_computation.1 | async-start | bytes 4194304 | tf_op jit(solution)/shard_map/all_to_all | solution.py:284
  140.9 26.1 %shard_map.127 = bf16[32,16,256]{2,1,0:T(8,128)(2,1)} custom-call(bf16[32,16,256]{2,1,0:T(8,128)(2,1)} %bitcast.56), custom_call_target="tpu_custom_call" | custom-call | tf_op jit(solution)/shard_map/pallas_call | solution.py:113
  167.0 2.7 %reduce_sum.24 = bf16[512,256]{1,0:T(8,128)(2,1)} reduce(bf16[8,512,256]{2,1,0:T(8,128)(2,1)} %all-to-all-done.1, bf16[]{:T(256)} %constant.88.clone.1), dimensions={0}, to_apply=%region_2.3 | reduce | flops 917504 | bytes 2359298 | tf_op jit(solution)/shard_map/reduce_sum | solution.py:287
  169.7 21.0 %shard_map.123 = bf16[32,16,256]{2,1,0:T(8,128)(2,1)} custom-call(bf16[32,16,256]{2,1,0:T(8,128)(2,1)} %bitcast.55), custom_call_target="tpu_custom_call" | custom-call | tf_op jit(solution)/shard_map/pallas_call | solution.py:113
  (61 shorter events, 24.3 us)
Async XLA Ops:
  21.7 12.7 %copy-start = (s32[32]{0:T(128)S(1)}, s32[32]{0:T(128)}, u32[]{:S(2)}) copy-start(s32[32]{0:T(128)} %param.22) | copy-start | bytes 388
  21.7 13.9 %copy-start.1 = (s32[32]{0:T(128)S(1)}, s32[32]{0:T(128)}, u32[]{:S(2)}) copy-start(s32[32]{0:T(128)} %param.21) | copy-start | bytes 388
  21.7 15.3 %copy-start.5 = (s32[1,256]{1,0:T(1,128)S(1)}, s32[1,256]{1,0:T(1,128)}, u32[]{:S(2)}) copy-start(s32[1,256]{1,0:T(1,128)} %param.23) | copy-start | bytes 3076
  21.8 49.5 %all-to-all-start = ((bf16[32,32,768]{2,1,0:T(8,128)(2,1)}), bf16[32,32,768]{2,1,0:T(8,128)(2,1)S(1)}, u32[]{:S(2)}, u32[]{:S(2)}) async-start(bf16[32,32,768]{2,1,0:T(8,128)(2,1)} %broadcast_select_fusion), calls=%async_computation | async-start | bytes 3145728 | tf_op jit(solution)/shard_map/all_to_all | solution.py:219
  32.9 64.2 %collective-permute-start = (bf16[2,2048,256]{2,1,0:T(8,128)(2,1)}, bf16[2,2048,256]{2,1,0:T(8,128)(2,1)}, u32[]{:S(2)}, u32[]{:S(2)}) collective-permute-start(bf16[2,2048,256]{2,1,0:T(8,128)(2,1)} %bitcast.63), channel_id=1, source_target_pairs={{0,128},{8,136},{16,144},{24,152},{32,160},{40,168},{48,176},{56,1... | collective-permute-start | bytes 6291464 | tf_op jit(solution)/shard_map/ppermute | solution.py:181
  71.4 2.4 %copy-start.2 = (bf16[2,32,16,768]{3,2,1,0:T(8,128)(2,1)}, bf16[2,32,16,768]{3,2,1,0:T(8,128)(2,1)S(1)}, u32[]{:S(2)}) copy-start(bf16[2,32,16,768]{3,2,1,0:T(8,128)(2,1)S(1)} %copy.33) | copy-start | bytes 4718596
  71.4 1.1 copy-start.3
  97.1 3.2 %copy-start.6 = (bf16[256,2048]{1,0:T(8,128)(2,1)S(1)}, bf16[256,2048]{1,0:T(8,128)(2,1)}, u32[]{:S(2)}) copy-start(bf16[256,2048]{1,0:T(8,128)(2,1)} %param.16) | copy-start | bytes 3145732
  103.6 29.6 %all-to-all-start.2 = ((bf16[8,512,256]{2,1,0:T(8,128)(2,1)}), bf16[8,512,256]{2,1,0:T(8,128)(2,1)S(1)}, u32[]{:S(2)}, u32[]{:S(2)}) async-start(bf16[8,512,256]{2,1,0:T(8,128)(2,1)} %convert_bitcast_fusion), calls=%async_computation.2 | async-start | bytes 4194304 | tf_op jit(solution)/shard_map/all_to_all | solution.py:284
  133.2 33.8 %all-to-all-start.1 = ((bf16[8,512,256]{2,1,0:T(8,128)(2,1)}), bf16[8,512,256]{2,1,0:T(8,128)(2,1)}, u32[]{:S(2)}, u32[]{:S(2)}) async-start(bf16[8,512,256]{2,1,0:T(8,128)(2,1)} %convert_bitcast_fusion.1), calls=%async_computation.1 | async-start | bytes 4194304 | tf_op jit(solution)/shard_map/all_to_all | solution.py:284
  167.0 23.7 %copy-start.4 = (bf16[32,16,256]{2,1,0:T(8,128)(2,1)S(1)}, bf16[32,16,256]{2,1,0:T(8,128)(2,1)}, u32[]{:S(2)}) copy-start(bf16[32,16,256]{2,1,0:T(8,128)(2,1)} %shard_map.127) | copy-start | bytes 786436

commit v11 on v10

--- a/solution.py
+++ b/solution.py
@@ -147,10 +147,10 @@
 def rope_tables(positions):
     half_dim = HEAD_DIM // 2
     frequency = jnp.exp(-jnp.log(rope_base) * jnp.arange(half_dim, dtype=jnp.float32) / half_dim)
-    angles = positions.astype(jnp.float32)[:, None] * frequency[None, :]
-    cosine = jnp.cos(angles)
-    sine = jnp.sin(angles)
-    return jnp.concatenate([cosine, cosine], axis=1), jnp.concatenate([-sine, sine], axis=1)
+    doubled = jnp.concatenate([frequency, frequency])
+    sign = jnp.concatenate([-jnp.ones((half_dim,), jnp.float32), jnp.ones((half_dim,), jnp.float32)])
+    angles = positions.astype(jnp.float32)[:, None] * doubled[None, :]
+    return jnp.cos(angles), jnp.sin(angles) * sign[None, :]
 
 
 def project(rows, positions, weights, turned, block_rows):
@@ -206,7 +206,9 @@
     fetched = swapped(guest_cache[0], "grp", swap_bit)
 
     server = jnp.zeros_like(deal_order).at[deal_order].set(jnp.arange(groups, dtype=jnp.int32))
-    start_of = own_len[server] + guest_len[(server + groups // 2) % groups]
+    start_of = jnp.zeros_like(deal_order).at[deal_order].set(
+        own_len + jnp.roll(guest_len, -(groups // 2))
+    )
     local_positions = (
         start_of[:, None] + group_id * local_rows + jnp.arange(local_rows, dtype=jnp.int32)[None, :]
     ).reshape(-1)

time: 194 us -> 196 us (1.010)
  Pallas kernels: 93.5 us -> 97.9 us
    mul x0 -> x2, other arithmetic: none -> 4.93 us  [rope_tables(): return (jnp.cos(angles), jnp.sin(angles) * sign[None, :])]
    pallas_call x2, Pallas kernels: 47.1 us -> 51.5 us  [exchange(): pl.pallas_call(functools.partial(exchange_step, axis, count), out_shape=j...]
    concatenate x3 -> x1, other arithmetic: 2.86 us -> 0.07 us  [rope_tables(): doubled = jnp.concatenate([frequency, frequency])]
    gather x2 -> x0, local copies, waits for them, and re-layouts: 2.72 us -> none  [shards(): start_of = own_len[server] + guest_len[(server + groups // 2) % groups]]
    neg x2 -> x0, other arithmetic: 2.45 us -> none  [rope_tables(): -sine]
  transfers between devices with their start and end apart: 4 -> 4, of which waited for: 2 -> 3; matrix products, arithmetic and copies ran while one was open for 10% -> 10% of each run, Pallas kernels for 31% -> 30%
where the time goes in v11:
time: 196 us
  Pallas kernels  97.9 us (50%)
  waiting for transfers between devices  31.2 us (16%)
  starting transfers between devices  25.6 us (13%)
  other arithmetic  17.1 us (9%)
  local copies, waits for them, and re-layouts  16.5 us (8%)
  matrix products  6.53 us (3%)
    pallas_call x2, Pallas kernels, exchange(): pl.pallas_call(functools.partial(exchange_step, axis, count), out_shape=j...  51.5 us
    pallas_call x6, Pallas kernels, attend(): pl.pallas_call(flash_step, grid_spec=grid_spec, out_shape=[shape, shape,...  33 us
    all_to_all x1, waiting for transfers between devices, shards(): lax.all_to_all(arranged, 'grp', split_axis=0, concat_axis=1, tiled=True)[0]  23.6 us
    pallas_call x2, Pallas kernels, project(): pl.pallas_call(functools.partial(project_step, tuple(turned)), grid=(coun...  13.4 us
    all_to_all x2, starting transfers between devices, shards(): lax.all_to_all(partial_value, 'tp', split_axis=0, concat_axis=0, tiled=True)  12.9 us
    all_to_all x1, starting transfers between devices, shards(): lax.all_to_all(arranged, 'grp', split_axis=0, concat_axis=1, tiled=True)[0]  11.2 us
    ppermute x1, waiting for transfers between devices, swapped(): return lax.ppermute(value, axis, pairs)  7.57 us
    dot_general x2, matrix products, shards(): jnp.einsum('qc,ctd->tqd', attended, out_by_block, preferred_element_type=...  6.53 us
  transfers between devices with their start and end apart: 4, of which 3 were waited for; matrix products, arithmetic and copies ran while one was open for 10% of the time, Pallas kernels for 30%

profile of v11, /device:TPU:1, one launch (start us, length us, event | category | flops | bytes accessed | tf_op | source)
XLA Modules:
  0.0 196.3 jit_solution(17111377164140612546)
XLA Ops:
  3.2 3.7 %fusion.4 = (f32[1024,128]{1,0:T(8,128)}, f32[1024,128]{1,0:T(8,128)}) fusion(f32[128]{0:T(128)} %constant.74.clone.1, f32[128]{0:T(128)S(1)} %pad_maximum_fusion.2, f32[1024]{0:T(1024)S(1)} %convert_element_type.50), kind=kLoop, calls=%fused_computation.15 | loop fusion | flops 262144 | bytes 1053696 | tf_op jit(solution)/shard_map/mul | solution.py:153
  6.9 9.4 %shard_map.118 = bf16[1024,768]{1,0:T(8,128)(2,1)} custom-call(bf16[1024,2048]{1,0:T(8,128)(2,1)} %bitcast.53, f32[1024,128]{1,0:T(8,128)} %get-tuple-element.40.cos_ref, f32[1024,128]{1,0:T(8,128)} %get-tuple-element.39.sin_ref, bf16[2048,256]{1,0:T(8,128)(2,1)} %refs_0_.2, bf16[2048,256]{1,0:T(8,128)(2,1)} %refs_0_.3, bf16[2048,256]{1,0:T(8,128)(2,1)} %refs_1_.3), custom_call_target="tpu_custom_call" | custom-call | tf_op jit(solution)/shard_map/pallas_call | solution.py:160
  16.3 2.1 %gather_fusion = bf16[32,32,768]{2,1,0:T(8,128)(2,1)S(1)} fusion(bf16[32,32,768]{2,1,0:T(8,128)(2,1)} %bitcast.52, s32[1024]{0:T(1024)S(1)} %pad_clamp_fusion.1), kind=kCustom, calls=%fused_computation | custom fusion | bytes 3145856 | tf_op jit(solution)/shard_map/jit(_take)/gather | solution.py:220
  18.3 1.4 broadcast_select_fusion
  19.7 11.2 %all-to-all-start = ((bf16[32,32,768]{2,1,0:T(8,128)(2,1)}), bf16[32,32,768]{2,1,0:T(8,128)(2,1)S(1)}, u32[]{:S(2)}, u32[]{:S(2)}) async-start(bf16[32,32,768]{2,1,0:T(8,128)(2,1)} %broadcast_select_fusion), calls=%async_computation | async-start | bytes 3145728 | tf_op jit(solution)/shard_map/all_to_all | solution.py:221
  30.9 1.5 collective-permute-start
  36.4 1.7 scatter_custom_fusion.2
  39.3 4.0 %shard_map.119 = bf16[256,512]{1,0:T(8,128)(2,1)} custom-call(bf16[256,2048]{1,0:T(8,128)(2,1)} %bitcast.55, f32[256,128]{1,0:T(8,128)} %get-tuple-element.42.cos_ref, f32[256,128]{1,0:T(8,128)} %get-tuple-element.41.sin_ref, bf16[2048,256]{1,0:T(8,128)(2,1)} %refs_0_.3, bf16[2048,256]{1,0:T(8,128)(2,1)} %refs_1_.3), custom_call_target="tpu_custom_call" | custom-call | tf_op jit(solution)/shard_map/pallas_call | solution.py:160
  43.3 1.2 compare_select_fusion.rank_ref
  45.7 23.6 %all-to-all-done = bf16[32,32,768]{2,1,0:T(8,128)(2,1)S(1)} async-done(((bf16[32,32,768]{2,1,0:T(8,128)(2,1)}), bf16[32,32,768]{2,1,0:T(8,128)(2,1)S(1)}, u32[]{:S(2)}, u32[]{:S(2)}) %all-to-all-start) | async-done | bytes 1572896 | tf_op jit(solution)/shard_map/all_to_all | solution.py:221
  74.2 6.1 %shard_map.124 = (f32[512,256]{1,0:T(8,128)}, f32[512,256]{1,0:T(8,128)}, f32[512,256]{1,0:T(8,128)}) custom-call(s32[1]{0:T(128)} %constant.79.clone.1.flags_ref, s32[512,1]{1,0:T(8,128)} %broadcast_in_dim.92.qrow_ref, s32[1,1280]{1,0:T(1,128)} %broadcast_in_dim.87.rank_ref, ...), custom_call_target="tpu_custom_call", output_to_operand_aliasing={{0}: (6, {}), {1}: (7, {}), {2}: (8, {})} | custom-call | tf_op jit(solution)/shard_map/pallas_call | solution.py:63
  80.3 7.2 %shard_map.125 = (f32[512,256]{1,0:T(8,128)}, f32[512,256]{1,0:T(8,128)}, f32[512,256]{1,0:T(8,128)}) custom-call(s32[1]{0:T(128)S(6)} %convert_element_type.51.flags_ref, s32[512,1]{1,0:T(8,128)} %broadcast_in_dim.92.qrow_ref, s32[1,2048]{1,0:T(1,128)} %bitcast.60, ...), custom_call_target="tpu_custom_call", output_to_operand_aliasing={{0}: (6, {}), {1}: (7, {}), {2}: (8, {})} | custom-call | tf_op jit(solution)/shard_map/pallas_call | solution.py:63
  87.5 7.6 %collective-permute-done.k_ref.v_ref = bf16[2,2048,256]{2,1,0:T(8,128)(2,1)} collective-permute-done((bf16[2,2048,256]{2,1,0:T(8,128)(2,1)}, bf16[2,2048,256]{2,1,0:T(8,128)(2,1)}, u32[]{:S(2)}, u32[]{:S(2)}) %collective-permute-start) | collective-permute-done | bytes 2097184 | tf_op jit(solution)/shard_map/ppermute | solution.py:181
  95.1 3.2 %shard_map.126 = (f32[512,256]{1,0:T(8,128)}, f32[512,256]{1,0:T(8,128)}, f32[512,256]{1,0:T(8,128)}) custom-call(s32[1]{0:T(128)S(6)} %convert_element_type.48.flags_ref, s32[512,1]{1,0:T(8,128)} %broadcast_in_dim.92.qrow_ref, s32[1,2048]{1,0:T(1,128)} %compare_select_fusion.rank_ref, ...), custom_call_target="tpu_custom_call", output_to_operand_aliasing={{0}: (6, {}), {1}: (7, {}), {2}: (8, {})} | custom-call | tf_op jit(solution)/shard_map/pallas_call | solution.py:63
  98.3 3.3 %convert_bitcast_fusion = bf16[8,512,256]{2,1,0:T(8,128)(2,1)} fusion(bf16[32,8,8,256]{3,2,1,0:T(8,128)(2,1)S(1)} %bitcast.65, f32[512,256]{1,0:T(8,128)} %get-tuple-element.35, f32[512,256]{1,0:T(8,128)} %get-tuple-element.36), kind=kOutput, calls=%fused_computation.5 | convolution fusion | flops 538181632 | bytes 4194304 | tf_op jit(solution)/shard_map/qc,ctd->tqd/dot_general | solution.py:282
  101.6 6.3 %all-to-all-start.2 = ((bf16[8,512,256]{2,1,0:T(8,128)(2,1)}), bf16[8,512,256]{2,1,0:T(8,128)(2,1)S(1)}, u32[]{:S(2)}, u32[]{:S(2)}) async-start(bf16[8,512,256]{2,1,0:T(8,128)(2,1)} %convert_bitcast_fusion), calls=%async_computation.2 | async-start | bytes 4194304 | tf_op jit(solution)/shard_map/all_to_all | solution.py:286
  111.3 6.1 %shard_map.120 = (f32[512,256]{1,0:T(8,128)}, f32[512,256]{1,0:T(8,128)}, f32[512,256]{1,0:T(8,128)}) custom-call(s32[1]{0:T(128)} %constant.79.clone.1.flags_ref, s32[512,1]{1,0:T(8,128)} %broadcast_in_dim.91.qrow_ref, s32[1,1280]{1,0:T(1,128)} %broadcast_in_dim.87.rank_ref, ...), custom_call_target="tpu_custom_call", output_to_operand_aliasing={{0}: (6, {}), {1}: (7, {}), {2}: (8, {})} | custom-call | tf_op jit(solution)/shard_map/pallas_call | solution.py:63
  117.4 7.3 %shard_map.121 = (f32[512,256]{1,0:T(8,128)}, f32[512,256]{1,0:T(8,128)}, f32[512,256]{1,0:T(8,128)}) custom-call(s32[1]{0:T(128)S(6)} %convert_element_type.51.flags_ref, s32[512,1]{1,0:T(8,128)} %broadcast_in_dim.91.qrow_ref, s32[1,2048]{1,0:T(1,128)} %bitcast.61, ...), custom_call_target="tpu_custom_call", output_to_operand_aliasing={{0}: (6, {}), {1}: (7, {}), {2}: (8, {})} | custom-call | tf_op jit(solution)/shard_map/pallas_call | solution.py:63
  124.7 3.1 %shard_map.122 = (f32[512,256]{1,0:T(8,128)}, f32[512,256]{1,0:T(8,128)}, f32[512,256]{1,0:T(8,128)}) custom-call(s32[1]{0:T(128)S(6)} %convert_element_type.48.flags_ref, s32[512,1]{1,0:T(8,128)} %broadcast_in_dim.91.qrow_ref, s32[1,2048]{1,0:T(1,128)} %compare_select_fusion.rank_ref, ...), custom_call_target="tpu_custom_call", output_to_operand_aliasing={{0}: (6, {}), {1}: (7, {}), {2}: (8, {})} | custom-call | tf_op jit(solution)/shard_map/pallas_call | solution.py:63
  127.8 3.3 %convert_bitcast_fusion.1 = bf16[8,512,256]{2,1,0:T(8,128)(2,1)} fusion(bf16[32,8,8,256]{3,2,1,0:T(8,128)(2,1)S(1)} %bitcast.66, f32[512,256]{1,0:T(8,128)} %get-tuple-element.27, f32[512,256]{1,0:T(8,128)} %get-tuple-element.28), kind=kOutput, calls=%fused_computation.6 | convolution fusion | flops 538181632 | bytes 4194304 | tf_op jit(solution)/shard_map/qc,ctd->tqd/dot_general | solution.py:282
  131.1 6.6 %all-to-all-start.1 = ((bf16[8,512,256]{2,1,0:T(8,128)(2,1)}), bf16[8,512,256]{2,1,0:T(8,128)(2,1)}, u32[]{:S(2)}, u32[]{:S(2)}) async-start(bf16[8,512,256]{2,1,0:T(8,128)(2,1)} %convert_bitcast_fusion.1), calls=%async_computation.1 | async-start | bytes 4194304 | tf_op jit(solution)/shard_map/all_to_all | solution.py:286
  139.5 25.3 %shard_map.127 = bf16[32,16,256]{2,1,0:T(8,128)(2,1)} custom-call(bf16[32,16,256]{2,1,0:T(8,128)(2,1)} %bitcast.57), custom_call_target="tpu_custom_call" | custom-call | tf_op jit(solution)/shard_map/pallas_call | solution.py:113
  164.9 2.7 %reduce_sum.24 = bf16[512,256]{1,0:T(8,128)(2,1)} reduce(bf16[8,512,256]{2,1,0:T(8,128)(2,1)} %all-to-all-done.1, bf16[]{:T(256)} %constant.82.clone.1), dimensions={0}, to_apply=%region_3.4 | reduce | flops 917504 | bytes 2359298 | tf_op jit(solution)/shard_map/reduce_sum | solution.py:289
  167.5 26.2 %shard_map.123 = bf16[32,16,256]{2,1,0:T(8,128)(2,1)} custom-call(bf16[32,16,256]{2,1,0:T(8,128)(2,1)} %bitcast.56), custom_call_target="tpu_custom_call" | custom-call | tf_op jit(solution)/shard_map/pallas_call | solution.py:113
  (61 shorter events, 21.0 us)
Async XLA Ops:
  19.7 12.7 %copy-start.5 = (s32[32]{0:T(128)S(1)}, s32[32]{0:T(128)}, u32[]{:S(2)}) copy-start(s32[32]{0:T(128)} %param.22) | copy-start | bytes 388
  19.7 13.9 %copy-start.6 = (s32[32]{0:T(128)S(1)}, s32[32]{0:T(128)}, u32[]{:S(2)}) copy-start(s32[32]{0:T(128)} %param.21) | copy-start | bytes 388
  19.7 15.1 %copy-start.3 = (s32[1,256]{1,0:T(1,128)S(1)}, s32[1,256]{1,0:T(1,128)}, u32[]{:S(2)}) copy-start(s32[1,256]{1,0:T(1,128)} %param.23) | copy-start | bytes 3076
  19.7 18.4 %copy-start.4 = (f32[128]{0:T(128)S(1)}, f32[128]{0:T(128)}, u32[]{:S(2)}) copy-start(f32[128]{0:T(128)} %constant.74.clone.1) | copy-start | bytes 1540
  19.7 49.5 %all-to-all-start = ((bf16[32,32,768]{2,1,0:T(8,128)(2,1)}), bf16[32,32,768]{2,1,0:T(8,128)(2,1)S(1)}, u32[]{:S(2)}, u32[]{:S(2)}) async-start(bf16[32,32,768]{2,1,0:T(8,128)(2,1)} %broadcast_select_fusion), calls=%async_computation | async-start | bytes 3145728 | tf_op jit(solution)/shard_map/all_to_all | solution.py:221
  30.9 64.2 %collective-permute-start = (bf16[2,2048,256]{2,1,0:T(8,128)(2,1)}, bf16[2,2048,256]{2,1,0:T(8,128)(2,1)}, u32[]{:S(2)}, u32[]{:S(2)}) collective-permute-start(bf16[2,2048,256]{2,1,0:T(8,128)(2,1)} %bitcast.64), channel_id=1, source_target_pairs={{0,128},{8,136},{16,144},{24,152},{32,160},{40,168},{48,176},{56,1... | collective-permute-start | bytes 6291464 | tf_op jit(solution)/shard_map/ppermute | solution.py:181
  69.4 2.3 %copy-start = (bf16[2,32,16,768]{3,2,1,0:T(8,128)(2,1)}, bf16[2,32,16,768]{3,2,1,0:T(8,128)(2,1)S(1)}, u32[]{:S(2)}) copy-start(bf16[2,32,16,768]{3,2,1,0:T(8,128)(2,1)S(1)} %copy.33) | copy-start | bytes 4718596
  69.4 1.1 copy-start.1
  95.1 3.2 %copy-start.7 = (bf16[256,2048]{1,0:T(8,128)(2,1)S(1)}, bf16[256,2048]{1,0:T(8,128)(2,1)}, u32[]{:S(2)}) copy-start(bf16[256,2048]{1,0:T(8,128)(2,1)} %param.16) | copy-start | bytes 3145732
  101.6 29.6 %all-to-all-start.2 = ((bf16[8,512,256]{2,1,0:T(8,128)(2,1)}), bf16[8,512,256]{2,1,0:T(8,128)(2,1)S(1)}, u32[]{:S(2)}, u32[]{:S(2)}) async-start(bf16[8,512,256]{2,1,0:T(8,128)(2,1)} %convert_bitcast_fusion), calls=%async_computation.2 | async-start | bytes 4194304 | tf_op jit(solution)/shard_map/all_to_all | solution.py:286
  131.1 33.7 %all-to-all-start.1 = ((bf16[8,512,256]{2,1,0:T(8,128)(2,1)}), bf16[8,512,256]{2,1,0:T(8,128)(2,1)}, u32[]{:S(2)}, u32[]{:S(2)}) async-start(bf16[8,512,256]{2,1,0:T(8,128)(2,1)} %convert_bitcast_fusion.1), calls=%async_computation.1 | async-start | bytes 4194304 | tf_op jit(solution)/shard_map/all_to_all | solution.py:286
  164.8 28.9 %copy-start.2 = (bf16[32,16,256]{2,1,0:T(8,128)(2,1)S(1)}, bf16[32,16,256]{2,1,0:T(8,128)(2,1)}, u32[]{:S(2)}) copy-start(bf16[32,16,256]{2,1,0:T(8,128)(2,1)} %shard_map.127) | copy-start | bytes 786436

commit v12 on v11

--- a/solution.py
+++ b/solution.py
@@ -124,8 +124,11 @@
     )(blocks)
 
 
-def project_step(turned, x_ref, cos_ref, sin_ref, *refs):
-    weights, out_ref = refs[:-1], refs[-1]
+def project_step(turned, placed, *refs):
+    if placed:
+        slot_ref, refs = refs[0], refs[1:]
+    x_ref, cos_ref, sin_ref = refs[:3]
+    weights, out_ref = refs[3:-1], refs[-1]
     widened = x_ref[...].astype(jnp.float32)
     centred = widened - jnp.mean(widened, axis=-1, keepdims=True)
     variance = jnp.mean(centred * centred, axis=-1, keepdims=True)
@@ -141,7 +144,15 @@
                 part = product[:, head * HEAD_DIM : (head + 1) * HEAD_DIM]
                 pieces.append(part * cosine + pltpu.roll(part, HEAD_DIM // 2, 1) * sine)
             product = jnp.concatenate(pieces, axis=1)
-        out_ref[:, index * width : (index + 1) * width] = product.astype(out_ref.dtype)
+        product = product.astype(out_ref.dtype)
+        columns = slice(index * width, (index + 1) * width)
+        if placed:
+            rows = out_ref.shape[1]
+            first = pl.program_id(0) * (product.shape[0] // rows)
+            for j in range(product.shape[0] // rows):
+                out_ref[slot_ref[first + j], :, columns] = product[j * rows : (j + 1) * rows]
+        else:
+            out_ref[:, columns] = product
 
 
 def rope_tables(positions):
@@ -153,23 +164,40 @@
     return jnp.cos(angles), jnp.sin(angles) * sign[None, :]
 
 
-def project(rows, positions, weights, turned, block_rows):
+def project(rows, positions, weights, turned, block_rows, slots=None, rows_per_slot=None):
     count, width = rows.shape
     cosine, sine = rope_tables(positions)
     out_width = sum(w.shape[1] for w in weights)
+    placed = slots is not None
+    extra = (lambda i, s: (i, 0)) if placed else (lambda i: (i, 0))
+    fixed = (lambda i, s: (0, 0)) if placed else (lambda i: (0, 0))
+    in_specs = [
+        pl.BlockSpec((block_rows, width), extra),
+        pl.BlockSpec((block_rows, HEAD_DIM), extra),
+        pl.BlockSpec((block_rows, HEAD_DIM), extra),
+    ] + [pl.BlockSpec(w.shape, fixed) for w in weights]
+    if placed:
+        out_shape = (count // rows_per_slot, rows_per_slot, out_width)
+        grid_spec = pltpu.PrefetchScalarGridSpec(
+            num_scalar_prefetch=1,
+            grid=(count // block_rows,),
+            in_specs=in_specs,
+            out_specs=pl.BlockSpec(out_shape, lambda i, s: (0, 0, 0)),
+        )
+        operands = (slots, rows, cosine, sine, *weights)
+    else:
+        out_shape = (count, out_width)
+        grid_spec = pl.GridSpec(
+            grid=(count // block_rows,),
+            in_specs=in_specs,
+            out_specs=pl.BlockSpec((block_rows, out_width), extra),
+        )
+        operands = (rows, cosine, sine, *weights)
     return pl.pallas_call(
-        functools.partial(project_step, tuple(turned)),
-        grid=(count // block_rows,),
-        in_specs=[
-            pl.BlockSpec((block_rows, width), lambda i: (i, 0)),
-            pl.BlockSpec((block_rows, HEAD_DIM), lambda i: (i, 0)),
-            pl.BlockSpec((block_rows, HEAD_DIM), lambda i: (i, 0)),
-        ]
-        + [pl.BlockSpec(w.shape, lambda i: (0, 0)) for w in weights],
-        out_specs=pl.BlockSpec((block_rows, out_width), lambda i: (i, 0)),
-        out_shape=jax.ShapeDtypeStruct((count, out_width), jnp.bfloat16),
-    )(rows, cosine, sine, *weights)
-
+        functools.partial(project_step, tuple(turned), placed),
+        grid_spec=grid_spec,
+        out_shape=jax.ShapeDtypeStruct(out_shape, jnp.bfloat16),
+    )(*operands)
 
 rope_base = 10000.0
 norm_eps = 1e-05
@@ -213,11 +241,10 @@
         start_of[:, None] + group_id * local_rows + jnp.arange(local_rows, dtype=jnp.int32)[None, :]
     ).reshape(-1)
 
-    projected = project(
+    arranged = project(
         tokens.reshape(-1, model_width), local_positions, [w_query, w_key, w_value],
-        [True, True, False], 256,
-    ).reshape(requests, local_rows, -1)
-    arranged = jnp.take(projected, deal_order, axis=0)
+        [True, True, False], 256, server, local_rows,
+    )
     dealt = lax.all_to_all(arranged, "grp", split_axis=0, concat_axis=1, tiled=True)[0]
     span_len = dealt.shape[0]
 

time: 196 us -> 195 us (level)
  other arithmetic: 17.1 us -> 15 us
  local copies, waits for them, and re-layouts: 16.5 us -> 14.5 us
    gather x1 -> x0, local copies, waits for them, and re-layouts: 2.05 us -> none  [shards(): arranged = jnp.take(projected, deal_order, axis=0)]
    another operation x6 -> x7, local copies, waits for them, and re-layouts: 5.01 us -> 5.09 us
  transfers between devices with their start and end apart: 4 -> 4, of which waited for: 3 -> 3; matrix products, arithmetic and copies ran while one was open for 10% -> 10% of each run, Pallas kernels for 30% -> 35%
where the time goes in v12:
time: 195 us; the launch traced here: 194 us
  Pallas kernels  99.4 us (51%)
  waiting for transfers between devices  31.7 us (16%)
  starting transfers between devices  25.5 us (13%)
  other arithmetic  15 us (8%)
  local copies, waits for them, and re-layouts  14.5 us (7%)
  matrix products  6.49 us (3%)
    pallas_call x2, Pallas kernels, exchange(): pl.pallas_call(functools.partial(exchange_step, axis, count), out_shape=j...  52 us
    pallas_call x6, Pallas kernels, attend(): pl.pallas_call(flash_step, grid_spec=grid_spec, out_shape=[shape, shape,...  33 us
    all_to_all x1, waiting for transfers between devices, shards(): lax.all_to_all(arranged, 'grp', split_axis=0, concat_axis=1, tiled=True)[0]  23.7 us
    pallas_call x2, Pallas kernels, project(): pl.pallas_call(functools.partial(project_step, tuple(turned), placed), gr...  14.5 us
    all_to_all x2, starting transfers between devices, shards(): lax.all_to_all(partial_value, 'tp', split_axis=0, concat_axis=0, tiled=True)  12.9 us
    all_to_all x1, starting transfers between devices, shards(): lax.all_to_all(arranged, 'grp', split_axis=0, concat_axis=1, tiled=True)[0]  11.2 us
    ppermute x1, waiting for transfers between devices, swapped(): return lax.ppermute(value, axis, pairs)  7.9 us
    dot_general x2, matrix products, shards(): jnp.einsum('qc,ctd->tqd', attended, out_by_block, preferred_element_type=...  6.49 us
  transfers between devices with their start and end apart: 4, of which 3 were waited for; matrix products, arithmetic and copies ran while one was open for 10% of the time, Pallas kernels for 35%

profile of v12, /device:TPU:1, one launch (start us, length us, event | category | flops | bytes accessed | tf_op | source)
XLA Modules:
  0.0 194.1 jit_solution(15507062758268433605)
XLA Ops:
  3.6 3.7 %fusion.4 = (f32[1024,128]{1,0:T(8,128)}, f32[1024,128]{1,0:T(8,128)}) fusion(f32[128]{0:T(128)} %constant.62.clone.1, f32[128]{0:T(128)S(1)} %pad_maximum_fusion.2, f32[1024]{0:T(1024)S(1)} %convert_element_type.50), kind=kLoop, calls=%fused_computation.13 | loop fusion | flops 262144 | bytes 1053696 | tf_op jit(solution)/shard_map/mul | solution.py:164
  7.3 10.5 %shard_map.118 = bf16[32,32,768]{2,1,0:T(8,128)(2,1)} custom-call(s32[32]{0:T(128)} %scatter_custom_fusion.refs_0_, bf16[1024,2048]{1,0:T(8,128)(2,1)} %bitcast.51, f32[1024,128]{1,0:T(8,128)} %get-tuple-element.40.refs_2_, f32[1024,128]{1,0:T(8,128)} %get-tuple-element.39.refs_3_, bf16[2048,256]{1,0:T(8,128)(2,1)} %refs_4_.2, bf16[2048,256]{1,0:T(8,128)(2,1)} %refs_3_.1, ...), custom_call_target="tpu_custom_call" | custom-call | tf_op jit(solution)/shard_map/pallas_call | solution.py:196
  17.9 11.2 %all-to-all-start = ((bf16[32,32,768]{2,1,0:T(8,128)(2,1)}), bf16[32,32,768]{2,1,0:T(8,128)(2,1)S(1)}, u32[]{:S(2)}, u32[]{:S(2)}) async-start(bf16[32,32,768]{2,1,0:T(8,128)(2,1)} %shard_map.118), calls=%async_computation | async-start | bytes 3145728 | tf_op jit(solution)/shard_map/all_to_all | solution.py:248
  29.1 1.5 collective-permute-start
  34.5 1.7 scatter_custom_fusion.2
  36.2 1.2 fusion.7
  37.4 4.0 %shard_map.119 = bf16[256,512]{1,0:T(8,128)(2,1)} custom-call(bf16[256,2048]{1,0:T(8,128)(2,1)} %bitcast.53, f32[256,128]{1,0:T(8,128)} %get-tuple-element.42.refs_1_, f32[256,128]{1,0:T(8,128)} %get-tuple-element.41.refs_2_, bf16[2048,256]{1,0:T(8,128)(2,1)} %refs_3_.1, bf16[2048,256]{1,0:T(8,128)(2,1)} %refs_4_.3), custom_call_target="tpu_custom_call" | custom-call | tf_op jit(solution)/shard_map/pallas_call | solution.py:196
  41.4 1.2 compare_select_fusion.rank_ref
  43.7 23.7 %all-to-all-done = bf16[32,32,768]{2,1,0:T(8,128)(2,1)S(1)} async-done(((bf16[32,32,768]{2,1,0:T(8,128)(2,1)}), bf16[32,32,768]{2,1,0:T(8,128)(2,1)S(1)}, u32[]{:S(2)}, u32[]{:S(2)}) %all-to-all-start) | async-done | bytes 1572896 | tf_op jit(solution)/shard_map/all_to_all | solution.py:248
  68.3 1.2 pad_maximum_fusion.k_ref.v_ref
  72.0 6.1 %shard_map.124 = (f32[512,256]{1,0:T(8,128)}, f32[512,256]{1,0:T(8,128)}, f32[512,256]{1,0:T(8,128)}) custom-call(s32[1]{0:T(128)} %constant.66.clone.1.flags_ref, s32[512,1]{1,0:T(8,128)} %broadcast_in_dim.80.qrow_ref, s32[1,1280]{1,0:T(1,128)} %broadcast_in_dim.75.rank_ref, ...), custom_call_target="tpu_custom_call", output_to_operand_aliasing={{0}: (6, {}), {1}: (7, {}), {2}: (8, {})} | custom-call | tf_op jit(solution)/shard_map/pallas_call | solution.py:63
  78.1 7.2 %shard_map.125 = (f32[512,256]{1,0:T(8,128)}, f32[512,256]{1,0:T(8,128)}, f32[512,256]{1,0:T(8,128)}) custom-call(s32[1]{0:T(128)S(6)} %convert_element_type.51.flags_ref, s32[512,1]{1,0:T(8,128)} %broadcast_in_dim.80.qrow_ref, s32[1,2048]{1,0:T(1,128)} %bitcast.58, ...), custom_call_target="tpu_custom_call", output_to_operand_aliasing={{0}: (6, {}), {1}: (7, {}), {2}: (8, {})} | custom-call | tf_op jit(solution)/shard_map/pallas_call | solution.py:63
  85.3 7.9 %collective-permute-done.k_ref.v_ref = bf16[2,2048,256]{2,1,0:T(8,128)(2,1)} collective-permute-done((bf16[2,2048,256]{2,1,0:T(8,128)(2,1)}, bf16[2,2048,256]{2,1,0:T(8,128)(2,1)}, u32[]{:S(2)}, u32[]{:S(2)}) %collective-permute-start) | collective-permute-done | bytes 2097184 | tf_op jit(solution)/shard_map/ppermute | solution.py:209
  93.2 3.2 %shard_map.126 = (f32[512,256]{1,0:T(8,128)}, f32[512,256]{1,0:T(8,128)}, f32[512,256]{1,0:T(8,128)}) custom-call(s32[1]{0:T(128)S(6)} %convert_element_type.48.flags_ref, s32[512,1]{1,0:T(8,128)} %broadcast_in_dim.80.qrow_ref, s32[1,2048]{1,0:T(1,128)} %compare_select_fusion.rank_ref, ...), custom_call_target="tpu_custom_call", output_to_operand_aliasing={{0}: (6, {}), {1}: (7, {}), {2}: (8, {})} | custom-call | tf_op jit(solution)/shard_map/pallas_call | solution.py:63
  96.4 3.2 %convert_bitcast_fusion = bf16[8,512,256]{2,1,0:T(8,128)(2,1)} fusion(bf16[32,8,8,256]{3,2,1,0:T(8,128)(2,1)S(1)} %bitcast.63, f32[512,256]{1,0:T(8,128)} %get-tuple-element.35, f32[512,256]{1,0:T(8,128)} %get-tuple-element.36), kind=kOutput, calls=%fused_computation.4 | convolution fusion | flops 538181632 | bytes 4194304 | tf_op jit(solution)/shard_map/qc,ctd->tqd/dot_general | solution.py:309
  99.7 6.3 %all-to-all-start.2 = ((bf16[8,512,256]{2,1,0:T(8,128)(2,1)}), bf16[8,512,256]{2,1,0:T(8,128)(2,1)S(1)}, u32[]{:S(2)}, u32[]{:S(2)}) async-start(bf16[8,512,256]{2,1,0:T(8,128)(2,1)} %convert_bitcast_fusion), calls=%async_computation.2 | async-start | bytes 4194304 | tf_op jit(solution)/shard_map/all_to_all | solution.py:313
  109.4 6.1 %shard_map.120 = (f32[512,256]{1,0:T(8,128)}, f32[512,256]{1,0:T(8,128)}, f32[512,256]{1,0:T(8,128)}) custom-call(s32[1]{0:T(128)} %constant.66.clone.1.flags_ref, s32[512,1]{1,0:T(8,128)} %broadcast_in_dim.79.qrow_ref, s32[1,1280]{1,0:T(1,128)} %broadcast_in_dim.75.rank_ref, ...), custom_call_target="tpu_custom_call", output_to_operand_aliasing={{0}: (6, {}), {1}: (7, {}), {2}: (8, {})} | custom-call | tf_op jit(solution)/shard_map/pallas_call | solution.py:63
  115.5 7.3 %shard_map.121 = (f32[512,256]{1,0:T(8,128)}, f32[512,256]{1,0:T(8,128)}, f32[512,256]{1,0:T(8,128)}) custom-call(s32[1]{0:T(128)S(6)} %convert_element_type.51.flags_ref, s32[512,1]{1,0:T(8,128)} %broadcast_in_dim.79.qrow_ref, s32[1,2048]{1,0:T(1,128)} %bitcast.59, ...), custom_call_target="tpu_custom_call", output_to_operand_aliasing={{0}: (6, {}), {1}: (7, {}), {2}: (8, {})} | custom-call | tf_op jit(solution)/shard_map/pallas_call | solution.py:63
  122.7 3.1 %shard_map.122 = (f32[512,256]{1,0:T(8,128)}, f32[512,256]{1,0:T(8,128)}, f32[512,256]{1,0:T(8,128)}) custom-call(s32[1]{0:T(128)S(6)} %convert_element_type.48.flags_ref, s32[512,1]{1,0:T(8,128)} %broadcast_in_dim.79.qrow_ref, s32[1,2048]{1,0:T(1,128)} %compare_select_fusion.rank_ref, ...), custom_call_target="tpu_custom_call", output_to_operand_aliasing={{0}: (6, {}), {1}: (7, {}), {2}: (8, {})} | custom-call | tf_op jit(solution)/shard_map/pallas_call | solution.py:63
  125.9 3.2 %convert_bitcast_fusion.1 = bf16[8,512,256]{2,1,0:T(8,128)(2,1)} fusion(bf16[32,8,8,256]{3,2,1,0:T(8,128)(2,1)S(1)} %bitcast.64, f32[512,256]{1,0:T(8,128)} %get-tuple-element.27, f32[512,256]{1,0:T(8,128)} %get-tuple-element.28), kind=kOutput, calls=%fused_computation.5 | convolution fusion | flops 538181632 | bytes 4194304 | tf_op jit(solution)/shard_map/qc,ctd->tqd/dot_general | solution.py:309
  129.2 6.5 %all-to-all-start.1 = ((bf16[8,512,256]{2,1,0:T(8,128)(2,1)}), bf16[8,512,256]{2,1,0:T(8,128)(2,1)}, u32[]{:S(2)}, u32[]{:S(2)}) async-start(bf16[8,512,256]{2,1,0:T(8,128)(2,1)} %convert_bitcast_fusion.1), calls=%async_computation.1 | async-start | bytes 4194304 | tf_op jit(solution)/shard_map/all_to_all | solution.py:313
  136.8 34.1 %shard_map.127 = bf16[32,16,256]{2,1,0:T(8,128)(2,1)} custom-call(bf16[32,16,256]{2,1,0:T(8,128)(2,1)} %bitcast.55), custom_call_target="tpu_custom_call" | custom-call | tf_op jit(solution)/shard_map/pallas_call | solution.py:113
  171.0 2.7 %reduce_sum.24 = bf16[512,256]{1,0:T(8,128)(2,1)} reduce(bf16[8,512,256]{2,1,0:T(8,128)(2,1)} %all-to-all-done.1, bf16[]{:T(256)} %constant.69.clone.1), dimensions={0}, to_apply=%region_3.4 | reduce | flops 917504 | bytes 2359298 | tf_op jit(solution)/shard_map/reduce_sum | solution.py:316
  173.7 17.9 %shard_map.123 = bf16[32,16,256]{2,1,0:T(8,128)(2,1)} custom-call(bf16[32,16,256]{2,1,0:T(8,128)(2,1)} %bitcast.54), custom_call_target="tpu_custom_call" | custom-call | tf_op jit(solution)/shard_map/pallas_call | solution.py:113
  (59 shorter events, 18.1 us)
Async XLA Ops:
  17.8 12.7 %copy-start.5 = (s32[32]{0:T(128)S(1)}, s32[32]{0:T(128)}, u32[]{:S(2)}) copy-start(s32[32]{0:T(128)} %param.22) | copy-start | bytes 388
  17.8 13.9 %copy-start.7 = (s32[32]{0:T(128)S(1)}, s32[32]{0:T(128)}, u32[]{:S(2)}) copy-start(s32[32]{0:T(128)} %param.21) | copy-start | bytes 388
  17.8 15.1 %copy-start.3 = (s32[1,256]{1,0:T(1,128)S(1)}, s32[1,256]{1,0:T(1,128)}, u32[]{:S(2)}) copy-start(s32[1,256]{1,0:T(1,128)} %param.23) | copy-start | bytes 3076
  17.8 18.3 %copy-start.4 = (f32[128]{0:T(128)S(1)}, f32[128]{0:T(128)}, u32[]{:S(2)}) copy-start(f32[128]{0:T(128)} %constant.62.clone.1) | copy-start | bytes 1540
  17.9 49.5 %all-to-all-start = ((bf16[32,32,768]{2,1,0:T(8,128)(2,1)}), bf16[32,32,768]{2,1,0:T(8,128)(2,1)S(1)}, u32[]{:S(2)}, u32[]{:S(2)}) async-start(bf16[32,32,768]{2,1,0:T(8,128)(2,1)} %shard_map.118), calls=%async_computation | async-start | bytes 3145728 | tf_op jit(solution)/shard_map/all_to_all | solution.py:248
  29.1 64.2 %collective-permute-start = (bf16[2,2048,256]{2,1,0:T(8,128)(2,1)}, bf16[2,2048,256]{2,1,0:T(8,128)(2,1)}, u32[]{:S(2)}, u32[]{:S(2)}) collective-permute-start(bf16[2,2048,256]{2,1,0:T(8,128)(2,1)} %bitcast.62), channel_id=1, source_target_pairs={{0,128},{8,136},{16,144},{24,152},{32,160},{40,168},{48,176},{56,1... | collective-permute-start | bytes 6291464 | tf_op jit(solution)/shard_map/ppermute | solution.py:209
  67.4 1.0 copy-start.1
  67.5 2.0 %copy-start = (bf16[32,2,16,768]{3,2,0,1:T(8,128)(2,1)}, bf16[32,2,16,768]{3,2,0,1:T(8,128)(2,1)S(1)}, u32[]{:S(2)}) copy-start(bf16[32,2,16,768]{3,2,0,1:T(8,128)(2,1)S(1)} %copy.34) | copy-start | bytes 4718596
  93.2 3.2 %copy-start.8 = (bf16[256,2048]{1,0:T(8,128)(2,1)S(1)}, bf16[256,2048]{1,0:T(8,128)(2,1)}, u32[]{:S(2)}) copy-start(bf16[256,2048]{1,0:T(8,128)(2,1)} %param.16) | copy-start | bytes 3145732
  99.7 29.6 %all-to-all-start.2 = ((bf16[8,512,256]{2,1,0:T(8,128)(2,1)}), bf16[8,512,256]{2,1,0:T(8,128)(2,1)S(1)}, u32[]{:S(2)}, u32[]{:S(2)}) async-start(bf16[8,512,256]{2,1,0:T(8,128)(2,1)} %convert_bitcast_fusion), calls=%async_computation.2 | async-start | bytes 4194304 | tf_op jit(solution)/shard_map/all_to_all | solution.py:313
  129.1 6.7 %copy-start.6 = (s32[32]{0:T(128)S(1)}, s32[32]{0:T(128)}, u32[]{:S(2)}) copy-start(s32[32]{0:T(128)} %scatter_custom_fusion.refs_0_) | copy-start | bytes 388
  129.2 41.7 %all-to-all-start.1 = ((bf16[8,512,256]{2,1,0:T(8,128)(2,1)}), bf16[8,512,256]{2,1,0:T(8,128)(2,1)}, u32[]{:S(2)}, u32[]{:S(2)}) async-start(bf16[8,512,256]{2,1,0:T(8,128)(2,1)} %convert_bitcast_fusion.1), calls=%async_computation.1 | async-start | bytes 4194304 | tf_op jit(solution)/shard_map/all_to_all | solution.py:313
  171.0 20.6 %copy-start.2 = (bf16[32,16,256]{2,1,0:T(8,128)(2,1)S(1)}, bf16[32,16,256]{2,1,0:T(8,128)(2,1)}, u32[]{:S(2)}) copy-start(bf16[32,16,256]{2,1,0:T(8,128)(2,1)} %shard_map.127) | copy-start | bytes 786436

commit v13 on v11

--- a/solution.py
+++ b/solution.py
@@ -256,35 +256,49 @@
 
     returned = []
     exchanged = []
-    for chunk in range(chunks):
-        query_rows = row_of[chunk * chunk_len : (chunk + 1) * chunk_len][:, None]
-        state = (
-            jnp.full((chunk_len, local_width), FLOOR, jnp.float32),
-            jnp.zeros((chunk_len, local_width), jnp.float32),
-            jnp.zeros((chunk_len, local_width), jnp.float32),
-        )
-        state = attend(
-            state, jnp.ones((1,), jnp.int32), query_rows, fresh_rank, order, chunk,
+    def fresh_call(chunk, state):
+        return attend(
+            state, jnp.ones((1,), jnp.int32), row_of[chunk * chunk_len : (chunk + 1) * chunk_len][:, None],
+            fresh_rank, order, chunk,
             fresh, lambda h, kb: (kb, h), fresh, lambda h, kb: (kb, heads + h),
             fresh_count, heads, fresh_count,
         )
-        state = attend(
-            state, own_flags, query_rows, own_rank, order, chunk,
+
+    def own_call(chunk, state):
+        return attend(
+            state, own_flags, row_of[chunk * chunk_len : (chunk + 1) * chunk_len][:, None],
+            own_rank, order, chunk,
             own_cache[0], lambda h, kb: (0, kb, h), own_cache[0], lambda h, kb: (1, kb, h),
             cap, heads, block_len,
         )
-        state = attend(
-            state, guest_flags, query_rows, guest_rank, order, chunk,
+
+    def guest_call(chunk, state):
+        return attend(
+            state, guest_flags, row_of[chunk * chunk_len : (chunk + 1) * chunk_len][:, None],
+            guest_rank, order, chunk,
             fetched, lambda h, kb: (0, kb, h), fetched, lambda h, kb: (1, kb, h),
             gcap, heads, block_len,
         )
+
+    def exchanged_partial(state):
         attended = (state[2] / state[1]).astype(jnp.bfloat16)
         partial_value = jnp.einsum(
             "qc,ctd->tqd", attended, out_by_block, preferred_element_type=jnp.float32
         ).astype(jnp.bfloat16)
-        exchanged.append(
-            lax.all_to_all(partial_value, "tp", split_axis=0, concat_axis=0, tiled=True)
-        )
+        return lax.all_to_all(partial_value, "tp", split_axis=0, concat_axis=0, tiled=True)
+
+    empty = (
+        jnp.full((chunk_len, local_width), FLOOR, jnp.float32),
+        jnp.zeros((chunk_len, local_width), jnp.float32),
+        jnp.zeros((chunk_len, local_width), jnp.float32),
+    )
+    first = own_call(0, fresh_call(0, empty))
+    second = fresh_call(1, empty)
+    first, second = lax.optimization_barrier((first, second))
+    first = guest_call(0, first)
+    first, second = lax.optimization_barrier((first, second))
+    exchanged.append(exchanged_partial(first))
+    exchanged.append(exchanged_partial(guest_call(1, own_call(1, second))))
     for chunk in range(chunks):
         mixed_rows = exchanged[chunk].astype(jnp.float32).sum(axis=0).astype(jnp.bfloat16)
         returned.append(exchange(mixed_rows.reshape(groups, piece, -1), "grp", 1 + chunk))

time: 196 us -> 197 us (level)
    all_to_all x2, waiting for transfers between devices: 0.07 us -> 9.25 us  [exchanged_partial(): lax.all_to_all(partial_value, 'tp', split_axis=0, concat_axis=0, tiled=True)]
    ppermute x1, waiting for transfers between devices: 7.57 us -> 0.01 us  [swapped(): return lax.ppermute(value, axis, pairs)]
    another operation x6 -> x4, local copies, waits for them, and re-layouts: 5.01 us -> 3.34 us
  transfers between devices with their start and end apart: 4 -> 4, of which waited for: 3 -> 2; matrix products, arithmetic and copies ran while one was open for 10% -> 10% of each run, Pallas kernels for 30% -> 31%
where the time goes in v13:
time: 197 us; the launch traced here: 196 us
  Pallas kernels  98.5 us (50%)
  waiting for transfers between devices  32.2 us (16%)
  starting transfers between devices  24.3 us (12%)
  other arithmetic  17.1 us (9%)
  local copies, waits for them, and re-layouts  16.4 us (8%)
  matrix products  6.54 us (3%)
    pallas_call x2, Pallas kernels, exchange(): pl.pallas_call(functools.partial(exchange_step, axis, count), out_shape=j...  52.1 us
    pallas_call x6, Pallas kernels, attend(): pl.pallas_call(flash_step, grid_spec=grid_spec, out_shape=[shape, shape,...  33 us
    all_to_all x1, waiting for transfers between devices, shards(): lax.all_to_all(arranged, 'grp', split_axis=0, concat_axis=1, tiled=True)[0]  22.9 us
    pallas_call x2, Pallas kernels, project(): pl.pallas_call(functools.partial(project_step, tuple(turned)), grid=(coun...  13.4 us
    all_to_all x2, starting transfers between devices, exchanged_partial(): lax.all_to_all(partial_value, 'tp', split_axis=0, concat_axis=0, tiled=True)  11.7 us
    all_to_all x1, starting transfers between devices, shards(): lax.all_to_all(arranged, 'grp', split_axis=0, concat_axis=1, tiled=True)[0]  11.2 us
    all_to_all x2, waiting for transfers between devices, exchanged_partial(): lax.all_to_all(partial_value, 'tp', split_axis=0, concat_axis=0, tiled=True)  9.25 us
    dot_general x2, matrix products, exchanged_partial(): jnp.einsum('qc,ctd->tqd', attended, out_by_block, preferred_element_type=...  6.54 us
  transfers between devices with their start and end apart: 4, of which 2 were waited for; matrix products, arithmetic and copies ran while one was open for 10% of the time, Pallas kernels for 31%

profile of v13, /device:TPU:1, one launch (start us, length us, event | category | flops | bytes accessed | tf_op | source)
XLA Modules:
  0.0 196.3 jit_solution(5769778776749431119)
XLA Ops:
  3.1 3.7 %fusion.4 = (f32[1024,128]{1,0:T(8,128)}, f32[1024,128]{1,0:T(8,128)}) fusion(f32[128]{0:T(128)} %constant.74.clone.1, f32[128]{0:T(128)S(1)} %pad_maximum_fusion.2, f32[1024]{0:T(1024)S(1)} %convert_element_type.50), kind=kLoop, calls=%fused_computation.15 | loop fusion | flops 262144 | bytes 1053696 | tf_op jit(solution)/shard_map/mul | solution.py:153
  6.9 9.4 %shard_map.118 = bf16[1024,768]{1,0:T(8,128)(2,1)} custom-call(bf16[1024,2048]{1,0:T(8,128)(2,1)} %bitcast.50, f32[1024,128]{1,0:T(8,128)} %get-tuple-element.62.cos_ref, f32[1024,128]{1,0:T(8,128)} %get-tuple-element.61.sin_ref, bf16[2048,256]{1,0:T(8,128)(2,1)} %refs_0_.2, bf16[2048,256]{1,0:T(8,128)(2,1)} %refs_0_.3, bf16[2048,256]{1,0:T(8,128)(2,1)} %refs_1_.3), custom_call_target="tpu_custom_call" | custom-call | tf_op jit(solution)/shard_map/pallas_call | solution.py:160
  16.3 2.1 %gather_fusion = bf16[32,32,768]{2,1,0:T(8,128)(2,1)S(1)} fusion(bf16[32,32,768]{2,1,0:T(8,128)(2,1)} %bitcast.49, s32[1024]{0:T(1024)S(1)} %pad_clamp_fusion.1), kind=kCustom, calls=%fused_computation | custom fusion | bytes 3145856 | tf_op jit(solution)/shard_map/jit(_take)/gather | solution.py:220
  18.3 1.4 broadcast_select_fusion
  19.7 11.2 %all-to-all-start = ((bf16[32,32,768]{2,1,0:T(8,128)(2,1)}), bf16[32,32,768]{2,1,0:T(8,128)(2,1)S(1)}, u32[]{:S(2)}, u32[]{:S(2)}) async-start(bf16[32,32,768]{2,1,0:T(8,128)(2,1)} %broadcast_select_fusion), calls=%async_computation | async-start | bytes 3145728 | tf_op jit(solution)/shard_map/all_to_all | solution.py:221
  30.9 1.5 collective-permute-start
  37.1 1.3 fusion.7
  38.4 4.0 %shard_map.119 = bf16[256,512]{1,0:T(8,128)(2,1)} custom-call(bf16[256,2048]{1,0:T(8,128)(2,1)} %bitcast.52, f32[256,128]{1,0:T(8,128)} %get-tuple-element.64.cos_ref, f32[256,128]{1,0:T(8,128)} %get-tuple-element.63.sin_ref, bf16[2048,256]{1,0:T(8,128)(2,1)} %refs_0_.3, bf16[2048,256]{1,0:T(8,128)(2,1)} %refs_1_.3), custom_call_target="tpu_custom_call" | custom-call | tf_op jit(solution)/shard_map/pallas_call | solution.py:160
  42.3 1.7 scatter_custom_fusion.2
  46.3 22.9 %all-to-all-done = bf16[32,32,768]{2,1,0:T(8,128)(2,1)S(1)} async-done(((bf16[32,32,768]{2,1,0:T(8,128)(2,1)}), bf16[32,32,768]{2,1,0:T(8,128)(2,1)S(1)}, u32[]{:S(2)}, u32[]{:S(2)}) %all-to-all-start) | async-done | bytes 1572896 | tf_op jit(solution)/shard_map/all_to_all | solution.py:221
  74.2 6.1 %shard_map.120 = (f32[512,256]{1,0:T(8,128)}, f32[512,256]{1,0:T(8,128)}, f32[512,256]{1,0:T(8,128)}) custom-call(s32[1]{0:T(128)} %constant.79.clone.1.flags_ref, s32[512,1]{1,0:T(8,128)} %broadcast_in_dim.99.qrow_ref, s32[1,1280]{1,0:T(1,128)} %broadcast_in_dim.94.rank_ref, ...), custom_call_target="tpu_custom_call", output_to_operand_aliasing={{0}: (6, {}), {1}: (7, {}), {2}: (8, {})} | custom-call | tf_op jit(solution)/shard_map/pallas_call | solution.py:63
  82.8 6.1 %shard_map.122 = (f32[512,256]{1,0:T(8,128)}, f32[512,256]{1,0:T(8,128)}, f32[512,256]{1,0:T(8,128)}) custom-call(s32[1]{0:T(128)} %constant.79.clone.1.flags_ref, s32[512,1]{1,0:T(8,128)} %broadcast_in_dim.100.qrow_ref, s32[1,1280]{1,0:T(1,128)} %broadcast_in_dim.94.rank_ref, ...), custom_call_target="tpu_custom_call", output_to_operand_aliasing={{0}: (6, {}), {1}: (7, {}), {2}: (8, {})} | custom-call | tf_op jit(solution)/shard_map/pallas_call | solution.py:63
  88.9 7.3 %shard_map.121 = (f32[512,256]{1,0:T(8,128)}, f32[512,256]{1,0:T(8,128)}, f32[512,256]{1,0:T(8,128)}) custom-call(s32[1]{0:T(128)S(6)} %convert_element_type.51.flags_ref, s32[512,1]{1,0:T(8,128)} %broadcast_in_dim.99.qrow_ref, s32[1,2048]{1,0:T(1,128)} %bitcast.57, ...), custom_call_target="tpu_custom_call", output_to_operand_aliasing={{0}: (6, {}), {1}: (7, {}), {2}: (8, {})} | custom-call | tf_op jit(solution)/shard_map/pallas_call | solution.py:63
  96.2 3.2 %shard_map.123 = (f32[512,256]{1,0:T(8,128)}, f32[512,256]{1,0:T(8,128)}, f32[512,256]{1,0:T(8,128)}) custom-call(s32[1]{0:T(128)S(6)} %convert_element_type.48.flags_ref, s32[512,1]{1,0:T(8,128)} %broadcast_in_dim.99.qrow_ref, s32[1,2048]{1,0:T(1,128)} %compare_select_fusion.rank_ref, ...), custom_call_target="tpu_custom_call", output_to_operand_aliasing={{0}: (6, {}), {1}: (7, {}), {2}: (8, {})} | custom-call | tf_op jit(solution)/shard_map/pallas_call | solution.py:63
  99.4 3.3 %convert_bitcast_fusion.1 = bf16[8,512,256]{2,1,0:T(8,128)(2,1)} fusion(bf16[32,8,8,256]{3,2,1,0:T(8,128)(2,1)S(1)} %bitcast.62, f32[512,256]{1,0:T(8,128)} %get-tuple-element.49, f32[512,256]{1,0:T(8,128)} %get-tuple-element.50), kind=kOutput, calls=%fused_computation.6 | convolution fusion | flops 538181632 | bytes 4194304 | tf_op jit(solution)/shard_map/qc,ctd->tqd/dot_general | solution.py:285
  102.6 6.4 %all-to-all-start.1 = ((bf16[8,512,256]{2,1,0:T(8,128)(2,1)}), bf16[8,512,256]{2,1,0:T(8,128)(2,1)S(1)}, u32[]{:S(2)}, u32[]{:S(2)}) async-start(bf16[8,512,256]{2,1,0:T(8,128)(2,1)} %convert_bitcast_fusion.1), calls=%async_computation.1 | async-start | bytes 4194304 | tf_op jit(solution)/shard_map/all_to_all | solution.py:288
  109.0 7.2 %shard_map.125 = (f32[512,256]{1,0:T(8,128)}, f32[512,256]{1,0:T(8,128)}, f32[512,256]{1,0:T(8,128)}) custom-call(s32[1]{0:T(128)S(6)} %convert_element_type.51.flags_ref, s32[512,1]{1,0:T(8,128)} %broadcast_in_dim.100.qrow_ref, s32[1,2048]{1,0:T(1,128)} %bitcast.58, ...), custom_call_target="tpu_custom_call", output_to_operand_aliasing={{0}: (6, {}), {1}: (7, {}), {2}: (8, {})} | custom-call | tf_op jit(solution)/shard_map/pallas_call | solution.py:63
  116.2 3.1 %shard_map.126 = (f32[512,256]{1,0:T(8,128)}, f32[512,256]{1,0:T(8,128)}, f32[512,256]{1,0:T(8,128)}) custom-call(s32[1]{0:T(128)S(6)} %convert_element_type.48.flags_ref, s32[512,1]{1,0:T(8,128)} %broadcast_in_dim.100.qrow_ref, s32[1,2048]{1,0:T(1,128)} %compare_select_fusion.rank_ref, ...), custom_call_target="tpu_custom_call", output_to_operand_aliasing={{0}: (6, {}), {1}: (7, {}), {2}: (8, {})} | custom-call | tf_op jit(solution)/shard_map/pallas_call | solution.py:63
  119.4 3.3 %convert_bitcast_fusion = bf16[8,512,256]{2,1,0:T(8,128)(2,1)} fusion(bf16[32,8,8,256]{3,2,1,0:T(8,128)(2,1)S(1)} %bitcast.63, f32[512,256]{1,0:T(8,128)} %get-tuple-element.57, f32[512,256]{1,0:T(8,128)} %get-tuple-element.58), kind=kOutput, calls=%fused_computation.5 | convolution fusion | flops 538181632 | bytes 4194304 | tf_op jit(solution)/shard_map/qc,ctd->tqd/dot_general | solution.py:285
  122.6 9.2 %all-to-all-done.1 = bf16[8,512,256]{2,1,0:T(8,128)(2,1)S(1)} async-done(((bf16[8,512,256]{2,1,0:T(8,128)(2,1)}), bf16[8,512,256]{2,1,0:T(8,128)(2,1)S(1)}, u32[]{:S(2)}, u32[]{:S(2)}) %all-to-all-start.1) | async-done | bytes 2097184 | tf_op jit(solution)/shard_map/all_to_all | solution.py:288
  131.9 5.3 %all-to-all-start.2 = ((bf16[8,512,256]{2,1,0:T(8,128)(2,1)}), bf16[8,512,256]{2,1,0:T(8,128)(2,1)}, u32[]{:S(2)}, u32[]{:S(2)}) async-start(bf16[8,512,256]{2,1,0:T(8,128)(2,1)} %convert_bitcast_fusion), calls=%async_computation.2 | async-start | bytes 4194304 | tf_op jit(solution)/shard_map/all_to_all | solution.py:288
  139.0 26.6 %shard_map.124 = bf16[32,16,256]{2,1,0:T(8,128)(2,1)} custom-call(bf16[32,16,256]{2,1,0:T(8,128)(2,1)} %bitcast.54), custom_call_target="tpu_custom_call" | custom-call | tf_op jit(solution)/shard_map/pallas_call | solution.py:113
  165.6 2.7 %reduce_sum.25 = bf16[512,256]{1,0:T(8,128)(2,1)} reduce(bf16[8,512,256]{2,1,0:T(8,128)(2,1)} %all-to-all-done.2, bf16[]{:T(256)} %constant.82.clone.1), dimensions={0}, to_apply=%region_4.5 | reduce | flops 917504 | bytes 2359298 | tf_op jit(solution)/shard_map/reduce_sum | solution.py:303
  168.3 25.4 %shard_map.127 = bf16[32,16,256]{2,1,0:T(8,128)(2,1)} custom-call(bf16[32,16,256]{2,1,0:T(8,128)(2,1)} %bitcast.53), custom_call_target="tpu_custom_call" | custom-call | tf_op jit(solution)/shard_map/pallas_call | solution.py:113
  (61 shorter events, 20.7 us)
Async XLA Ops:
  19.7 12.7 %copy-start.3 = (s32[1,256]{1,0:T(1,128)S(1)}, s32[1,256]{1,0:T(1,128)}, u32[]{:S(2)}) copy-start(s32[1,256]{1,0:T(1,128)} %param.23) | copy-start | bytes 3076
  19.7 14.3 %copy-start.6 = (s32[32]{0:T(128)S(1)}, s32[32]{0:T(128)}, u32[]{:S(2)}) copy-start(s32[32]{0:T(128)} %param.21) | copy-start | bytes 388
  19.7 16.2 %copy-start.5 = (s32[32]{0:T(128)S(1)}, s32[32]{0:T(128)}, u32[]{:S(2)}) copy-start(s32[32]{0:T(128)} %param.22) | copy-start | bytes 388
  19.7 17.4 %copy-start.4 = (f32[128]{0:T(128)S(1)}, f32[128]{0:T(128)}, u32[]{:S(2)}) copy-start(f32[128]{0:T(128)} %constant.74.clone.1) | copy-start | bytes 1540
  19.7 49.5 %all-to-all-start = ((bf16[32,32,768]{2,1,0:T(8,128)(2,1)}), bf16[32,32,768]{2,1,0:T(8,128)(2,1)S(1)}, u32[]{:S(2)}, u32[]{:S(2)}) async-start(bf16[32,32,768]{2,1,0:T(8,128)(2,1)} %broadcast_select_fusion), calls=%async_computation | async-start | bytes 3145728 | tf_op jit(solution)/shard_map/all_to_all | solution.py:221
  30.9 65.2 %collective-permute-start = (bf16[2,2048,256]{2,1,0:T(8,128)(2,1)}, bf16[2,2048,256]{2,1,0:T(8,128)(2,1)}, u32[]{:S(2)}, u32[]{:S(2)}) collective-permute-start(bf16[2,2048,256]{2,1,0:T(8,128)(2,1)} %bitcast.61), channel_id=1, source_target_pairs={{0,128},{8,136},{16,144},{24,152},{32,160},{40,168},{48,176},{56,1... | collective-permute-start | bytes 6291464 | tf_op jit(solution)/shard_map/ppermute | solution.py:181
  69.4 2.3 %copy-start = (bf16[2,32,16,768]{3,2,1,0:T(8,128)(2,1)}, bf16[2,32,16,768]{3,2,1,0:T(8,128)(2,1)S(1)}, u32[]{:S(2)}) copy-start(bf16[2,32,16,768]{3,2,1,0:T(8,128)(2,1)S(1)} %copy.33) | copy-start | bytes 4718596
  69.4 1.1 copy-start.1
  96.2 3.2 %copy-start.7 = (bf16[256,2048]{1,0:T(8,128)(2,1)S(1)}, bf16[256,2048]{1,0:T(8,128)(2,1)}, u32[]{:S(2)}) copy-start(bf16[256,2048]{1,0:T(8,128)(2,1)} %param.16) | copy-start | bytes 3145732
  102.6 29.2 %all-to-all-start.1 = ((bf16[8,512,256]{2,1,0:T(8,128)(2,1)}), bf16[8,512,256]{2,1,0:T(8,128)(2,1)S(1)}, u32[]{:S(2)}, u32[]{:S(2)}) async-start(bf16[8,512,256]{2,1,0:T(8,128)(2,1)} %convert_bitcast_fusion.1), calls=%async_computation.1 | async-start | bytes 4194304 | tf_op jit(solution)/shard_map/all_to_all | solution.py:288
  131.9 33.7 %all-to-all-start.2 = ((bf16[8,512,256]{2,1,0:T(8,128)(2,1)}), bf16[8,512,256]{2,1,0:T(8,128)(2,1)}, u32[]{:S(2)}, u32[]{:S(2)}) async-start(bf16[8,512,256]{2,1,0:T(8,128)(2,1)} %convert_bitcast_fusion), calls=%async_computation.2 | async-start | bytes 4194304 | tf_op jit(solution)/shard_map/all_to_all | solution.py:288
  165.6 28.1 %copy-start.2 = (bf16[32,16,256]{2,1,0:T(8,128)(2,1)S(1)}, bf16[32,16,256]{2,1,0:T(8,128)(2,1)}, u32[]{:S(2)}) copy-start(bf16[32,16,256]{2,1,0:T(8,128)(2,1)} %shard_map.124) | copy-start | bytes 786436

commit v14 on v11

--- a/solution.py
+++ b/solution.py
@@ -231,13 +231,16 @@
     chunks = 2
     piece = local_rows // chunks
     chunk_len = span_len // chunks
-    order = dealt.reshape(groups, chunks, piece, -1).transpose(1, 0, 2, 3).reshape(span_len, -1)
+    def chunk_major(rows):
+        return rows.reshape(groups, chunks, piece, -1).transpose(1, 0, 2, 3).reshape(span_len, -1)
+
+    order = chunk_major(dealt[:, :local_width])
     row_of = (
         jnp.arange(span_len, dtype=jnp.int32).reshape(groups, chunks, piece).transpose(1, 0, 2).reshape(-1)
     )
     rec_count = recomputed.shape[0]
     fresh = jnp.concatenate(
-        [order[:, local_width:], recomputed], axis=0
+        [chunk_major(dealt[:, local_width:]), recomputed], axis=0
     )
     fresh_rank = jnp.concatenate([row_of, jnp.full((rec_count,), -1, jnp.int32)])[None, :]
     fresh_count = span_len + rec_count

time: 196 us -> 198 us (1.010)
  Pallas kernels: 97.9 us -> 93.4 us
  local copies, waits for them, and re-layouts: 16.5 us -> 20 us
    pallas_call x2, Pallas kernels: 51.5 us -> 38.5 us  [exchange(): pl.pallas_call(functools.partial(exchange_step, axis, count), out_shape=j...]
    pallas_call x6, Pallas kernels: 33 us -> 41.5 us  [attend(): pl.pallas_call(flash_step, grid_spec=grid_spec, out_shape=[shape, shape,...]
    all_to_all x2, waiting for transfers between devices: 0.07 us -> 4.62 us  [shards(): lax.all_to_all(partial_value, 'tp', split_axis=0, concat_axis=0, tiled=True)]
    ppermute x1, waiting for transfers between devices: 7.57 us -> 5.17 us  [swapped(): return lax.ppermute(value, axis, pairs)]
    slice x1 -> x2, local copies, waits for them, and re-layouts: 0.08 us -> 2.37 us  [the longest x1 1.29 us: shards(): dealt[:, local_width:]]
  transfers between devices with their start and end apart: 4 -> 4, of which waited for: 3 -> 4; matrix products, arithmetic and copies ran while one was open for 10% -> 12% of each run, Pallas kernels for 30% -> 31%
where the time goes in v14:
time: 198 us; the launch traced here: 197 us
  Pallas kernels  93.4 us (47%)
  waiting for transfers between devices  33.1 us (17%)
  starting transfers between devices  25.7 us (13%)
  local copies, waits for them, and re-layouts  20 us (10%)
  other arithmetic  17.2 us (9%)
  matrix products  6.53 us (3%)
    pallas_call x6, Pallas kernels, attend(): pl.pallas_call(flash_step, grid_spec=grid_spec, out_shape=[shape, shape,...  41.5 us
    pallas_call x2, Pallas kernels, exchange(): pl.pallas_call(functools.partial(exchange_step, axis, count), out_shape=j...  38.5 us
    all_to_all x1, waiting for transfers between devices, shards(): lax.all_to_all(arranged, 'grp', split_axis=0, concat_axis=1, tiled=True)[0]  23.3 us
    pallas_call x2, Pallas kernels, project(): pl.pallas_call(functools.partial(project_step, tuple(turned)), grid=(coun...  13.4 us
    all_to_all x2, starting transfers between devices, shards(): lax.all_to_all(partial_value, 'tp', split_axis=0, concat_axis=0, tiled=True)  12.9 us
    all_to_all x1, starting transfers between devices, shards(): lax.all_to_all(arranged, 'grp', split_axis=0, concat_axis=1, tiled=True)[0]  11.3 us
    dot_general x2, matrix products, shards(): jnp.einsum('qc,ctd->tqd', attended, out_by_block, preferred_element_type=...  6.53 us
    ppermute x1, waiting for transfers between devices, swapped(): return lax.ppermute(value, axis, pairs)  5.17 us
  transfers between devices with their start and end apart: 4, of which 4 were waited for; matrix products, arithmetic and copies ran while one was open for 12% of the time, Pallas kernels for 31%

profile of v14, /device:TPU:1, one launch (start us, length us, event | category | flops | bytes accessed | tf_op | source)
XLA Modules:
  0.0 197.4 jit_solution(16021232982132265469)
XLA Ops:
  3.2 3.7 %fusion.4 = (f32[1024,128]{1,0:T(8,128)}, f32[1024,128]{1,0:T(8,128)}) fusion(f32[128]{0:T(128)} %constant.74.clone.1, f32[128]{0:T(128)S(1)} %pad_maximum_fusion.2, f32[1024]{0:T(1024)S(1)} %convert_element_type.50), kind=kLoop, calls=%fused_computation.15 | loop fusion | flops 262144 | bytes 1053696 | tf_op jit(solution)/shard_map/mul | solution.py:153
  6.9 9.4 %shard_map.118 = bf16[1024,768]{1,0:T(8,128)(2,1)} custom-call(bf16[1024,2048]{1,0:T(8,128)(2,1)} %bitcast.56, f32[1024,128]{1,0:T(8,128)} %get-tuple-element.40.cos_ref, f32[1024,128]{1,0:T(8,128)} %get-tuple-element.39.sin_ref, bf16[2048,256]{1,0:T(8,128)(2,1)} %refs_0_.2, bf16[2048,256]{1,0:T(8,128)(2,1)} %refs_0_.3, bf16[2048,256]{1,0:T(8,128)(2,1)} %refs_1_.3), custom_call_target="tpu_custom_call" | custom-call | tf_op jit(solution)/shard_map/pallas_call | solution.py:160
  16.3 2.1 %gather_fusion = bf16[32,32,768]{2,1,0:T(8,128)(2,1)S(1)} fusion(bf16[32,32,768]{2,1,0:T(8,128)(2,1)} %bitcast.55, s32[1024]{0:T(1024)S(1)} %pad_clamp_fusion.1), kind=kCustom, calls=%fused_computation | custom fusion | bytes 3145856 | tf_op jit(solution)/shard_map/jit(_take)/gather | solution.py:220
  18.3 1.3 broadcast_select_fusion
  19.7 11.3 %all-to-all-start = ((bf16[32,32,768]{2,1,0:T(8,128)(2,1)}), bf16[32,32,768]{2,1,0:T(8,128)(2,1)}, u32[]{:S(2)}, u32[]{:S(2)}) async-start(bf16[32,32,768]{2,1,0:T(8,128)(2,1)} %broadcast_select_fusion), calls=%async_computation | async-start | bytes 3145728 | tf_op jit(solution)/shard_map/all_to_all | solution.py:221
  31.0 1.5 collective-permute-start
  36.7 1.7 scatter_custom_fusion.2
  39.6 4.0 %shard_map.119 = bf16[256,512]{1,0:T(8,128)(2,1)} custom-call(bf16[256,2048]{1,0:T(8,128)(2,1)} %bitcast.61, f32[256,128]{1,0:T(8,128)} %get-tuple-element.42.cos_ref, f32[256,128]{1,0:T(8,128)} %get-tuple-element.41.sin_ref, bf16[2048,256]{1,0:T(8,128)(2,1)} %refs_0_.3, bf16[2048,256]{1,0:T(8,128)(2,1)} %refs_1_.3), custom_call_target="tpu_custom_call" | custom-call | tf_op jit(solution)/shard_map/pallas_call | solution.py:160
  46.0 23.3 %all-to-all-done = bf16[32,32,768]{2,1,0:T(8,128)(2,1)} async-done(((bf16[32,32,768]{2,1,0:T(8,128)(2,1)}), bf16[32,32,768]{2,1,0:T(8,128)(2,1)}, u32[]{:S(2)}, u32[]{:S(2)}) %all-to-all-start) | async-done | bytes 1572896 | tf_op jit(solution)/shard_map/all_to_all | solution.py:221
  76.3 6.1 %shard_map.124 = (f32[512,256]{1,0:T(8,128)}, f32[512,256]{1,0:T(8,128)}, f32[512,256]{1,0:T(8,128)}) custom-call(s32[1]{0:T(128)} %constant.79.clone.1.flags_ref, s32[512,1]{1,0:T(8,128)} %broadcast_in_dim.92.qrow_ref, s32[1,1280]{1,0:T(1,128)} %broadcast_in_dim.87.rank_ref, ...), custom_call_target="tpu_custom_call", output_to_operand_aliasing={{0}: (6, {}), {1}: (7, {}), {2}: (8, {})} | custom-call | tf_op jit(solution)/shard_map/pallas_call | solution.py:63
  82.5 7.3 %shard_map.125 = (f32[512,256]{1,0:T(8,128)}, f32[512,256]{1,0:T(8,128)}, f32[512,256]{1,0:T(8,128)}) custom-call(s32[1]{0:T(128)S(6)} %convert_element_type.51.flags_ref, s32[512,1]{1,0:T(8,128)} %broadcast_in_dim.92.qrow_ref, s32[1,2048]{1,0:T(1,128)} %bitcast.66, ...), custom_call_target="tpu_custom_call", output_to_operand_aliasing={{0}: (6, {}), {1}: (7, {}), {2}: (8, {})} | custom-call | tf_op jit(solution)/shard_map/pallas_call | solution.py:63
  89.8 5.2 %collective-permute-done.k_ref.v_ref = bf16[2,2048,256]{2,1,0:T(8,128)(2,1)S(1)} collective-permute-done((bf16[2,2048,256]{2,1,0:T(8,128)(2,1)}, bf16[2,2048,256]{2,1,0:T(8,128)(2,1)S(1)}, u32[]{:S(2)}, u32[]{:S(2)}) %collective-permute-start) | collective-permute-done | bytes 2097184 | tf_op jit(solution)/shard_map/ppermute | solution.py:181
  96.3 7.4 %shard_map.126 = (f32[512,256]{1,0:T(8,128)}, f32[512,256]{1,0:T(8,128)}, f32[512,256]{1,0:T(8,128)}) custom-call(s32[1]{0:T(128)S(6)} %convert_element_type.48.flags_ref, s32[512,1]{1,0:T(8,128)} %broadcast_in_dim.92.qrow_ref, s32[1,2048]{1,0:T(1,128)} %compare_select_fusion.rank_ref, ...), custom_call_target="tpu_custom_call", output_to_operand_aliasing={{0}: (6, {}), {1}: (7, {}), {2}: (8, {})} | custom-call | tf_op jit(solution)/shard_map/pallas_call | solution.py:63
  103.7 3.3 %convert_bitcast_fusion = bf16[8,512,256]{2,1,0:T(8,128)(2,1)} fusion(bf16[32,8,8,256]{3,2,1,0:T(8,128)(2,1)S(1)} %bitcast.71, f32[512,256]{1,0:T(8,128)} %get-tuple-element.35, f32[512,256]{1,0:T(8,128)} %get-tuple-element.36), kind=kOutput, calls=%fused_computation.5 | convolution fusion | flops 538181632 | bytes 4194304 | tf_op jit(solution)/shard_map/qc,ctd->tqd/dot_general | solution.py:285
  107.0 6.3 %all-to-all-start.2 = ((bf16[8,512,256]{2,1,0:T(8,128)(2,1)}), bf16[8,512,256]{2,1,0:T(8,128)(2,1)S(1)}, u32[]{:S(2)}, u32[]{:S(2)}) async-start(bf16[8,512,256]{2,1,0:T(8,128)(2,1)} %convert_bitcast_fusion), calls=%async_computation.2 | async-start | bytes 4194304 | tf_op jit(solution)/shard_map/all_to_all | solution.py:289
  116.8 6.1 %shard_map.120 = (f32[512,256]{1,0:T(8,128)}, f32[512,256]{1,0:T(8,128)}, f32[512,256]{1,0:T(8,128)}) custom-call(s32[1]{0:T(128)} %constant.79.clone.1.flags_ref, s32[512,1]{1,0:T(8,128)} %broadcast_in_dim.91.qrow_ref, s32[1,1280]{1,0:T(1,128)} %broadcast_in_dim.87.rank_ref, ...), custom_call_target="tpu_custom_call", output_to_operand_aliasing={{0}: (6, {}), {1}: (7, {}), {2}: (8, {})} | custom-call | tf_op jit(solution)/shard_map/pallas_call | solution.py:63
  122.9 7.2 %shard_map.121 = (f32[512,256]{1,0:T(8,128)}, f32[512,256]{1,0:T(8,128)}, f32[512,256]{1,0:T(8,128)}) custom-call(s32[1]{0:T(128)S(6)} %convert_element_type.51.flags_ref, s32[512,1]{1,0:T(8,128)} %broadcast_in_dim.91.qrow_ref, s32[1,2048]{1,0:T(1,128)} %bitcast.67, ...), custom_call_target="tpu_custom_call", output_to_operand_aliasing={{0}: (6, {}), {1}: (7, {}), {2}: (8, {})} | custom-call | tf_op jit(solution)/shard_map/pallas_call | solution.py:63
  130.1 7.2 %shard_map.122 = (f32[512,256]{1,0:T(8,128)}, f32[512,256]{1,0:T(8,128)}, f32[512,256]{1,0:T(8,128)}) custom-call(s32[1]{0:T(128)S(6)} %convert_element_type.48.flags_ref, s32[512,1]{1,0:T(8,128)} %broadcast_in_dim.91.qrow_ref, s32[1,2048]{1,0:T(1,128)} %compare_select_fusion.rank_ref, ...), custom_call_target="tpu_custom_call", output_to_operand_aliasing={{0}: (6, {}), {1}: (7, {}), {2}: (8, {})} | custom-call | tf_op jit(solution)/shard_map/pallas_call | solution.py:63
  137.3 3.3 %convert_bitcast_fusion.1 = bf16[8,512,256]{2,1,0:T(8,128)(2,1)} fusion(bf16[32,8,8,256]{3,2,1,0:T(8,128)(2,1)S(1)} %bitcast.72, f32[512,256]{1,0:T(8,128)} %get-tuple-element.27, f32[512,256]{1,0:T(8,128)} %get-tuple-element.28), kind=kOutput, calls=%fused_computation.6 | convolution fusion | flops 538181632 | bytes 4194304 | tf_op jit(solution)/shard_map/qc,ctd->tqd/dot_general | solution.py:285
  140.7 6.6 %all-to-all-start.1 = ((bf16[8,512,256]{2,1,0:T(8,128)(2,1)}), bf16[8,512,256]{2,1,0:T(8,128)(2,1)}, u32[]{:S(2)}, u32[]{:S(2)}) async-start(bf16[8,512,256]{2,1,0:T(8,128)(2,1)} %convert_bitcast_fusion.1), calls=%async_computation.1 | async-start | bytes 4194304 | tf_op jit(solution)/shard_map/all_to_all | solution.py:289
  149.0 23.0 %shard_map.127 = bf16[32,16,256]{2,1,0:T(8,128)(2,1)} custom-call(bf16[32,16,256]{2,1,0:T(8,128)(2,1)} %bitcast.63), custom_call_target="tpu_custom_call" | custom-call | tf_op jit(solution)/shard_map/pallas_call | solution.py:113
  172.0 4.6 %all-to-all-done.1 = bf16[8,512,256]{2,1,0:T(8,128)(2,1)} async-done(((bf16[8,512,256]{2,1,0:T(8,128)(2,1)}), bf16[8,512,256]{2,1,0:T(8,128)(2,1)}, u32[]{:S(2)}, u32[]{:S(2)}) %all-to-all-start.1) | async-done | bytes 2097184 | tf_op jit(solution)/shard_map/all_to_all | solution.py:289
  176.6 2.6 %reduce_sum.24 = bf16[512,256]{1,0:T(8,128)(2,1)} reduce(bf16[8,512,256]{2,1,0:T(8,128)(2,1)} %all-to-all-done.1, bf16[]{:T(256)} %constant.82.clone.1), dimensions={0}, to_apply=%region_3.4 | reduce | flops 917504 | bytes 2359298 | tf_op jit(solution)/shard_map/reduce_sum | solution.py:292
  179.2 15.5 %shard_map.123 = bf16[32,16,256]{2,1,0:T(8,128)(2,1)} custom-call(bf16[32,16,256]{2,1,0:T(8,128)(2,1)} %bitcast.62), custom_call_target="tpu_custom_call" | custom-call | tf_op jit(solution)/shard_map/pallas_call | solution.py:113
  (63 shorter events, 25.8 us)
Async XLA Ops:
  19.7 12.8 %copy-start.5 = (s32[32]{0:T(128)S(1)}, s32[32]{0:T(128)}, u32[]{:S(2)}) copy-start(s32[32]{0:T(128)} %param.22) | copy-start | bytes 388
  19.7 14.1 %copy-start.6 = (s32[32]{0:T(128)S(1)}, s32[32]{0:T(128)}, u32[]{:S(2)}) copy-start(s32[32]{0:T(128)} %param.21) | copy-start | bytes 388
  19.7 15.4 %copy-start.3 = (s32[1,256]{1,0:T(1,128)S(1)}, s32[1,256]{1,0:T(1,128)}, u32[]{:S(2)}) copy-start(s32[1,256]{1,0:T(1,128)} %param.23) | copy-start | bytes 3076
  19.7 18.6 %copy-start.4 = (f32[128]{0:T(128)S(1)}, f32[128]{0:T(128)}, u32[]{:S(2)}) copy-start(f32[128]{0:T(128)} %constant.74.clone.1) | copy-start | bytes 1540
  19.7 49.6 %all-to-all-start = ((bf16[32,32,768]{2,1,0:T(8,128)(2,1)}), bf16[32,32,768]{2,1,0:T(8,128)(2,1)}, u32[]{:S(2)}, u32[]{:S(2)}) async-start(bf16[32,32,768]{2,1,0:T(8,128)(2,1)} %broadcast_select_fusion), calls=%async_computation | async-start | bytes 3145728 | tf_op jit(solution)/shard_map/all_to_all | solution.py:221
  31.0 64.0 %collective-permute-start = (bf16[2,2048,256]{2,1,0:T(8,128)(2,1)}, bf16[2,2048,256]{2,1,0:T(8,128)(2,1)S(1)}, u32[]{:S(2)}, u32[]{:S(2)}) collective-permute-start(bf16[2,2048,256]{2,1,0:T(8,128)(2,1)} %bitcast.70), channel_id=1, source_target_pairs={{0,128},{8,136},{16,144},{24,152},{32,160},{40,168},{48,176},{56,1... | collective-permute-start | bytes 6291464 | tf_op jit(solution)/shard_map/ppermute | solution.py:181
  71.7 1.0 copy-start.1
  95.0 1.3 copy-start
  96.3 7.4 %copy-start.7 = (bf16[256,2048]{1,0:T(8,128)(2,1)S(1)}, bf16[256,2048]{1,0:T(8,128)(2,1)}, u32[]{:S(2)}) copy-start(bf16[256,2048]{1,0:T(8,128)(2,1)} %param.16) | copy-start | bytes 3145732
  107.0 33.7 %all-to-all-start.2 = ((bf16[8,512,256]{2,1,0:T(8,128)(2,1)}), bf16[8,512,256]{2,1,0:T(8,128)(2,1)S(1)}, u32[]{:S(2)}, u32[]{:S(2)}) async-start(bf16[8,512,256]{2,1,0:T(8,128)(2,1)} %convert_bitcast_fusion), calls=%async_computation.2 | async-start | bytes 4194304 | tf_op jit(solution)/shard_map/all_to_all | solution.py:289
  140.7 35.9 %all-to-all-start.1 = ((bf16[8,512,256]{2,1,0:T(8,128)(2,1)}), bf16[8,512,256]{2,1,0:T(8,128)(2,1)}, u32[]{:S(2)}, u32[]{:S(2)}) async-start(bf16[8,512,256]{2,1,0:T(8,128)(2,1)} %convert_bitcast_fusion.1), calls=%async_computation.1 | async-start | bytes 4194304 | tf_op jit(solution)/shard_map/all_to_all | solution.py:289
  172.0 22.8 %copy-start.2 = (bf16[32,16,256]{2,1,0:T(8,128)(2,1)S(1)}, bf16[32,16,256]{2,1,0:T(8,128)(2,1)}, u32[]{:S(2)}) copy-start(bf16[32,16,256]{2,1,0:T(8,128)(2,1)} %shard_map.127) | copy-start | bytes 786436

commit v15 on v12

--- a/solution.py
+++ b/solution.py
@@ -258,13 +258,16 @@
     chunks = 2
     piece = local_rows // chunks
     chunk_len = span_len // chunks
-    order = dealt.reshape(groups, chunks, piece, -1).transpose(1, 0, 2, 3).reshape(span_len, -1)
+    def chunk_major(rows):
+        return rows.reshape(groups, chunks, piece, -1).transpose(1, 0, 2, 3).reshape(span_len, -1)
+
+    order = chunk_major(dealt[:, :local_width])
     row_of = (
         jnp.arange(span_len, dtype=jnp.int32).reshape(groups, chunks, piece).transpose(1, 0, 2).reshape(-1)
     )
     rec_count = recomputed.shape[0]
     fresh = jnp.concatenate(
-        [order[:, local_width:], recomputed], axis=0
+        [chunk_major(dealt[:, local_width:]), recomputed], axis=0
     )
     fresh_rank = jnp.concatenate([row_of, jnp.full((rec_count,), -1, jnp.int32)])[None, :]
     fresh_count = span_len + rec_count

time: 195 us -> 196 us (level)
  local copies, waits for them, and re-layouts: 14.5 us -> 18.5 us
  waiting for transfers between devices: 31.7 us -> 28.6 us
    ppermute x1, waiting for transfers between devices: 7.9 us -> 5.15 us  [swapped(): return lax.ppermute(value, axis, pairs)]
    slice x1 -> x2, local copies, waits for them, and re-layouts: 0.08 us -> 2.37 us  [the longest x1 1.29 us: shards(): dealt[:, local_width:]]
    another operation x7 -> x6, local copies, waits for them, and re-layouts: 5.09 us -> 5.07 us
  transfers between devices with their start and end apart: 4 -> 4, of which waited for: 3 -> 2; matrix products, arithmetic and copies ran while one was open for 10% -> 12% of each run, Pallas kernels for 35% -> 31%
where the time goes in v15:
time: 196 us; the launch traced here: 195 us
  Pallas kernels  99.4 us (51%)
  waiting for transfers between devices  28.6 us (15%)
  starting transfers between devices  25.7 us (13%)
  local copies, waits for them, and re-layouts  18.5 us (9%)
  other arithmetic  15.2 us (8%)
  matrix products  6.52 us (3%)
    pallas_call x2, Pallas kernels, exchange(): pl.pallas_call(functools.partial(exchange_step, axis, count), out_shape=j...  51.7 us
    pallas_call x6, Pallas kernels, attend(): pl.pallas_call(flash_step, grid_spec=grid_spec, out_shape=[shape, shape,...  33.2 us
    all_to_all x1, waiting for transfers between devices, shards(): lax.all_to_all(arranged, 'grp', split_axis=0, concat_axis=1, tiled=True)[0]  23.4 us
    pallas_call x2, Pallas kernels, project(): pl.pallas_call(functools.partial(project_step, tuple(turned), placed), gr...  14.5 us
    all_to_all x2, starting transfers between devices, shards(): lax.all_to_all(partial_value, 'tp', split_axis=0, concat_axis=0, tiled=True)  13 us
    all_to_all x1, starting transfers between devices, shards(): lax.all_to_all(arranged, 'grp', split_axis=0, concat_axis=1, tiled=True)[0]  11.3 us
    dot_general x2, matrix products, shards(): jnp.einsum('qc,ctd->tqd', attended, out_by_block, preferred_element_type=...  6.52 us
    ppermute x1, waiting for transfers between devices, swapped(): return lax.ppermute(value, axis, pairs)  5.15 us
  transfers between devices with their start and end apart: 4, of which 2 were waited for; matrix products, arithmetic and copies ran while one was open for 12% of the time, Pallas kernels for 31%

profile of v15, /device:TPU:1, one launch (start us, length us, event | category | flops | bytes accessed | tf_op | source)
XLA Modules:
  0.0 195.3 jit_solution(5686410167810812260)
XLA Ops:
  3.7 3.7 %fusion.4 = (f32[1024,128]{1,0:T(8,128)}, f32[1024,128]{1,0:T(8,128)}) fusion(f32[128]{0:T(128)} %constant.62.clone.1, f32[128]{0:T(128)S(1)} %pad_maximum_fusion.2, f32[1024]{0:T(1024)S(1)} %convert_element_type.50), kind=kLoop, calls=%fused_computation.13 | loop fusion | flops 262144 | bytes 1053696 | tf_op jit(solution)/shard_map/mul | solution.py:164
  7.4 10.5 %shard_map.118 = bf16[32,32,768]{2,1,0:T(8,128)(2,1)} custom-call(s32[32]{0:T(128)} %scatter_custom_fusion.refs_0_, bf16[1024,2048]{1,0:T(8,128)(2,1)} %bitcast.54, f32[1024,128]{1,0:T(8,128)} %get-tuple-element.40.refs_2_, f32[1024,128]{1,0:T(8,128)} %get-tuple-element.39.refs_3_, bf16[2048,256]{1,0:T(8,128)(2,1)} %refs_4_.2, bf16[2048,256]{1,0:T(8,128)(2,1)} %refs_3_.1, ...), custom_call_target="tpu_custom_call" | custom-call | tf_op jit(solution)/shard_map/pallas_call | solution.py:196
  17.9 11.3 %all-to-all-start = ((bf16[32,32,768]{2,1,0:T(8,128)(2,1)}), bf16[32,32,768]{2,1,0:T(8,128)(2,1)}, u32[]{:S(2)}, u32[]{:S(2)}) async-start(bf16[32,32,768]{2,1,0:T(8,128)(2,1)} %shard_map.118), calls=%async_computation | async-start | bytes 3145728 | tf_op jit(solution)/shard_map/all_to_all | solution.py:248
  29.2 1.5 collective-permute-start
  34.8 1.7 scatter_custom_fusion.2
  36.5 1.2 fusion.7
  37.7 3.9 %shard_map.119 = bf16[256,512]{1,0:T(8,128)(2,1)} custom-call(bf16[256,2048]{1,0:T(8,128)(2,1)} %bitcast.59, f32[256,128]{1,0:T(8,128)} %get-tuple-element.42.refs_1_, f32[256,128]{1,0:T(8,128)} %get-tuple-element.41.refs_2_, bf16[2048,256]{1,0:T(8,128)(2,1)} %refs_3_.1, bf16[2048,256]{1,0:T(8,128)(2,1)} %refs_4_.3), custom_call_target="tpu_custom_call" | custom-call | tf_op jit(solution)/shard_map/pallas_call | solution.py:196
  44.1 23.4 %all-to-all-done = bf16[32,32,768]{2,1,0:T(8,128)(2,1)} async-done(((bf16[32,32,768]{2,1,0:T(8,128)(2,1)}), bf16[32,32,768]{2,1,0:T(8,128)(2,1)}, u32[]{:S(2)}, u32[]{:S(2)}) %all-to-all-start) | async-done | bytes 1572896 | tf_op jit(solution)/shard_map/all_to_all | solution.py:248
  68.6 1.3 slice.40
  74.6 6.1 %shard_map.124 = (f32[512,256]{1,0:T(8,128)}, f32[512,256]{1,0:T(8,128)}, f32[512,256]{1,0:T(8,128)}) custom-call(s32[1]{0:T(128)} %constant.66.clone.1.flags_ref, s32[512,1]{1,0:T(8,128)} %broadcast_in_dim.80.qrow_ref, s32[1,1280]{1,0:T(1,128)} %broadcast_in_dim.75.rank_ref, ...), custom_call_target="tpu_custom_call", output_to_operand_aliasing={{0}: (6, {}), {1}: (7, {}), {2}: (8, {})} | custom-call | tf_op jit(solution)/shard_map/pallas_call | solution.py:63
  80.7 7.3 %shard_map.125 = (f32[512,256]{1,0:T(8,128)}, f32[512,256]{1,0:T(8,128)}, f32[512,256]{1,0:T(8,128)}) custom-call(s32[1]{0:T(128)S(6)} %convert_element_type.51.flags_ref, s32[512,1]{1,0:T(8,128)} %broadcast_in_dim.80.qrow_ref, s32[1,2048]{1,0:T(1,128)} %bitcast.64, ...), custom_call_target="tpu_custom_call", output_to_operand_aliasing={{0}: (6, {}), {1}: (7, {}), {2}: (8, {})} | custom-call | tf_op jit(solution)/shard_map/pallas_call | solution.py:63
  88.0 5.2 %collective-permute-done.k_ref.v_ref = bf16[2,2048,256]{2,1,0:T(8,128)(2,1)S(1)} collective-permute-done((bf16[2,2048,256]{2,1,0:T(8,128)(2,1)}, bf16[2,2048,256]{2,1,0:T(8,128)(2,1)S(1)}, u32[]{:S(2)}, u32[]{:S(2)}) %collective-permute-start) | collective-permute-done | bytes 2097184 | tf_op jit(solution)/shard_map/ppermute | solution.py:209
  93.2 1.3 copy-done
  94.5 3.2 %shard_map.126 = (f32[512,256]{1,0:T(8,128)}, f32[512,256]{1,0:T(8,128)}, f32[512,256]{1,0:T(8,128)}) custom-call(s32[1]{0:T(128)S(6)} %convert_element_type.48.flags_ref, s32[512,1]{1,0:T(8,128)} %broadcast_in_dim.80.qrow_ref, s32[1,2048]{1,0:T(1,128)} %compare_select_fusion.rank_ref, ...), custom_call_target="tpu_custom_call", output_to_operand_aliasing={{0}: (6, {}), {1}: (7, {}), {2}: (8, {})} | custom-call | tf_op jit(solution)/shard_map/pallas_call | solution.py:63
  97.8 3.3 %convert_bitcast_fusion = bf16[8,512,256]{2,1,0:T(8,128)(2,1)} fusion(bf16[32,8,8,256]{3,2,1,0:T(8,128)(2,1)S(1)} %bitcast.69, f32[512,256]{1,0:T(8,128)} %get-tuple-element.35, f32[512,256]{1,0:T(8,128)} %get-tuple-element.36), kind=kOutput, calls=%fused_computation.4 | convolution fusion | flops 538181632 | bytes 4194304 | tf_op jit(solution)/shard_map/qc,ctd->tqd/dot_general | solution.py:312
  101.0 6.3 %all-to-all-start.2 = ((bf16[8,512,256]{2,1,0:T(8,128)(2,1)}), bf16[8,512,256]{2,1,0:T(8,128)(2,1)S(1)}, u32[]{:S(2)}, u32[]{:S(2)}) async-start(bf16[8,512,256]{2,1,0:T(8,128)(2,1)} %convert_bitcast_fusion), calls=%async_computation.2 | async-start | bytes 4194304 | tf_op jit(solution)/shard_map/all_to_all | solution.py:316
  110.8 6.1 %shard_map.120 = (f32[512,256]{1,0:T(8,128)}, f32[512,256]{1,0:T(8,128)}, f32[512,256]{1,0:T(8,128)}) custom-call(s32[1]{0:T(128)} %constant.66.clone.1.flags_ref, s32[512,1]{1,0:T(8,128)} %broadcast_in_dim.79.qrow_ref, s32[1,1280]{1,0:T(1,128)} %broadcast_in_dim.75.rank_ref, ...), custom_call_target="tpu_custom_call", output_to_operand_aliasing={{0}: (6, {}), {1}: (7, {}), {2}: (8, {})} | custom-call | tf_op jit(solution)/shard_map/pallas_call | solution.py:63
  116.9 7.3 %shard_map.121 = (f32[512,256]{1,0:T(8,128)}, f32[512,256]{1,0:T(8,128)}, f32[512,256]{1,0:T(8,128)}) custom-call(s32[1]{0:T(128)S(6)} %convert_element_type.51.flags_ref, s32[512,1]{1,0:T(8,128)} %broadcast_in_dim.79.qrow_ref, s32[1,2048]{1,0:T(1,128)} %bitcast.65, ...), custom_call_target="tpu_custom_call", output_to_operand_aliasing={{0}: (6, {}), {1}: (7, {}), {2}: (8, {})} | custom-call | tf_op jit(solution)/shard_map/pallas_call | solution.py:63
  124.1 3.1 %shard_map.122 = (f32[512,256]{1,0:T(8,128)}, f32[512,256]{1,0:T(8,128)}, f32[512,256]{1,0:T(8,128)}) custom-call(s32[1]{0:T(128)S(6)} %convert_element_type.48.flags_ref, s32[512,1]{1,0:T(8,128)} %broadcast_in_dim.79.qrow_ref, s32[1,2048]{1,0:T(1,128)} %compare_select_fusion.rank_ref, ...), custom_call_target="tpu_custom_call", output_to_operand_aliasing={{0}: (6, {}), {1}: (7, {}), {2}: (8, {})} | custom-call | tf_op jit(solution)/shard_map/pallas_call | solution.py:63
  127.3 3.3 %convert_bitcast_fusion.1 = bf16[8,512,256]{2,1,0:T(8,128)(2,1)} fusion(bf16[32,8,8,256]{3,2,1,0:T(8,128)(2,1)S(1)} %bitcast.70, f32[512,256]{1,0:T(8,128)} %get-tuple-element.27, f32[512,256]{1,0:T(8,128)} %get-tuple-element.28), kind=kOutput, calls=%fused_computation.5 | convolution fusion | flops 538181632 | bytes 4194304 | tf_op jit(solution)/shard_map/qc,ctd->tqd/dot_general | solution.py:312
  130.6 6.6 %all-to-all-start.1 = ((bf16[8,512,256]{2,1,0:T(8,128)(2,1)}), bf16[8,512,256]{2,1,0:T(8,128)(2,1)}, u32[]{:S(2)}, u32[]{:S(2)}) async-start(bf16[8,512,256]{2,1,0:T(8,128)(2,1)} %convert_bitcast_fusion.1), calls=%async_computation.1 | async-start | bytes 4194304 | tf_op jit(solution)/shard_map/all_to_all | solution.py:316
  138.3 26.0 %shard_map.127 = bf16[32,16,256]{2,1,0:T(8,128)(2,1)} custom-call(bf16[32,16,256]{2,1,0:T(8,128)(2,1)} %bitcast.61), custom_call_target="tpu_custom_call" | custom-call | tf_op jit(solution)/shard_map/pallas_call | solution.py:113
  164.3 2.7 %reduce_sum.24 = bf16[512,256]{1,0:T(8,128)(2,1)} reduce(bf16[8,512,256]{2,1,0:T(8,128)(2,1)} %all-to-all-done.1, bf16[]{:T(256)} %constant.69.clone.1), dimensions={0}, to_apply=%region_3.4 | reduce | flops 917504 | bytes 2359298 | tf_op jit(solution)/shard_map/reduce_sum | solution.py:319
  167.0 25.7 %shard_map.123 = bf16[32,16,256]{2,1,0:T(8,128)(2,1)} custom-call(bf16[32,16,256]{2,1,0:T(8,128)(2,1)} %bitcast.60), custom_call_target="tpu_custom_call" | custom-call | tf_op jit(solution)/shard_map/pallas_call | solution.py:113
  (61 shorter events, 21.7 us)
Async XLA Ops:
  17.9 12.8 %copy-start.5 = (s32[32]{0:T(128)S(1)}, s32[32]{0:T(128)}, u32[]{:S(2)}) copy-start(s32[32]{0:T(128)} %param.22) | copy-start | bytes 388
  17.9 14.0 %copy-start.7 = (s32[32]{0:T(128)S(1)}, s32[32]{0:T(128)}, u32[]{:S(2)}) copy-start(s32[32]{0:T(128)} %param.21) | copy-start | bytes 388
  17.9 15.3 %copy-start.3 = (s32[1,256]{1,0:T(1,128)S(1)}, s32[1,256]{1,0:T(1,128)}, u32[]{:S(2)}) copy-start(s32[1,256]{1,0:T(1,128)} %param.23) | copy-start | bytes 3076
  17.9 18.6 %copy-start.4 = (f32[128]{0:T(128)S(1)}, f32[128]{0:T(128)}, u32[]{:S(2)}) copy-start(f32[128]{0:T(128)} %constant.62.clone.1) | copy-start | bytes 1540
  17.9 49.6 %all-to-all-start = ((bf16[32,32,768]{2,1,0:T(8,128)(2,1)}), bf16[32,32,768]{2,1,0:T(8,128)(2,1)}, u32[]{:S(2)}, u32[]{:S(2)}) async-start(bf16[32,32,768]{2,1,0:T(8,128)(2,1)} %shard_map.118), calls=%async_computation | async-start | bytes 3145728 | tf_op jit(solution)/shard_map/all_to_all | solution.py:248
  29.2 64.0 %collective-permute-start = (bf16[2,2048,256]{2,1,0:T(8,128)(2,1)}, bf16[2,2048,256]{2,1,0:T(8,128)(2,1)S(1)}, u32[]{:S(2)}, u32[]{:S(2)}) collective-permute-start(bf16[2,2048,256]{2,1,0:T(8,128)(2,1)} %bitcast.68), channel_id=1, source_target_pairs={{0,128},{8,136},{16,144},{24,152},{32,160},{40,168},{48,176},{56,1... | collective-permute-start | bytes 6291464 | tf_op jit(solution)/shard_map/ppermute | solution.py:209
  69.9 1.0 copy-start.1
  93.2 1.3 copy-start
  94.5 3.2 %copy-start.8 = (bf16[256,2048]{1,0:T(8,128)(2,1)S(1)}, bf16[256,2048]{1,0:T(8,128)(2,1)}, u32[]{:S(2)}) copy-start(bf16[256,2048]{1,0:T(8,128)(2,1)} %param.16) | copy-start | bytes 3145732
  101.0 29.5 %all-to-all-start.2 = ((bf16[8,512,256]{2,1,0:T(8,128)(2,1)}), bf16[8,512,256]{2,1,0:T(8,128)(2,1)S(1)}, u32[]{:S(2)}, u32[]{:S(2)}) async-start(bf16[8,512,256]{2,1,0:T(8,128)(2,1)} %convert_bitcast_fusion), calls=%async_computation.2 | async-start | bytes 4194304 | tf_op jit(solution)/shard_map/all_to_all | solution.py:316
  130.5 6.6 %copy-start.6 = (s32[32]{0:T(128)S(1)}, s32[32]{0:T(128)}, u32[]{:S(2)}) copy-start(s32[32]{0:T(128)} %scatter_custom_fusion.refs_0_) | copy-start | bytes 388
  130.6 33.8 %all-to-all-start.1 = ((bf16[8,512,256]{2,1,0:T(8,128)(2,1)}), bf16[8,512,256]{2,1,0:T(8,128)(2,1)}, u32[]{:S(2)}, u32[]{:S(2)}) async-start(bf16[8,512,256]{2,1,0:T(8,128)(2,1)} %convert_bitcast_fusion.1), calls=%async_computation.1 | async-start | bytes 4194304 | tf_op jit(solution)/shard_map/all_to_all | solution.py:316
  164.3 28.4 %copy-start.2 = (bf16[32,16,256]{2,1,0:T(8,128)(2,1)S(1)}, bf16[32,16,256]{2,1,0:T(8,128)(2,1)}, u32[]{:S(2)}) copy-start(bf16[32,16,256]{2,1,0:T(8,128)(2,1)} %shard_map.127) | copy-start | bytes 786436

commit v16 on v11

--- a/solution.py
+++ b/solution.py
@@ -215,7 +215,7 @@
 
     projected = project(
         tokens.reshape(-1, model_width), local_positions, [w_query, w_key, w_value],
-        [True, True, False], 256,
+        [True, True, False], 512,
     ).reshape(requests, local_rows, -1)
     arranged = jnp.take(projected, deal_order, axis=0)
     dealt = lax.all_to_all(arranged, "grp", split_axis=0, concat_axis=1, tiled=True)[0]

time: 196 us -> 196 us (level)
  no operation moved by 1% of the time
where the time goes in v16:
time: 196 us
  Pallas kernels  97.4 us (50%)
  waiting for transfers between devices  31.2 us (16%)
  starting transfers between devices  25.6 us (13%)
  other arithmetic  17.1 us (9%)
  local copies, waits for them, and re-layouts  16.5 us (8%)
  matrix products  6.54 us (3%)
    pallas_call x2, Pallas kernels, exchange(): pl.pallas_call(functools.partial(exchange_step, axis, count), out_shape=j...  51.1 us
    pallas_call x6, Pallas kernels, attend(): pl.pallas_call(flash_step, grid_spec=grid_spec, out_shape=[shape, shape,...  33 us
    all_to_all x1, waiting for transfers between devices, shards(): lax.all_to_all(arranged, 'grp', split_axis=0, concat_axis=1, tiled=True)[0]  23.6 us
    pallas_call x2, Pallas kernels, project(): pl.pallas_call(functools.partial(project_step, tuple(turned)), grid=(coun...  13.4 us
    all_to_all x2, starting transfers between devices, shards(): lax.all_to_all(partial_value, 'tp', split_axis=0, concat_axis=0, tiled=True)  12.9 us
    all_to_all x1, starting transfers between devices, shards(): lax.all_to_all(arranged, 'grp', split_axis=0, concat_axis=1, tiled=True)[0]  11.2 us
    ppermute x1, waiting for transfers between devices, swapped(): return lax.ppermute(value, axis, pairs)  7.57 us
    dot_general x2, matrix products, shards(): jnp.einsum('qc,ctd->tqd', attended, out_by_block, preferred_element_type=...  6.54 us
  transfers between devices with their start and end apart: 4, of which 3 were waited for; matrix products, arithmetic and copies ran while one was open for 10% of the time, Pallas kernels for 30%

profile of v16, /device:TPU:1, one launch (start us, length us, event | category | flops | bytes accessed | tf_op | source)
XLA Modules:
  0.0 195.8 jit_solution(8115723737521526870)
XLA Ops:
  3.2 3.7 %fusion.4 = (f32[1024,128]{1,0:T(8,128)}, f32[1024,128]{1,0:T(8,128)}) fusion(f32[128]{0:T(128)} %constant.74.clone.1, f32[128]{0:T(128)S(1)} %pad_maximum_fusion.2, f32[1024]{0:T(1024)S(1)} %convert_element_type.50), kind=kLoop, calls=%fused_computation.15 | loop fusion | flops 262144 | bytes 1053696 | tf_op jit(solution)/shard_map/mul | solution.py:153
  6.9 9.4 %shard_map.118 = bf16[1024,768]{1,0:T(8,128)(2,1)} custom-call(bf16[1024,2048]{1,0:T(8,128)(2,1)} %bitcast.53, f32[1024,128]{1,0:T(8,128)} %get-tuple-element.40.cos_ref, f32[1024,128]{1,0:T(8,128)} %get-tuple-element.39.sin_ref, bf16[2048,256]{1,0:T(8,128)(2,1)} %refs_0_.2, bf16[2048,256]{1,0:T(8,128)(2,1)} %refs_0_.3, bf16[2048,256]{1,0:T(8,128)(2,1)} %refs_1_.3), custom_call_target="tpu_custom_call" | custom-call | tf_op jit(solution)/shard_map/pallas_call | solution.py:160
  16.3 2.1 %gather_fusion = bf16[32,32,768]{2,1,0:T(8,128)(2,1)S(1)} fusion(bf16[32,32,768]{2,1,0:T(8,128)(2,1)} %bitcast.52, s32[1024]{0:T(1024)S(1)} %pad_clamp_fusion.1), kind=kCustom, calls=%fused_computation | custom fusion | bytes 3145856 | tf_op jit(solution)/shard_map/jit(_take)/gather | solution.py:220
  18.3 1.4 broadcast_select_fusion
  19.7 11.2 %all-to-all-start = ((bf16[32,32,768]{2,1,0:T(8,128)(2,1)}), bf16[32,32,768]{2,1,0:T(8,128)(2,1)S(1)}, u32[]{:S(2)}, u32[]{:S(2)}) async-start(bf16[32,32,768]{2,1,0:T(8,128)(2,1)} %broadcast_select_fusion), calls=%async_computation | async-start | bytes 3145728 | tf_op jit(solution)/shard_map/all_to_all | solution.py:221
  30.9 1.5 collective-permute-start
  36.4 1.7 scatter_custom_fusion.2
  39.3 4.0 %shard_map.119 = bf16[256,512]{1,0:T(8,128)(2,1)} custom-call(bf16[256,2048]{1,0:T(8,128)(2,1)} %bitcast.55, f32[256,128]{1,0:T(8,128)} %get-tuple-element.42.cos_ref, f32[256,128]{1,0:T(8,128)} %get-tuple-element.41.sin_ref, bf16[2048,256]{1,0:T(8,128)(2,1)} %refs_0_.3, bf16[2048,256]{1,0:T(8,128)(2,1)} %refs_1_.3), custom_call_target="tpu_custom_call" | custom-call | tf_op jit(solution)/shard_map/pallas_call | solution.py:160
  43.3 1.2 compare_select_fusion.rank_ref
  45.6 23.6 %all-to-all-done = bf16[32,32,768]{2,1,0:T(8,128)(2,1)S(1)} async-done(((bf16[32,32,768]{2,1,0:T(8,128)(2,1)}), bf16[32,32,768]{2,1,0:T(8,128)(2,1)S(1)}, u32[]{:S(2)}, u32[]{:S(2)}) %all-to-all-start) | async-done | bytes 1572896 | tf_op jit(solution)/shard_map/all_to_all | solution.py:221
  74.2 6.1 %shard_map.124 = (f32[512,256]{1,0:T(8,128)}, f32[512,256]{1,0:T(8,128)}, f32[512,256]{1,0:T(8,128)}) custom-call(s32[1]{0:T(128)} %constant.79.clone.1.flags_ref, s32[512,1]{1,0:T(8,128)} %broadcast_in_dim.92.qrow_ref, s32[1,1280]{1,0:T(1,128)} %broadcast_in_dim.87.rank_ref, ...), custom_call_target="tpu_custom_call", output_to_operand_aliasing={{0}: (6, {}), {1}: (7, {}), {2}: (8, {})} | custom-call | tf_op jit(solution)/shard_map/pallas_call | solution.py:63
  80.3 7.2 %shard_map.125 = (f32[512,256]{1,0:T(8,128)}, f32[512,256]{1,0:T(8,128)}, f32[512,256]{1,0:T(8,128)}) custom-call(s32[1]{0:T(128)S(6)} %convert_element_type.51.flags_ref, s32[512,1]{1,0:T(8,128)} %broadcast_in_dim.92.qrow_ref, s32[1,2048]{1,0:T(1,128)} %bitcast.60, ...), custom_call_target="tpu_custom_call", output_to_operand_aliasing={{0}: (6, {}), {1}: (7, {}), {2}: (8, {})} | custom-call | tf_op jit(solution)/shard_map/pallas_call | solution.py:63
  87.5 7.6 %collective-permute-done.k_ref.v_ref = bf16[2,2048,256]{2,1,0:T(8,128)(2,1)} collective-permute-done((bf16[2,2048,256]{2,1,0:T(8,128)(2,1)}, bf16[2,2048,256]{2,1,0:T(8,128)(2,1)}, u32[]{:S(2)}, u32[]{:S(2)}) %collective-permute-start) | collective-permute-done | bytes 2097184 | tf_op jit(solution)/shard_map/ppermute | solution.py:181
  95.1 3.2 %shard_map.126 = (f32[512,256]{1,0:T(8,128)}, f32[512,256]{1,0:T(8,128)}, f32[512,256]{1,0:T(8,128)}) custom-call(s32[1]{0:T(128)S(6)} %convert_element_type.48.flags_ref, s32[512,1]{1,0:T(8,128)} %broadcast_in_dim.92.qrow_ref, s32[1,2048]{1,0:T(1,128)} %compare_select_fusion.rank_ref, ...), custom_call_target="tpu_custom_call", output_to_operand_aliasing={{0}: (6, {}), {1}: (7, {}), {2}: (8, {})} | custom-call | tf_op jit(solution)/shard_map/pallas_call | solution.py:63
  98.3 3.3 %convert_bitcast_fusion = bf16[8,512,256]{2,1,0:T(8,128)(2,1)} fusion(bf16[32,8,8,256]{3,2,1,0:T(8,128)(2,1)S(1)} %bitcast.65, f32[512,256]{1,0:T(8,128)} %get-tuple-element.35, f32[512,256]{1,0:T(8,128)} %get-tuple-element.36), kind=kOutput, calls=%fused_computation.5 | convolution fusion | flops 538181632 | bytes 4194304 | tf_op jit(solution)/shard_map/qc,ctd->tqd/dot_general | solution.py:282
  101.6 6.4 %all-to-all-start.2 = ((bf16[8,512,256]{2,1,0:T(8,128)(2,1)}), bf16[8,512,256]{2,1,0:T(8,128)(2,1)S(1)}, u32[]{:S(2)}, u32[]{:S(2)}) async-start(bf16[8,512,256]{2,1,0:T(8,128)(2,1)} %convert_bitcast_fusion), calls=%async_computation.2 | async-start | bytes 4194304 | tf_op jit(solution)/shard_map/all_to_all | solution.py:286
  111.3 6.1 %shard_map.120 = (f32[512,256]{1,0:T(8,128)}, f32[512,256]{1,0:T(8,128)}, f32[512,256]{1,0:T(8,128)}) custom-call(s32[1]{0:T(128)} %constant.79.clone.1.flags_ref, s32[512,1]{1,0:T(8,128)} %broadcast_in_dim.91.qrow_ref, s32[1,1280]{1,0:T(1,128)} %broadcast_in_dim.87.rank_ref, ...), custom_call_target="tpu_custom_call", output_to_operand_aliasing={{0}: (6, {}), {1}: (7, {}), {2}: (8, {})} | custom-call | tf_op jit(solution)/shard_map/pallas_call | solution.py:63
  117.4 7.3 %shard_map.121 = (f32[512,256]{1,0:T(8,128)}, f32[512,256]{1,0:T(8,128)}, f32[512,256]{1,0:T(8,128)}) custom-call(s32[1]{0:T(128)S(6)} %convert_element_type.51.flags_ref, s32[512,1]{1,0:T(8,128)} %broadcast_in_dim.91.qrow_ref, s32[1,2048]{1,0:T(1,128)} %bitcast.61, ...), custom_call_target="tpu_custom_call", output_to_operand_aliasing={{0}: (6, {}), {1}: (7, {}), {2}: (8, {})} | custom-call | tf_op jit(solution)/shard_map/pallas_call | solution.py:63
  124.7 3.1 %shard_map.122 = (f32[512,256]{1,0:T(8,128)}, f32[512,256]{1,0:T(8,128)}, f32[512,256]{1,0:T(8,128)}) custom-call(s32[1]{0:T(128)S(6)} %convert_element_type.48.flags_ref, s32[512,1]{1,0:T(8,128)} %broadcast_in_dim.91.qrow_ref, s32[1,2048]{1,0:T(1,128)} %compare_select_fusion.rank_ref, ...), custom_call_target="tpu_custom_call", output_to_operand_aliasing={{0}: (6, {}), {1}: (7, {}), {2}: (8, {})} | custom-call | tf_op jit(solution)/shard_map/pallas_call | solution.py:63
  127.8 3.3 %convert_bitcast_fusion.1 = bf16[8,512,256]{2,1,0:T(8,128)(2,1)} fusion(bf16[32,8,8,256]{3,2,1,0:T(8,128)(2,1)S(1)} %bitcast.66, f32[512,256]{1,0:T(8,128)} %get-tuple-element.27, f32[512,256]{1,0:T(8,128)} %get-tuple-element.28), kind=kOutput, calls=%fused_computation.6 | convolution fusion | flops 538181632 | bytes 4194304 | tf_op jit(solution)/shard_map/qc,ctd->tqd/dot_general | solution.py:282
  131.1 6.6 %all-to-all-start.1 = ((bf16[8,512,256]{2,1,0:T(8,128)(2,1)}), bf16[8,512,256]{2,1,0:T(8,128)(2,1)}, u32[]{:S(2)}, u32[]{:S(2)}) async-start(bf16[8,512,256]{2,1,0:T(8,128)(2,1)} %convert_bitcast_fusion.1), calls=%async_computation.1 | async-start | bytes 4194304 | tf_op jit(solution)/shard_map/all_to_all | solution.py:286
  139.5 25.4 %shard_map.127 = bf16[32,16,256]{2,1,0:T(8,128)(2,1)} custom-call(bf16[32,16,256]{2,1,0:T(8,128)(2,1)} %bitcast.57), custom_call_target="tpu_custom_call" | custom-call | tf_op jit(solution)/shard_map/pallas_call | solution.py:113
  164.9 2.7 %reduce_sum.24 = bf16[512,256]{1,0:T(8,128)(2,1)} reduce(bf16[8,512,256]{2,1,0:T(8,128)(2,1)} %all-to-all-done.1, bf16[]{:T(256)} %constant.82.clone.1), dimensions={0}, to_apply=%region_3.4 | reduce | flops 917504 | bytes 2359298 | tf_op jit(solution)/shard_map/reduce_sum | solution.py:289
  167.6 25.7 %shard_map.123 = bf16[32,16,256]{2,1,0:T(8,128)(2,1)} custom-call(bf16[32,16,256]{2,1,0:T(8,128)(2,1)} %bitcast.56), custom_call_target="tpu_custom_call" | custom-call | tf_op jit(solution)/shard_map/pallas_call | solution.py:113
  (61 shorter events, 21.0 us)
Async XLA Ops:
  19.7 12.7 %copy-start.5 = (s32[32]{0:T(128)S(1)}, s32[32]{0:T(128)}, u32[]{:S(2)}) copy-start(s32[32]{0:T(128)} %param.22) | copy-start | bytes 388
  19.7 13.9 %copy-start.6 = (s32[32]{0:T(128)S(1)}, s32[32]{0:T(128)}, u32[]{:S(2)}) copy-start(s32[32]{0:T(128)} %param.21) | copy-start | bytes 388
  19.7 15.1 %copy-start.3 = (s32[1,256]{1,0:T(1,128)S(1)}, s32[1,256]{1,0:T(1,128)}, u32[]{:S(2)}) copy-start(s32[1,256]{1,0:T(1,128)} %param.23) | copy-start | bytes 3076
  19.7 18.4 %copy-start.4 = (f32[128]{0:T(128)S(1)}, f32[128]{0:T(128)}, u32[]{:S(2)}) copy-start(f32[128]{0:T(128)} %constant.74.clone.1) | copy-start | bytes 1540
  19.7 49.5 %all-to-all-start = ((bf16[32,32,768]{2,1,0:T(8,128)(2,1)}), bf16[32,32,768]{2,1,0:T(8,128)(2,1)S(1)}, u32[]{:S(2)}, u32[]{:S(2)}) async-start(bf16[32,32,768]{2,1,0:T(8,128)(2,1)} %broadcast_select_fusion), calls=%async_computation | async-start | bytes 3145728 | tf_op jit(solution)/shard_map/all_to_all | solution.py:221
  30.9 64.2 %collective-permute-start = (bf16[2,2048,256]{2,1,0:T(8,128)(2,1)}, bf16[2,2048,256]{2,1,0:T(8,128)(2,1)}, u32[]{:S(2)}, u32[]{:S(2)}) collective-permute-start(bf16[2,2048,256]{2,1,0:T(8,128)(2,1)} %bitcast.64), channel_id=1, source_target_pairs={{0,128},{8,136},{16,144},{24,152},{32,160},{40,168},{48,176},{56,1... | collective-permute-start | bytes 6291464 | tf_op jit(solution)/shard_map/ppermute | solution.py:181
  69.4 2.3 %copy-start = (bf16[2,32,16,768]{3,2,1,0:T(8,128)(2,1)}, bf16[2,32,16,768]{3,2,1,0:T(8,128)(2,1)S(1)}, u32[]{:S(2)}) copy-start(bf16[2,32,16,768]{3,2,1,0:T(8,128)(2,1)S(1)} %copy.33) | copy-start | bytes 4718596
  69.4 1.1 copy-start.1
  95.1 3.2 %copy-start.7 = (bf16[256,2048]{1,0:T(8,128)(2,1)S(1)}, bf16[256,2048]{1,0:T(8,128)(2,1)}, u32[]{:S(2)}) copy-start(bf16[256,2048]{1,0:T(8,128)(2,1)} %param.16) | copy-start | bytes 3145732
  101.6 29.6 %all-to-all-start.2 = ((bf16[8,512,256]{2,1,0:T(8,128)(2,1)}), bf16[8,512,256]{2,1,0:T(8,128)(2,1)S(1)}, u32[]{:S(2)}, u32[]{:S(2)}) async-start(bf16[8,512,256]{2,1,0:T(8,128)(2,1)} %convert_bitcast_fusion), calls=%async_computation.2 | async-start | bytes 4194304 | tf_op jit(solution)/shard_map/all_to_all | solution.py:286
  131.1 33.8 %all-to-all-start.1 = ((bf16[8,512,256]{2,1,0:T(8,128)(2,1)}), bf16[8,512,256]{2,1,0:T(8,128)(2,1)}, u32[]{:S(2)}, u32[]{:S(2)}) async-start(bf16[8,512,256]{2,1,0:T(8,128)(2,1)} %convert_bitcast_fusion.1), calls=%async_computation.1 | async-start | bytes 4194304 | tf_op jit(solution)/shard_map/all_to_all | solution.py:286
  164.9 28.4 %copy-start.2 = (bf16[32,16,256]{2,1,0:T(8,128)(2,1)S(1)}, bf16[32,16,256]{2,1,0:T(8,128)(2,1)}, u32[]{:S(2)}) copy-start(bf16[32,16,256]{2,1,0:T(8,128)(2,1)} %shard_map.127) | copy-start | bytes 786436
